TPU v7x, 32 devices: a whole 2x2x4 slice. The times are simulated.
32 devices in a mesh: dp: 8 (over y, x, core), mp: 4 (over z).
Axes of the slice: x: 2, y: 2, z: 4, core: 2. Of those that a mesh axis runs over, the one named last changes fastest.
Arguments:
- inputs: bfloat16 [16, 1088, 1024], P('dp'), may hold values from -6 to 6
- encoded: bfloat16 [16, 512, 1024], P('dp'), may hold values from -6 to 6
- decoder_segments: int32 [16, 1088], P('dp'), may hold values from 0 to 3, as said below
- encoder_segments: int32 [16, 512], P('dp'), may hold values from 0 to 3, as said below
- buckets: int32 [1088], replicated, may hold values from 0 to 31, as said below
- self_gain: bfloat16 [1024], P('dp'), may hold values from 0.5 to 1.5
- self_query: bfloat16 [1024, 1024], P('dp', 'mp'), may hold values from -0.09375 to 0.09375
- self_key: bfloat16 [1024, 512], P('dp', 'mp'), may hold values from -0.09375 to 0.09375
- self_value: bfloat16 [1024, 512], P('dp', 'mp'), may hold values from -0.1875 to 0.1875
- self_out: bfloat16 [1024, 1024], P('mp', 'dp'), may hold values from -0.75 to 0.75
- position_bias: bfloat16 [32, 16], P('dp', 'mp'), may hold values from -4 to 4
- cross_gain: bfloat16 [1024], P('dp'), may hold values from 0.5 to 1.5
- cross_query: bfloat16 [1024, 1024], P('dp', 'mp'), may hold values from -0.09375 to 0.09375
- cross_key: bfloat16 [1024, 512], P('dp', 'mp'), may hold values from -0.09375 to 0.09375
- cross_value: bfloat16 [1024, 512], P('dp', 'mp'), may hold values from -0.1875 to 0.1875
- cross_out: bfloat16 [1024, 1024], P('mp', 'dp'), may hold values from -0.75 to 0.75
- feed_gain: bfloat16 [1024], P('dp'), may hold values from 0.5 to 1.5
- feed_gate: bfloat16 [1024, 2816], P('dp', 'mp'), may hold values from -0.1875 to 0.1875
- feed_up: bfloat16 [1024, 2816], P('dp', 'mp'), may hold values from -0.1875 to 0.1875
- feed_down: bfloat16 [2816, 1024], P('mp', 'dp'), may hold values from -0.21875 to 0.21875
- cotangent: bfloat16 [16, 1088, 1024], P('dp'), may hold values from -6 to 6
Outputs:
- outputs: bfloat16 [16, 1088, 1024], P('dp')
- grad_inputs: bfloat16 [16, 1088, 1024], P('dp')
- grad_encoded: bfloat16 [16, 512, 1024], P('dp')
- grad_self_gain: float32 [1024], P('dp')
- grad_self_query: float32 [1024, 1024], P('dp', 'mp')
- grad_self_key: float32 [1024, 512], P('dp', 'mp')
- grad_self_value: float32 [1024, 512], P('dp', 'mp')
- grad_self_out: float32 [1024, 1024], P('mp', 'dp')
- grad_position_bias: float32 [32, 16], P('dp', 'mp')
- grad_cross_gain: float32 [1024], P('dp')
- grad_cross_query: float32 [1024, 1024], P('dp', 'mp')
- grad_cross_key: float32 [1024, 512], P('dp', 'mp')
- grad_cross_value: float32 [1024, 512], P('dp', 'mp')
- grad_cross_out: float32 [1024, 1024], P('mp', 'dp')
- grad_feed_gain: float32 [1024], P('dp')
- grad_feed_gate: float32 [1024, 2816], P('dp', 'mp')
- grad_feed_up: float32 [1024, 2816], P('dp', 'mp')
- grad_feed_down: float32 [2816, 1024], P('mp', 'dp')
Inputs may be any that keep to these rules, and one draw needn't show every extreme that they name: `decoder_segments`: in each sequence the numbers never fall and run through 0 to 3; every document has 60 to 800 tokens, and one of each sequence has exactly 800. `encoder_segments`: in each sequence the numbers never fall and run through 0 to 3; every document has 32 encoder outputs or more. `buckets`: entry d is the bucket of a key d positions before its query.
All inputs are finite; a program needn't handle non-finite values.
Results may differ from a plain program's by a relative error of at most 0.025.
The roundings to bfloat16 on the way count: a program that leaves them out, or rounds other values in their place, can miss the bound.
Values may be sent and summed in bfloat16 or wider, within the bound.
A program may use at most 448 MiB of HBM per device.

v0:
```python
import jax
import jax.numpy as jnp
from jax import lax
from jax.sharding import PartitionSpec as P

HEAD_DIM = 64


epsilon = 1e-06
negative_fill = -1e30
highest = lax.Precision.HIGHEST


def times_transposed(left, right):
    return lax.dot_general(
        left, right, (((1,), (1,)), ((), ())), preferred_element_type=jnp.float32
    )


def contract_rows(left, right):
    return lax.dot_general(
        left, right, (((0,), (0,)), ((), ())), preferred_element_type=jnp.float32
    )


def forward_product(left, right):
    return jnp.dot(left, right, preferred_element_type=jnp.float32)


def normalize(state, gain):
    scale = lax.rsqrt(jnp.mean(state * state, axis=-1, keepdims=True) + epsilon)
    return (state * scale * gain, scale)


def norm_back(state, scale, gain, grad_normed):
    weighted = grad_normed * gain
    grad_gain = jnp.sum(grad_normed * state * scale, axis=0)
    inner = jnp.mean(weighted * state, axis=-1, keepdims=True)
    grad_state = scale * weighted - state * (scale * scale * scale) * inner
    return (grad_state, grad_gain)


def smooth_gate(value):
    return (
        0.5
        * value
        * (1.0 + jnp.tanh(0.7978845608028654 * (value + 0.044715 * value * value * value)))
    )


def split_heads(query, keys):
    rows = query.shape[0]
    key_heads = keys.shape[1] // HEAD_DIM
    group = query.shape[1] // keys.shape[1]
    return (
        query.reshape(rows, key_heads, group, HEAD_DIM),
        keys.reshape(keys.shape[0], key_heads, HEAD_DIM),
    )


def scores_of(grouped, keyed, bias, mask):
    raw = jnp.einsum("qgjd,kgd->gjqk", grouped, keyed, preferred_element_type=jnp.float32)
    return jnp.where(mask, raw + bias, negative_fill)


def attend_forward(query, keys, values, bias, mask):
    grouped, keyed = split_heads(query, keys)
    valued = values.reshape(keyed.shape)
    scores = scores_of(grouped, keyed, bias, mask)
    top = jnp.max(scores, axis=-1, keepdims=True)
    weights = jnp.exp(scores - top)
    total = jnp.sum(weights, axis=-1, keepdims=True)
    softened = (weights / total).astype(jnp.bfloat16)
    mixed = jnp.einsum("gjqk,kgd->qgjd", softened, valued, preferred_element_type=jnp.float32)
    return (mixed.reshape(query.shape).astype(jnp.bfloat16), top + jnp.log(total))


def attend_backward(query, keys, values, bias, mask, summit, grad_mixed):
    grouped, keyed = split_heads(query, keys)
    valued = values.reshape(keyed.shape)
    softened = jnp.exp(scores_of(grouped, keyed, bias, mask) - summit)
    grad_out = grad_mixed.reshape(grouped.shape)
    grad_soft = jnp.einsum("qgjd,kgd->gjqk", grad_out, valued, preferred_element_type=jnp.float32)
    grad_values = jnp.einsum(
        "gjqk,qgjd->kgd",
        softened.astype(jnp.bfloat16),
        grad_out,
        preferred_element_type=jnp.float32,
    )
    grad_scores = softened * (grad_soft - jnp.sum(softened * grad_soft, axis=-1, keepdims=True))
    rounded = grad_scores.astype(jnp.bfloat16)
    grad_query = jnp.einsum("gjqk,kgd->qgjd", rounded, keyed, preferred_element_type=jnp.float32)
    grad_keys = jnp.einsum("gjqk,qgjd->kgd", rounded, grouped, preferred_element_type=jnp.float32)
    return (
        grad_query.reshape(query.shape).astype(jnp.bfloat16),
        grad_keys.reshape(keys.shape).astype(jnp.bfloat16),
        grad_values.reshape(values.shape).astype(jnp.bfloat16),
        grad_scores,
    )


def bias_rows(buckets, table):
    count = table.shape[0]
    onehot = (buckets[:, None] == jnp.arange(count, dtype=jnp.int32)[None, :]).astype(jnp.float32)
    return (
        onehot,
        jnp.dot(
            onehot, table.astype(jnp.float32), precision=highest, preferred_element_type=jnp.float32
        ),
    )


def diagonal_bias(by_distance):
    length = by_distance.shape[0]
    heads_here = by_distance.shape[1]
    reverse = jnp.flip(by_distance.T, axis=1)
    padded = jnp.concatenate([reverse, jnp.zeros((heads_here, length), jnp.float32)], axis=1)
    tiled = jnp.tile(padded, (1, length + 1))
    window = tiled[:, length - 1 : length - 1 + length * (2 * length - 1)]
    return window.reshape(heads_here, length, 2 * length - 1)[:, :, :length]


def bias_grad(grad_scores, onehot):
    length = grad_scores.shape[-1]
    local_heads = grad_scores.shape[0] * grad_scores.shape[1]
    flat = jnp.flip(grad_scores.reshape(local_heads, length, length), axis=2)
    padded = jnp.concatenate([flat, jnp.zeros((local_heads, length, length), jnp.float32)], axis=2)
    spread_rows = padded.reshape(local_heads, 2 * length * length)[:, : length * (2 * length - 1)]
    skewed = spread_rows.reshape(local_heads, length, 2 * length - 1)
    by_distance = jnp.sum(skewed, axis=1)[:, length - 1 :]
    return lax.dot_general(
        onehot,
        by_distance,
        (((0,), (1,)), ((), ())),
        precision=highest,
        preferred_element_type=jnp.float32,
    )


def body(
    inputs,
    encoded,
    decoder_segments,
    encoder_segments,
    buckets,
    self_gain,
    self_query,
    self_key,
    self_value,
    self_out,
    position_bias,
    cross_gain,
    cross_query,
    cross_key,
    cross_value,
    cross_out,
    feed_gain,
    feed_gate,
    feed_up,
    feed_down,
    cotangent,
):
    batches = inputs.shape[0]
    length = inputs.shape[1]

    def collect(partial_value):
        return lax.psum(partial_value, "mp")

    def fetch_self():
        return (
            lax.all_gather(self_gain, "dp", axis=0, tiled=True),
            lax.all_gather(self_query, "dp", axis=0, tiled=True),
            lax.all_gather(self_key, "dp", axis=0, tiled=True),
            lax.all_gather(self_value, "dp", axis=0, tiled=True),
            lax.all_gather(self_out, "dp", axis=1, tiled=True),
            lax.all_gather(position_bias, "dp", axis=0, tiled=True),
        )

    def fetch_cross():
        return (
            lax.all_gather(cross_gain, "dp", axis=0, tiled=True),
            lax.all_gather(cross_query, "dp", axis=0, tiled=True),
            lax.all_gather(cross_key, "dp", axis=0, tiled=True),
            lax.all_gather(cross_value, "dp", axis=0, tiled=True),
            lax.all_gather(cross_out, "dp", axis=1, tiled=True),
        )

    def fetch_feed():
        return (
            lax.all_gather(feed_gain, "dp", axis=0, tiled=True),
            lax.all_gather(feed_gate, "dp", axis=0, tiled=True),
            lax.all_gather(feed_up, "dp", axis=0, tiled=True),
            lax.all_gather(feed_down, "dp", axis=1, tiled=True),
        )

    positions = jnp.arange(length, dtype=jnp.int32)
    causal = positions[:, None] >= positions[None, :]
    outputs = []
    input_grads = []
    memory_grads = []
    totals = None
    for index in range(batches):
        rows = inputs[index].astype(jnp.float32)
        memory = encoded[index]
        decoder_docs = decoder_segments[index]
        encoder_docs = encoder_segments[index]
        self_weights = fetch_self()
        first_gain, first_query, first_keys, first_values, first_out, table = self_weights
        normed_one, scale_one = normalize(rows, first_gain.astype(jnp.float32))
        normed_one = normed_one.astype(jnp.bfloat16)
        query_one = forward_product(normed_one, first_query).astype(jnp.bfloat16)
        keys_one = forward_product(normed_one, first_keys).astype(jnp.bfloat16)
        values_one = forward_product(normed_one, first_values).astype(jnp.bfloat16)
        onehot, by_distance = bias_rows(buckets, table)
        key_heads = first_keys.shape[1] // HEAD_DIM
        bias = diagonal_bias(by_distance)
        bias = bias.reshape(key_heads, bias.shape[0] // key_heads, length, length)
        mask_one = causal & (decoder_docs[:, None] == decoder_docs[None, :])
        mixed_one, summit_one = attend_forward(query_one, keys_one, values_one, bias, mask_one)
        state_one = rows + collect(forward_product(mixed_one, first_out))
        cross_weights = fetch_cross()
        second_gain, second_query, second_keys, second_values, second_out = cross_weights
        normed_two, scale_two = normalize(state_one, second_gain.astype(jnp.float32))
        normed_two = normed_two.astype(jnp.bfloat16)
        query_two = forward_product(normed_two, second_query).astype(jnp.bfloat16)
        keys_two = forward_product(memory, second_keys).astype(jnp.bfloat16)
        values_two = forward_product(memory, second_values).astype(jnp.bfloat16)
        mask_two = decoder_docs[:, None] == encoder_docs[None, :]
        mixed_two, summit_two = attend_forward(query_two, keys_two, values_two, 0.0, mask_two)
        state_two = state_one + collect(forward_product(mixed_two, second_out))
        feed_weights = fetch_feed()
        third_gain, gate_weight, up_weight, down_weight = feed_weights
        normed_three, scale_three = normalize(state_two, third_gain.astype(jnp.float32))
        normed_three = normed_three.astype(jnp.bfloat16)
        gate = forward_product(normed_three, gate_weight)
        upward = forward_product(normed_three, up_weight)
        activated, gate_pull = jax.vjp(smooth_gate, gate)
        hidden = (activated * upward).astype(jnp.bfloat16)
        state_three = state_two + collect(forward_product(hidden, down_weight))
        outputs.append(state_three.astype(jnp.bfloat16))
        third_gain, gate_weight, up_weight, down_weight = fetch_feed()
        grad_three = cotangent[index].astype(jnp.float32)
        grad_rows = cotangent[index]
        grad_down = contract_rows(hidden, grad_rows)
        grad_hidden = times_transposed(grad_rows, down_weight)
        grad_gate = gate_pull(grad_hidden * upward)[0].astype(jnp.bfloat16)
        grad_up = (grad_hidden * activated).astype(jnp.bfloat16)
        grad_gate_weight = contract_rows(normed_three, grad_gate)
        grad_up_weight = contract_rows(normed_three, grad_up)
        summed = collect(
            times_transposed(grad_gate, gate_weight) + times_transposed(grad_up, up_weight)
        )
        back, grad_third_gain = norm_back(
            state_two, scale_three, third_gain.astype(jnp.float32), summed
        )
        grad_two = grad_three + back
        second_gain, second_query, second_keys, second_values, second_out = fetch_cross()
        grad_rows = grad_two.astype(jnp.bfloat16)
        grad_second_out = contract_rows(mixed_two, grad_rows)
        grad_mixed = times_transposed(grad_rows, second_out).astype(jnp.bfloat16)
        grad_query, grad_keys, grad_values, unused = attend_backward(
            query_two, keys_two, values_two, 0.0, mask_two, summit_two, grad_mixed
        )
        grad_second_query = contract_rows(normed_two, grad_query)
        grad_second_keys = contract_rows(memory, grad_keys)
        grad_second_values = contract_rows(memory, grad_values)
        memory_term = times_transposed(grad_keys, second_keys) + times_transposed(
            grad_values, second_values
        )
        memory_grads.append(lax.psum(memory_term.astype(jnp.bfloat16), "mp"))
        summed = collect(times_transposed(grad_query, second_query))
        back, grad_second_gain = norm_back(
            state_one, scale_two, second_gain.astype(jnp.float32), summed
        )
        grad_one = grad_two + back
        first_gain, first_query, first_keys, first_values, first_out, table = fetch_self()
        grad_rows = grad_one.astype(jnp.bfloat16)
        grad_first_out = contract_rows(mixed_one, grad_rows)
        grad_mixed = times_transposed(grad_rows, first_out).astype(jnp.bfloat16)
        grad_query, grad_keys, grad_values, grad_scores = attend_backward(
            query_one, keys_one, values_one, bias, mask_one, summit_one, grad_mixed
        )
        grad_table = bias_grad(grad_scores, onehot)
        grad_first_query = contract_rows(normed_one, grad_query)
        grad_first_keys = contract_rows(normed_one, grad_keys)
        grad_first_values = contract_rows(normed_one, grad_values)
        summed = collect(
            times_transposed(grad_query, first_query)
            + times_transposed(grad_keys, first_keys)
            + times_transposed(grad_values, first_values)
        )
        back, grad_first_gain = norm_back(rows, scale_one, first_gain.astype(jnp.float32), summed)
        input_grads.append((grad_one + back).astype(jnp.bfloat16))
        grads = (
            grad_first_gain,
            grad_first_query,
            grad_first_keys,
            grad_first_values,
            grad_first_out,
            grad_table,
            grad_second_gain,
            grad_second_query,
            grad_second_keys,
            grad_second_values,
            grad_second_out,
            grad_third_gain,
            grad_gate_weight,
            grad_up_weight,
            grad_down,
        )
        if totals is None:
            totals = grads
        else:
            totals = tuple((left + right for left, right in zip(totals, grads)))
    shards = (
        lax.psum_scatter(
            totals[0].astype(jnp.bfloat16), "dp", scatter_dimension=0, tiled=True
        ).astype(jnp.float32),
        lax.psum_scatter(
            totals[1].astype(jnp.bfloat16), "dp", scatter_dimension=0, tiled=True
        ).astype(jnp.float32),
        lax.psum_scatter(
            totals[2].astype(jnp.bfloat16), "dp", scatter_dimension=0, tiled=True
        ).astype(jnp.float32),
        lax.psum_scatter(
            totals[3].astype(jnp.bfloat16), "dp", scatter_dimension=0, tiled=True
        ).astype(jnp.float32),
        lax.psum_scatter(
            totals[4].astype(jnp.bfloat16), "dp", scatter_dimension=1, tiled=True
        ).astype(jnp.float32),
        lax.psum_scatter(
            totals[5].astype(jnp.bfloat16), "dp", scatter_dimension=0, tiled=True
        ).astype(jnp.float32),
        lax.psum_scatter(
            totals[6].astype(jnp.bfloat16), "dp", scatter_dimension=0, tiled=True
        ).astype(jnp.float32),
        lax.psum_scatter(
            totals[7].astype(jnp.bfloat16), "dp", scatter_dimension=0, tiled=True
        ).astype(jnp.float32),
        lax.psum_scatter(
            totals[8].astype(jnp.bfloat16), "dp", scatter_dimension=0, tiled=True
        ).astype(jnp.float32),
        lax.psum_scatter(
            totals[9].astype(jnp.bfloat16), "dp", scatter_dimension=0, tiled=True
        ).astype(jnp.float32),
        lax.psum_scatter(
            totals[10].astype(jnp.bfloat16), "dp", scatter_dimension=1, tiled=True
        ).astype(jnp.float32),
        lax.psum_scatter(
            totals[11].astype(jnp.bfloat16), "dp", scatter_dimension=0, tiled=True
        ).astype(jnp.float32),
        lax.psum_scatter(
            totals[12].astype(jnp.bfloat16), "dp", scatter_dimension=0, tiled=True
        ).astype(jnp.float32),
        lax.psum_scatter(
            totals[13].astype(jnp.bfloat16), "dp", scatter_dimension=0, tiled=True
        ).astype(jnp.float32),
        lax.psum_scatter(
            totals[14].astype(jnp.bfloat16), "dp", scatter_dimension=1, tiled=True
        ).astype(jnp.float32),
    )
    return (jnp.stack(outputs), jnp.stack(input_grads), jnp.stack(memory_grads)) + tuple(shards)


def solution(mesh):
    return jax.shard_map(
        body,
        mesh=mesh,
        in_specs=(
            P("dp", None, None),
            P("dp", None, None),
            P("dp", None),
            P("dp", None),
            P(),
            P("dp"),
            P("dp", "mp"),
            P("dp", "mp"),
            P("dp", "mp"),
            P("mp", "dp"),
            P("dp", "mp"),
            P("dp"),
            P("dp", "mp"),
            P("dp", "mp"),
            P("dp", "mp"),
            P("mp", "dp"),
            P("dp"),
            P("dp", "mp"),
            P("dp", "mp"),
            P("mp", "dp"),
            P("dp", None, None),
        ),
        out_specs=(
            P("dp", None, None),
            P("dp", None, None),
            P("dp", None, None),
            P("dp"),
            P("dp", "mp"),
            P("dp", "mp"),
            P("dp", "mp"),
            P("mp", "dp"),
            P("dp", "mp"),
            P("dp"),
            P("dp", "mp"),
            P("dp", "mp"),
            P("dp", "mp"),
            P("mp", "dp"),
            P("dp"),
            P("dp", "mp"),
            P("dp", "mp"),
            P("mp", "dp"),
        ),
        check_vma=False,
    )
```

profile of v0, /device:TPU:8, one launch (start us, length us, event | category | flops | bytes accessed | tf_op | source)
XLA Modules:
  0.0 3019.2 jit_solution(4161100210902852889)
XLA Ops:
  89.2 33.5 %copy.165 = f32[1,4,1089,2176]{3,1,2,0:T(4,128)} copy(f32[1,4,1089,2176]{3,2,1,0:T(8,128)} %broadcast_bitcast_fusion) | data formatting | bytes 75829248
  122.7 25.6 slice.68
  148.2 109.8 %reshape.481 = f32[9465600]{0:T(1024)} reshape(f32[4,2366400]{1,0:T(4,128)} %slice.68) | data formatting | bytes 75724800
  258.0 61.1 %reshape.411 = f32[4,1088,2175]{2,1,0:T(8,128)} reshape(f32[9465600]{0:T(1024)} %reshape.481) | data formatting | bytes 75724800 | tf_op jit(solution)/shard_map/reshape | solution.py:120
  319.1 15.0 slice.69
  334.1 21.7 copy.104
  478.0 255.8 %all-reduce.29.cloned.1.call-done = (f32[1088,1024]{1,0:T(8,128)}, f32[1088,1024]{1,0:T(8,128)}) async-done(((f32[1088,1024]{1,0:T(8,128)}, f32[1088,1024]{1,0:T(8,128)}), (f32[1088,1024]{1,0:T(8,128)}, f32[1088,1024]{1,0:T(8,128)})) %all-reduce.29.cloned.1.call-update) | async-done | bytes 8912912 | tf_op jit(solution)/shard_map/psum | solution.py:167
  786.3 296.9 %all-reduce.27.cloned.1.call-done = (f32[1088,1024]{1,0:T(8,128)}, f32[1088,1024]{1,0:T(8,128)}) async-done(((f32[1088,1024]{1,0:T(8,128)}, f32[1088,1024]{1,0:T(8,128)}), (f32[1088,1024]{1,0:T(8,128)}, f32[1088,1024]{1,0:T(8,128)})) %all-reduce.27.cloned.1.call-update) | async-done | bytes 8912912 | tf_op jit(solution)/shard_map/psum | solution.py:167
  1147.9 307.5 %all-reduce.25.cloned.1.call-done = (f32[1088,1024]{1,0:T(8,128)}, f32[1088,1024]{1,0:T(8,128)}) async-done(((f32[1088,1024]{1,0:T(8,128)}, f32[1088,1024]{1,0:T(8,128)}), (f32[1088,1024]{1,0:T(8,128)}, f32[1088,1024]{1,0:T(8,128)})) %all-reduce.25.cloned.1.call-update) | async-done | bytes 8912912 | tf_op jit(solution)/shard_map/psum | solution.py:167
  1590.4 221.3 %all-reduce.23.cloned.1.call-done = (f32[1088,1024]{1,0:T(8,128)}, f32[1088,1024]{1,0:T(8,128)}) async-done(((f32[1088,1024]{1,0:T(8,128)}, f32[1088,1024]{1,0:T(8,128)}), (f32[1088,1024]{1,0:T(8,128)}, f32[1088,1024]{1,0:T(8,128)})) %all-reduce.23.cloned.1.call-update) | async-done | bytes 8912912 | tf_op jit(solution)/shard_map/psum | solution.py:167
  1882.5 20.6 subtract_multiply_fusion.1
  2012.0 21.8 copy.122
  2033.8 168.9 %reverse.1 = f32[4,1088,1152]{2,1,0:T(8,128)} reverse(f32[4,1088,1152]{2,1,0:T(8,128)} %bitcast.554), dimensions={2} | reverse | bytes 40108032
  2225.2 42.5 %copy.166 = f32[1,4,1088,2176]{3,1,2,0:T(4,128)} copy(f32[1,4,1088,2176]{3,2,1,0:T(8,128)} %pad_bitcast_fusion.1) | data formatting | bytes 75759616
  2267.7 26.1 slice.70
  2293.8 110.6 %reshape.483 = f32[9465600]{0:T(1024)} reshape(f32[4,2366400]{1,0:T(4,128)} %slice.70) | data formatting | bytes 75724800
  2404.4 61.8 %reshape.428 = f32[4,1088,2175]{2,1,0:T(8,128)} reshape(f32[9465600]{0:T(1024)} %reshape.483) | data formatting | bytes 75724800 | tf_op jit(solution)/shard_map/reshape | solution.py:129
  2480.1 21.9 copy.123
  2502.0 168.9 %reverse.2 = f32[4,1088,1152]{2,1,0:T(8,128)} reverse(f32[4,1088,1152]{2,1,0:T(8,128)} %bitcast.555), dimensions={2} | reverse | bytes 40108032
  2693.2 42.5 %copy.167 = f32[1,4,1088,2176]{3,1,2,0:T(4,128)} copy(f32[1,4,1088,2176]{3,2,1,0:T(8,128)} %pad_bitcast_fusion) | data formatting | bytes 75759616
  2735.8 26.3 slice.72
  2762.1 109.9 %reshape.485 = f32[9465600]{0:T(1024)} reshape(f32[4,2366400]{1,0:T(4,128)} %slice.72) | data formatting | bytes 75724800
  2872.0 61.2 %reshape.431 = f32[4,1088,2175]{2,1,0:T(8,128)} reshape(f32[9465600]{0:T(1024)} %reshape.485) | data formatting | bytes 75724800 | tf_op jit(solution)/shard_map/reshape | solution.py:129
  2969.5 24.1 all-reduce.12
  (601 shorter events, 744.1 us)
Async XLA Ops:
  8.0 725.8 %all-reduce.29.cloned.1.call-start = ((), (), s32[]{:S(2)}) async-start(), calls=%async_computation.29 | async-start | bytes 17825792 | tf_op jit(solution)/shard_map/psum | solution.py:167
  65.1 315.6 %copy-start.49 = (bf16[1088,128]{0,1:T(8,128)(2,1)}, bf16[1088,128]{0,1:T(8,128)(2,1)S(1)}, u32[]{:S(2)}) copy-start(bf16[1088,128]{0,1:T(8,128)(2,1)S(1)} %copy.101) | copy-start | bytes 835588
  427.2 655.9 %all-reduce.27.cloned.1.call-start = ((), (), s32[]{:S(2)}) async-start(), calls=%async_computation.28 | async-start | bytes 17825792 | tf_op jit(solution)/shard_map/psum | solution.py:167
  435.8 310.5 %copy-start.81 = (f32[8,1,128]{2,1,0:T(1,128)}, f32[8,1,128]{2,1,0:T(1,128)S(1)}, u32[]{:S(2)}) copy-start(f32[8,1,128]{2,1,0:T(1,128)S(1)} %convert_element_type.622) | copy-start | bytes 12292
  775.5 312.0 %slice-start.2 = ((s8[4456448]{0:T(1024)(128)(4,1)}), s8[262144]{0:T(1024)(128)(4,1)S(1)}, s32[]{:S(2)}) async-start(s8[4456448]{0:T(1024)(128)(4,1)} %bitcast.537), calls=%async_computation.33 | async-start | bytes 524288
  775.5 320.8 %all-gather.10.cloned.1.call-start = ((), (), s32[]{:S(2)}) async-start(), calls=%async_computation.12 | async-start | bytes 1622016 | tf_op jit(solution)/shard_map/all_gather | solution.py:192
  776.1 326.1 %all-gather.8.cloned.1.call-start = ((), (), s32[]{:S(2)}) async-start(), calls=%async_computation.11 | async-start | bytes 1622016 | tf_op jit(solution)/shard_map/all_gather | solution.py:191
  776.7 339.0 %all-gather.12.cloned.1.call-start = ((), (), s32[]{:S(2)}) async-start(), calls=%async_computation.13 | async-start | bytes 1622016 | tf_op jit(solution)/shard_map/all_gather | solution.py:193
  777.3 678.1 %all-reduce.25.cloned.1.call-start = ((), (), s32[]{:S(2)}) async-start(), calls=%async_computation.27 | async-start | bytes 17825792 | tf_op jit(solution)/shard_map/psum | solution.py:167
  1147.7 316.1 %slice-start.13 = ((s8[4456448]{0:T(1024)(128)(4,1)}), s8[262144]{0:T(1024)(128)(4,1)S(1)}, s32[]{:S(2)}) async-start(s8[4456448]{0:T(1024)(128)(4,1)} %bitcast.548), calls=%async_computation.44 | async-start | bytes 524288
  1147.8 664.0 %all-reduce.23.cloned.1.call-start = ((), (), s32[]{:S(2)}) async-start(), calls=%async_computation.26 | async-start | bytes 17825792 | tf_op jit(solution)/shard_map/psum | solution.py:167
  1504.1 492.2 %reduce-scatter.42.cloned.1.call-start = ((), (), s32[]{:S(2)}) async-start(), calls=%async_computation.22 | async-start | bytes 1769472
  1514.4 483.9 %reduce-scatter.44.cloned.1.call-start = ((), (), s32[]{:S(2)}) async-start(), calls=%async_computation.23 | async-start | bytes 1769472
  1524.7 475.4 %reduce-scatter.46.cloned.1.call-start = ((), (), s32[]{:S(2)}) async-start(), calls=%async_computation.24 | async-start | bytes 1769472
  1537.4 465.2 %reduce-scatter.38.cloned.1.call-start = ((), (), s32[]{:S(2)}) async-start(), calls=%async_computation.20 | async-start | bytes 294912
  1559.2 445.0 %reduce-scatter.36.cloned.1.call-start = ((), (), s32[]{:S(2)}) async-start(), calls=%async_computation.19 | async-start | bytes 294912
  1563.3 442.5 %reduce-scatter.40.cloned.1.call-start = ((), (), s32[]{:S(2)}) async-start(), calls=%async_computation.21 | async-start | bytes 589824
  1571.5 436.0 %reduce-scatter.32.cloned.1.call-start = ((), (), s32[]{:S(2)}) async-start(), calls=%async_computation.17 | async-start | bytes 589824 | tf_op jit(solution)/shard_map/reduce_scatter | solution.py:337
  1586.0 423.0 %all-reduce.31.cloned.1.call-start = ((), (), s32[]{:S(2)}) async-start(), calls=%async_computation.30 | async-start | bytes 4194304 | tf_op jit(solution)/shard_map/psum | solution.py:270
  1589.9 1358.3 %reduce-scatter.30.cloned.1.call-start = ((), (), s32[]{:S(2)}) async-start(), calls=%async_computation.16 | async-start | bytes 294912 | tf_op jit(solution)/shard_map/reduce_scatter | solution.py:325
  1961.9 987.8 %reduce-scatter.28.cloned.1.call-start = ((), (), s32[]{:S(2)}) async-start(), calls=%async_computation.15 | async-start | bytes 294912 | tf_op jit(solution)/shard_map/reduce_scatter | solution.py:322
  1969.7 981.3 %reduce-scatter.34.cloned.1.call-start = ((), (), s32[]{:S(2)}) async-start(), calls=%async_computation.18 | async-start | bytes 589824
  1976.8 975.9 %reduce-scatter.26.cloned.1.call-start = ((), (), s32[]{:S(2)}) async-start(), calls=%async_computation.14 | async-start | bytes 589824 | tf_op jit(solution)/shard_map/reduce_scatter | solution.py:319
  1987.1 967.0 %all-reduce.21.cloned.1.call-start = ((), (), s32[]{:S(2)}) async-start(), calls=%async_computation.25 | async-start | bytes 35651584 | tf_op jit(solution)/shard_map/psum | solution.py:167
  (160 other events, 3285.5 us)
Sparse Core Ops, SparseCore 0:
  427.3 306.4 all-reduce.28
  775.7 307.4 all-reduce.26
  1147.9 307.4 all-reduce.24
  1504.2 307.4 all-reduce.22
  1814.5 86.6 all-reduce.30
  1993.9 598.2 all-reduce.20
Sparse Core Ops, SparseCore 1:
  777.9 26.3 all-gather.9
  806.0 25.1 all-gather.7
  832.9 25.1 all-gather.11
  1514.4 39.4 reduce-scatter.41
  1557.2 38.3 reduce-scatter.43
  1598.9 38.3 reduce-scatter.45
  1640.1 33.6 reduce-scatter.37
  1677.0 33.7 reduce-scatter.35
  1713.6 34.1 reduce-scatter.39
  1751.2 34.1 reduce-scatter.31
  1961.9 34.9 reduce-scatter.29
  2000.2 33.7 reduce-scatter.27
  2036.9 34.1 reduce-scatter.33
  2074.5 34.2 reduce-scatter.25
where the time goes:
time: 3060 us; the launch traced here: 3020 us
  local copies, waits for them, and re-layouts  1240 us (41%)
  waiting for transfers between devices  1080 us (35%)
  matrix products  343 us (11%)
  other arithmetic  196 us (6%)
  blocking collectives  133 us (4%)
    psum x5, waiting for transfers between devices, collect(): return lax.psum(partial_value, 'mp')  1080 us
    unnamed x360, local copies, waits for them, and re-layouts  889 us
    reshape x2, local copies, waits for them, and re-layouts, bias_grad(): skewed = spread_rows.reshape(local_heads, length, 2 * length - 1)  123 us
    dot_general x22, matrix products, contract_rows(): lax.dot_general(left, right, (((0,), (0,)), ((), ())), preferred_element_...  63.6 us
    dot_general x22, matrix products, times_transposed(): lax.dot_general(left, right, (((1,), (1,)), ((), ())), preferred_element_...  61.5 us
  transfers between devices with their start and end apart: 20, of which 4 were waited for; matrix products, arithmetic and copies ran while one was open for 41% of the time, Pallas kernels for 0%

commit v1 on v0

v1 whole, which is shorter than its diff:
```python
import functools

import jax
import jax.numpy as jnp
from jax import lax
from jax.experimental import pallas as pl
from jax.experimental.pallas import tpu as pltpu
from jax.sharding import PartitionSpec as P

HEAD_DIM = 64
TILE_Q = 128
TILE_K = 256
EPSILON = 1e-06
NEGATIVE = -1e30
HIGHEST = lax.Precision.HIGHEST
F32 = jnp.float32
BF16 = jnp.bfloat16


def dot(left, right, dims, precision=None):
    return lax.dot_general(
        left, right, ((dims[0], dims[1]), ((), ())), precision=precision, preferred_element_type=F32
    )


def mm(left, right):
    return dot(left, right, ((1,), (0,)))


def mm_nt(left, right):
    return dot(left, right, ((1,), (1,)))


def mm_tn(left, right):
    return dot(left, right, ((0,), (0,)))


def round_up(value, unit):
    return (value + unit - 1) // unit * unit


def skew(row, height):
    wide = jnp.broadcast_to(row, (height, row.shape[1]))
    return pltpu.roll(wide, 0, axis=1, stride=1, stride_axis=0)


def stacked(tile, g):
    base = 2 * HEAD_DIM * g
    return jnp.concatenate(
        [tile[:, base : base + HEAD_DIM], tile[:, base + HEAD_DIM : base + 2 * HEAD_DIM]], axis=0
    )


def unstacked(pair):
    return jnp.concatenate([pair[:TILE_Q], pair[TILE_Q:]], axis=1)


def twice(row):
    return jnp.concatenate([row, row], axis=1)


def tile_mask(biased, mask_ref, keys_ref, a, u0):
    cols = pl.ds(pl.multiple_of(a * TILE_Q, TILE_Q), TILE_Q)
    row = twice(mask_ref[0:1, cols])
    if biased:
        index = lax.broadcasted_iota(jnp.int32, (TILE_K, 2 * TILE_Q), 0)
        return index >= row - u0
    keys = keys_ref[pl.ds(u0, TILE_K), :]
    return jnp.concatenate([keys, keys], axis=1) == row


def tile_bias(strip_ref, g, off):
    lanes = pl.ds(off, TILE_Q)
    return jnp.concatenate([strip_ref[2 * g, :, lanes], strip_ref[2 * g + 1, :, lanes]], axis=1)


def forward_kernel(biased, front, lead, lo_ref, hi_ref, *refs):
    if biased:
        q_ref, k_ref, v_ref, mask_ref, vec_ref, o_ref, lse_ref, strip, m_s, l_s, acc_s = refs
        keys_ref = None
        for h in range(4):
            strip[h] = skew(vec_ref[0, h : h + 1, :], TILE_K)
    else:
        q_ref, k_ref, v_ref, mask_ref, keys_ref, o_ref, lse_ref, m_s, l_s, acc_s = refs
    tiles = q_ref.shape[0] // TILE_Q

    def q_tile(a, carry):
        rows = pl.ds(pl.multiple_of(a * TILE_Q, TILE_Q), TILE_Q)
        qt = q_ref[rows, :]
        q2 = [stacked(qt, g) for g in range(2)]
        m_s[...] = jnp.full_like(m_s, NEGATIVE)
        l_s[...] = jnp.zeros_like(l_s)
        acc_s[...] = jnp.zeros_like(acc_s)

        def k_tile(m, carry):
            u0 = pl.multiple_of(m * TILE_K, TILE_K)
            kt = k_ref[pl.ds(u0, TILE_K), :]
            vt = v_ref[pl.ds(u0, TILE_K), :]
            valid = tile_mask(biased, mask_ref, keys_ref, a, u0)
            for g in range(2):
                head = slice(HEAD_DIM * g, HEAD_DIM * (g + 1))
                s = mm_nt(kt[:, head], q2[g])
                if biased:
                    off = pl.multiple_of(a * TILE_Q - m * TILE_K + front + lead, TILE_Q)
                    s = s + tile_bias(strip, g, off)
                s = jnp.where(valid, s, NEGATIVE)
                top = m_s[g : g + 1, :]
                new = jnp.maximum(top, jnp.max(s, axis=0, keepdims=True))
                alpha = jnp.exp(top - new)
                p = jnp.exp(s - new)
                m_s[g : g + 1, :] = new
                l_s[g : g + 1, :] = l_s[g : g + 1, :] * alpha + jnp.sum(p, axis=0, keepdims=True)
                acc_s[g] = acc_s[g] * alpha + mm_tn(vt[:, head], p.astype(BF16))
            return carry

        lax.fori_loop(lo_ref[a], hi_ref[a], k_tile, 0)
        for g in range(2):
            total = l_s[g : g + 1, :]
            mixed = (acc_s[g] / total).T
            o_ref[rows, 2 * HEAD_DIM * g : 2 * HEAD_DIM * (g + 1)] = unstacked(mixed).astype(BF16)
            lse = m_s[g : g + 1, :] + jnp.log(total)
            lse_ref[0, 2 * g : 2 * g + 1, rows] = lse[:, :TILE_Q]
            lse_ref[0, 2 * g + 1 : 2 * g + 2, rows] = lse[:, TILE_Q:]
        return carry

    lax.fori_loop(0, tiles, q_tile, 0)


def backward_kernel(biased, front, lead, lo_ref, hi_ref, *refs):
    if biased:
        (
            q_ref, k_ref, v_ref, o_ref, do_ref, lse_ref, mask_ref, vec_ref,
            dq_ref, dk_ref, dv_ref, dist_ref, strip, slope, dk_s, dv_s, dq_s,
        ) = refs
        keys_ref = None
        for h in range(4):
            strip[h] = skew(vec_ref[0, h : h + 1, :], TILE_K)
        slope[...] = jnp.zeros_like(slope)
    else:
        (
            q_ref, k_ref, v_ref, o_ref, do_ref, lse_ref, mask_ref, keys_ref,
            dq_ref, dk_ref, dv_ref, dk_s, dv_s, dq_s,
        ) = refs
    tiles = q_ref.shape[0] // TILE_Q
    dk_s[...] = jnp.zeros_like(dk_s)
    dv_s[...] = jnp.zeros_like(dv_s)

    def q_tile(a, carry):
        rows = pl.ds(pl.multiple_of(a * TILE_Q, TILE_Q), TILE_Q)
        qt = q_ref[rows, :]
        ot = o_ref[rows, :]
        dot_ = do_ref[rows, :]
        q2 = [stacked(qt, g) for g in range(2)]
        do2 = [stacked(dot_, g) for g in range(2)]
        lse = []
        delta = []
        for g in range(2):
            both = stacked(ot, g).astype(F32) * do2[g].astype(F32)
            delta.append(jnp.sum(both.T, axis=0, keepdims=True))
            lse.append(
                jnp.concatenate(
                    [lse_ref[0, 2 * g : 2 * g + 1, rows], lse_ref[0, 2 * g + 1 : 2 * g + 2, rows]],
                    axis=1,
                )
            )
        dq_s[...] = jnp.zeros_like(dq_s)

        def k_tile(m, carry):
            u0 = pl.multiple_of(m * TILE_K, TILE_K)
            keys = pl.ds(u0, TILE_K)
            kt = k_ref[keys, :]
            vt = v_ref[keys, :]
            valid = tile_mask(biased, mask_ref, keys_ref, a, u0)
            grad_k = []
            grad_v = []
            for g in range(2):
                head = slice(HEAD_DIM * g, HEAD_DIM * (g + 1))
                s = mm_nt(kt[:, head], q2[g])
                if biased:
                    off = pl.multiple_of(a * TILE_Q - m * TILE_K + front + lead, TILE_Q)
                    s = s + tile_bias(strip, g, off)
                p = jnp.exp(jnp.where(valid, s - lse[g], NEGATIVE))
                dp = mm_nt(vt[:, head], do2[g])
                ds = p * (dp - delta[g])
                low = ds.astype(BF16)
                if biased:
                    lanes = pl.ds(off, TILE_Q)
                    slope[2 * g, :, lanes] += ds[:, :TILE_Q]
                    slope[2 * g + 1, :, lanes] += ds[:, TILE_Q:]
                grad_v.append(mm(p.astype(BF16), do2[g]))
                grad_k.append(mm(low, q2[g]))
                dq_s[g] += mm_tn(kt[:, head], low)
            dk_s[keys, :] += jnp.concatenate(grad_k, axis=1)
            dv_s[keys, :] += jnp.concatenate(grad_v, axis=1)
            return carry

        lax.fori_loop(lo_ref[a], hi_ref[a], k_tile, 0)
        for g in range(2):
            dq_ref[rows, 2 * HEAD_DIM * g : 2 * HEAD_DIM * (g + 1)] = unstacked(dq_s[g].T).astype(
                BF16
            )
        return carry

    lax.fori_loop(0, tiles, q_tile, 0)
    dk_ref[...] = dk_s[...].astype(BF16)
    dv_ref[...] = dv_s[...].astype(BF16)
    if biased:
        width = slope.shape[2]
        for h in range(4):
            part = slope[h]
            height = TILE_K
            while height > 8:
                height //= 2
                part = part[:height] + pltpu.roll(part[height:], width - height, axis=1)
            row = part[0:1]
            for j in range(1, 8):
                row = row + pltpu.roll(part, width - j, axis=1)[j : j + 1]
            dist_ref[0, h : h + 1, :] = row


def spec(shape, index):
    return pl.BlockSpec(shape, index)


def attention_call(kernel, biased, outs, scratch, args, bounds, front, lead, name, flops):
    rows = args[0].shape[0]
    steps = args[1].shape[1] // (2 * HEAD_DIM)

    def column(array, lanes):
        return spec((array.shape[0], lanes), lambda i, *_: (0, i))

    specs = []
    for array, kind in args_kinds(args, biased, kernel):
        if kind == "wide":
            specs.append(column(array, 4 * HEAD_DIM))
        elif kind == "key":
            specs.append(column(array, 2 * HEAD_DIM))
        elif kind == "head":
            specs.append(spec((1,) + array.shape[1:], lambda i, *_: (i, 0, 0)))
        else:
            specs.append(spec(array.shape, lambda i, *_: (0, 0)))
    out_specs = []
    for item, kind in outs:
        if kind == "wide":
            out_specs.append(column(item, 4 * HEAD_DIM))
        elif kind == "key":
            out_specs.append(column(item, 2 * HEAD_DIM))
        else:
            out_specs.append(spec((1,) + item.shape[1:], lambda i, *_: (i, 0, 0)))
    return pl.pallas_call(
        functools.partial(kernel, biased, front, lead),
        out_shape=[item for item, _ in outs],
        grid_spec=pltpu.PrefetchScalarGridSpec(
            num_scalar_prefetch=2,
            grid=(steps,),
            in_specs=specs,
            out_specs=out_specs,
            scratch_shapes=scratch,
        ),
        compiler_params=pltpu.CompilerParams(vmem_limit_bytes=56 << 20),
        cost_estimate=pl.CostEstimate(flops=flops, bytes_accessed=16 << 20, transcendentals=0),
        name=name,
    )(*bounds, *args)


def args_kinds(args, biased, kernel):
    tail = ["flat", "head" if biased else "flat"]
    if kernel is forward_kernel:
        kinds = ["wide", "key", "key"] + tail
    else:
        kinds = ["wide", "key", "key", "wide", "wide", "head"] + tail
    return list(zip(args, kinds))


def attend_forward(q, k, v, mask, extra, bounds, front, lead, biased, name):
    rows = q.shape[0]
    steps = k.shape[1] // (2 * HEAD_DIM)
    outs = [
        (jax.ShapeDtypeStruct(q.shape, BF16), "wide"),
        (jax.ShapeDtypeStruct((steps, 4, rows), F32), "head"),
    ]
    scratch = []
    if biased:
        scratch.append(pltpu.VMEM((4, TILE_K, extra.shape[2]), F32))
    scratch += [
        pltpu.VMEM((2, 2 * TILE_Q), F32),
        pltpu.VMEM((2, 2 * TILE_Q), F32),
        pltpu.VMEM((2, HEAD_DIM, 2 * TILE_Q), F32),
    ]
    flops = 4 * rows * k.shape[0] * q.shape[1]
    return attention_call(
        forward_kernel, biased, outs, scratch, (q, k, v, mask, extra), bounds, front, lead, name, flops
    )


def attend_backward(q, k, v, o, do, lse, mask, extra, bounds, front, lead, biased, name):
    rows = q.shape[0]
    keys = k.shape[0]
    outs = [
        (jax.ShapeDtypeStruct(q.shape, BF16), "wide"),
        (jax.ShapeDtypeStruct(k.shape, BF16), "key"),
        (jax.ShapeDtypeStruct(k.shape, BF16), "key"),
    ]
    scratch = []
    if biased:
        outs.append((jax.ShapeDtypeStruct(extra.shape, F32), "head"))
        scratch += [pltpu.VMEM((4, TILE_K, extra.shape[2]), F32)] * 2
    scratch += [
        pltpu.VMEM((keys, 2 * HEAD_DIM), F32),
        pltpu.VMEM((keys, 2 * HEAD_DIM), F32),
        pltpu.VMEM((2, HEAD_DIM, 2 * TILE_Q), F32),
    ]
    flops = 10 * rows * keys * q.shape[1]
    return attention_call(
        backward_kernel, biased, outs, scratch, (q, k, v, o, do, lse, mask, extra), bounds, front,
        lead, name, flops,
    )


MESH = pl.DeviceIdType.MESH


class Place:
    def __init__(self, mp):
        self.mp = mp
        self.i = lax.axis_index("dp")
        self.z = lax.axis_index("mp")
        core = lax.rem(self.i, 2)
        across = lax.rem(lax.div(self.i, 2), 2)
        up = lax.div(self.i, 4)
        self.core, self.across, self.up = core, across, up
        self.ic = self.i + 1 - 2 * core
        self.ix = self.i + 2 - 4 * across
        self.iy = self.i + 4 - 8 * up
        self.ixy = self.ix + 4 - 8 * up


def enter(place):
    barrier = pltpu.get_barrier_semaphore()
    z, mp = place.z, place.mp
    for near in (place.ic, place.ix, place.iy):
        pl.semaphore_signal(barrier, 1, device_id=(near, z), device_id_type=MESH)

    @pl.when(z > 0)
    def _():
        pl.semaphore_signal(barrier, 1, device_id=(place.i, z - 1), device_id_type=MESH)

    @pl.when(z < mp - 1)
    def _():
        pl.semaphore_signal(barrier, 1, device_id=(place.i, z + 1), device_id_type=MESH)

    low = jnp.minimum(z, 1)
    high = jnp.minimum(mp - 1 - z, 1)
    pl.semaphore_wait(barrier, 3 + low + high)


def region(ref, i, z, shard):
    if len(ref.shape) == 4:
        return ref.at[z, i]
    rows, cols = shard
    return ref.at[pl.ds(pl.multiple_of(z * rows, rows), rows), pl.ds(pl.multiple_of(i * cols, cols), cols)]


def gather_steps(place, shards, outs, send, recv, local):
    mp, i, z = place.mp, place.i, place.z
    units = range(len(shards))

    def here(u, i2, z2):
        return region(outs[u], i2, z2, shards[u].shape)

    def copy(u, kind, i2, z2, to, src=None):
        spot = here(u, i2, z2)
        return pltpu.make_async_remote_copy(
            src_ref=spot if src is None else src, dst_ref=spot, send_sem=send.at[u, kind, z2],
            recv_sem=recv.at[u, kind, z2], device_id=to, device_id_type=MESH)

    def route(u, z2):
        odd = lax.rem(z2 + u, 2)
        first = place.ix + odd * (place.iy - place.ix)
        second = place.iy + odd * (place.ix - place.iy)
        return odd, first, second

    slots = [(0, 0)] + [(d, s) for d in range(1, mp) for s in (0, 1)]

    def when(slot, f):
        d, s = slot
        z2 = z if d == 0 else (z - d if s == 0 else z + d)
        if d == 0:
            f(z2)
        elif s == 0:
            pl.when(z >= d)(lambda: f(z2))
        else:
            pl.when(z < mp - d)(lambda: f(z2))

    def stage1(slot):
        d, s = slot

        def run(z2):
            for u in units:
                src = shards[u] if d == 0 else None
                if d > 0:
                    kind = 0 if s == 0 else 1
                    copy(u, kind, i, z2, (i, z)).wait_recv()
                if d == 0 or s == 0:
                    pl.when(z < mp - 1)(lambda u=u, src=src: copy(u, 0, i, z2, (i, z + 1), src).start())
                if d == 0 or s == 1:
                    pl.when(z > 0)(lambda u=u, src=src: copy(u, 1, i, z2, (i, z - 1), src).start())
                copy(u, 2, i, z2, (place.ix, z), src).start()
                copy(u, 3, i, z2, (place.iy, z), src).start()
                copy(u, 5, i, z2, (place.ic, z), src).start()
                if d == 0:
                    pltpu.make_async_copy(shards[u], here(u, i, z), local.at[u]).start()

        when(slot, run)

    def stage2(slot):
        def run(z2):
            for u in units:
                odd, first, second = route(u, z2)
                kind = 2 + odd
                spot = here(u, first, z2)
                pltpu.make_async_remote_copy(src_ref=spot, dst_ref=spot, send_sem=send.at[u, kind, z2],
                    recv_sem=recv.at[u, kind, z2], device_id=(first, z), device_id_type=MESH).wait_recv()
                copy(u, 4, first, z2, (second, z)).start()
                copy(u, 6, first, z2, (place.ic, z)).start()

        when(slot, run)

    def stage3(slot):
        def run(z2):
            for u in units:
                odd, first, second = route(u, z2)
                kind = 3 - odd
                spot = here(u, second, z2)
                pltpu.make_async_remote_copy(src_ref=spot, dst_ref=spot, send_sem=send.at[u, kind, z2],
                    recv_sem=recv.at[u, kind, z2], device_id=(second, z), device_id_type=MESH).wait_recv()
                copy(u, 7, second, z2, (place.ic, z)).start()
                copy(u, 4, place.ixy, z2, (second, z)).wait_recv()
                copy(u, 8, place.ixy, z2, (place.ic, z)).start()

        when(slot, run)

    def other(i2):
        return i2 + place.ic - i

    def finish(slot):
        d, s = slot

        def run(z2):
            for u in units:
                odd, first, second = route(u, z2)
                for kind, i2 in ((5, i), (6, first), (7, second), (8, place.ixy)):
                    copy(u, kind, other(i2), z2, (place.ic, z)).wait_recv()
                if d == 0 or s == 0:
                    pl.when(z < mp - 1)(lambda u=u: copy(u, 0, i, z2, (i, z)).wait_send())
                if d == 0 or s == 1:
                    pl.when(z > 0)(lambda u=u: copy(u, 1, i, z2, (i, z)).wait_send())
                for kind in range(2, 9):
                    copy(u, kind, i, z2, (i, z)).wait_send()
                if d == 0:
                    pltpu.make_async_copy(shards[u], here(u, i, z), local.at[u]).wait()

        when(slot, run)

    steps = []
    n = len(slots)
    for k in range(n + 2):
        if k < n:
            steps.append(functools.partial(stage1, slots[k]))
        if 0 <= k - 1 < n:
            steps.append(functools.partial(stage2, slots[k - 1]))
        if 0 <= k - 2 < n:
            steps.append(functools.partial(stage3, slots[k - 2]))
    for slot in slots:
        steps.append(functools.partial(finish, slot))
    return steps


def gather_shape(shard, kind, dp, mp):
    rows, cols = shard.shape
    if kind == "by_dp":
        return jax.ShapeDtypeStruct((mp, dp, rows, cols), shard.dtype)
    return jax.ShapeDtypeStruct((mp * rows, dp * cols), shard.dtype)


def gather_kernel(count, mp, *refs):
    shards, outs, (send, recv, local) = refs[:count], refs[count:2 * count], refs[2 * count:]
    place = Place(mp)
    enter(place)
    for step in gather_steps(place, shards, outs, send, recv, local):
        step()


def gather_weights(shards, kinds, dp, mp, cid, name):
    count = len(shards)
    any_space = pl.BlockSpec(memory_space=pl.ANY)
    sems = pltpu.SemaphoreType.DMA((count, 9, mp))
    return pl.pallas_call(
        functools.partial(gather_kernel, count, mp),
        out_shape=[gather_shape(s, k, dp, mp) for s, k in zip(shards, kinds)],
        in_specs=[any_space] * count, out_specs=[any_space] * count,
        scratch_shapes=[sems, sems, pltpu.SemaphoreType.DMA((count,))],
        compiler_params=pltpu.CompilerParams(collective_id=cid, has_side_effects=True),
        name=name,
    )(*shards)


def inverse_rms(state):
    return lax.rsqrt(jnp.mean(state * state, axis=-1, keepdims=True) + EPSILON)


def norm_back(state, gain, grad_normed):
    scale = inverse_rms(state)
    weighted = grad_normed * gain
    grad_gain = jnp.sum(grad_normed * state * scale, axis=0, keepdims=True)
    inner = jnp.mean(weighted * state, axis=-1, keepdims=True)
    return scale * weighted - state * (scale * scale * scale) * inner, grad_gain


def chunked(total, size, run):
    def once(n, carry):
        run(pl.multiple_of(n * size, size))
        return carry

    lax.fori_loop(0, total // size, once, 0)


def row_chunk(rows):
    for size in (272, 256, 128):
        if rows % size == 0:
            return size
    return rows


def full(array):
    return pl.BlockSpec(array.shape, lambda j: (0,) * len(array.shape))


def lead_block(array):
    return pl.BlockSpec((1,) + array.shape[1:], lambda j: (j,) + (0,) * (len(array.shape) - 1))


def col_block(array, parts):
    return pl.BlockSpec((array.shape[0], array.shape[1] // parts), lambda j: (0, j))


def row_block(array, parts):
    return pl.BlockSpec((array.shape[0] // parts, array.shape[1]), lambda j: (j, 0))


def kernel_call(body, name, steps, ins, outs, scratch, flops):
    return pl.pallas_call(
        body,
        grid=(steps,),
        out_shape=[jax.ShapeDtypeStruct(a.shape, a.dtype) for a, _ in outs],
        in_specs=[s for _, s in ins],
        out_specs=[s for _, s in outs],
        scratch_shapes=scratch,
        compiler_params=pltpu.CompilerParams(vmem_limit_bytes=60 << 20),
        cost_estimate=pl.CostEstimate(flops=flops, bytes_accessed=16 << 20, transcendentals=0),
        name=name,
    )(*[a for a, _ in ins])


def shape(dims, dtype=BF16):
    return jax.ShapeDtypeStruct(dims, dtype)


def project_kernel(front, x_ref, gain_ref, w_ref, q_ref, k_ref, v_ref, n_ref, normed):
    reach = x_ref.shape[0]
    padded, qcols = q_ref.shape
    kcols = k_ref.shape[1]
    rows = n_ref.shape[0]
    size = row_chunk(reach)

    @pl.when(pl.program_id(0) == 0)
    def _():
        def norm_rows(at):
            x = x_ref[pl.ds(at, size), :].astype(F32)
            normed[pl.ds(at, size), :] = (x * inverse_rms(x) * gain_ref[...]).astype(BF16)

        chunked(reach, size, norm_rows)
        n_ref[...] = normed[front : front + rows, :]

    q_ref[...] = mm(normed[front : front + padded, :], w_ref[0, :, :qcols]).astype(BF16)

    def keys(at):
        kv = mm(normed[pl.ds(at, size), :], w_ref[0, :, qcols:]).astype(BF16)
        k_ref[pl.ds(at, size), :] = kv[:, :kcols]
        v_ref[pl.ds(at, size), :] = kv[:, kcols:]

    chunked(reach, size, keys)


def self_project(x, gain, w, front, padded, rows):
    reach, width = x.shape
    groups, _, cols = w.shape
    q, k = shape((padded, groups * cols // 2)), shape((reach, groups * cols // 4))
    n = shape((rows, width))
    return kernel_call(
        functools.partial(project_kernel, front), "self_project", groups,
        [(x, full(x)), (gain, full(gain)), (w, lead_block(w))],
        [(q, col_block(q, groups)), (k, col_block(k, groups)), (k, col_block(k, groups)), (n, full(n))],
        [pltpu.VMEM(x.shape, BF16)], 2 * (reach + padded) * width * groups * cols // 2,
    )


def middle_kernel(o_ref, wo_ref, x_ref, gain_ref, m_ref, w_ref, h_ref, n_ref, q_ref, k_ref, v_ref):
    rows = x_ref.shape[0]
    qcols = q_ref.shape[1]
    kcols = k_ref.shape[1]
    size = row_chunk(rows)

    @pl.when(pl.program_id(0) == 0)
    def _():
        def state(at):
            some = pl.ds(at, size)
            h = x_ref[some, :].astype(F32) + mm(o_ref[some, :], wo_ref[...])
            h_ref[some, :] = h
            n_ref[some, :] = (h * inverse_rms(h) * gain_ref[...]).astype(BF16)

        chunked(rows, size, state)

    q_ref[0:rows, :] = mm(n_ref[...], w_ref[0, :, :qcols]).astype(BF16)
    q_ref[rows:, :] = jnp.zeros((q_ref.shape[0] - rows, qcols), BF16)
    kv = mm(m_ref[...], w_ref[0, :, qcols:]).astype(BF16)
    k_ref[...] = kv[:, :kcols]
    v_ref[...] = kv[:, kcols:]


def cross_project(o, wo, x, gain, memory, w):
    rows, width = x.shape
    groups, _, cols = w.shape
    h, n = shape(x.shape, F32), shape(x.shape)
    q = shape((o.shape[0], groups * cols // 2))
    k = shape((memory.shape[0], groups * cols // 4))
    return kernel_call(
        middle_kernel, "cross_project", groups,
        [(o, full(o)), (wo, full(wo)), (x, full(x)), (gain, full(gain)), (memory, full(memory)),
         (w, lead_block(w))],
        [(h, full(h)), (n, full(n)), (q, col_block(q, groups)), (k, col_block(k, groups)),
         (k, col_block(k, groups))],
        [], 6 * rows * width * width,
    )


def gate_parts(value):
    square = value * value
    inner = jnp.tanh(0.7978845608028654 * (value + 0.044715 * square * value))
    half = 0.5 * (1.0 + inner)
    slope = 0.7978845608028654 * (1.0 + 3.0 * 0.044715 * square)
    return value * half, half + 0.5 * value * (1.0 - inner * inner) * slope


def feed_kernel(
    o_ref, wo_ref, h1_ref, gain_ref, up_ref, wg_ref, wu_ref, wd_ref,
    out_ref, g2_ref, gain_out, gwg_ref, gwu_ref, gwd_ref, do_ref, gwo_ref,
    h2, normed, total, back, hidden_s, dgate_s, dup_s,
):
    rows, width = h1_ref.shape
    j = pl.program_id(0)
    size = row_chunk(rows)

    @pl.when(j == 0)
    def _():
        def state(at):
            some = pl.ds(at, size)
            h = h1_ref[some, :] + mm(o_ref[some, :], wo_ref[...])
            h2[some, :] = h
            normed[some, :] = (h * inverse_rms(h) * gain_ref[...]).astype(BF16)
            total[some, :] = h
            back[some, :] = jnp.zeros((size, width), F32)

        chunked(rows, size, state)

    def hidden_rows(at):
        some = pl.ds(at, size)
        n = normed[some, :]
        g = up_ref[some, :]
        gate = mm(n, wg_ref[0])
        up = mm(n, wu_ref[0])
        grad_hidden = mm_nt(g, wd_ref[...])
        active, pull = gate_parts(gate)
        hidden = (active * up).astype(BF16)
        grad_gate = (grad_hidden * up * pull).astype(BF16)
        grad_up = (grad_hidden * active).astype(BF16)
        hidden_s[some, :] = hidden
        dgate_s[some, :] = grad_gate
        dup_s[some, :] = grad_up
        total[some, :] += mm(hidden, wd_ref[...])
        back[some, :] += mm_nt(grad_gate, wg_ref[0]) + mm_nt(grad_up, wu_ref[0])

    chunked(rows, size, hidden_rows)

    def weight_rows(at):
        some = pl.ds(at, 128)
        n = normed[:, some]
        gwg_ref[0, some, :] = mm_tn(n, dgate_s[...]).astype(BF16)
        gwu_ref[0, some, :] = mm_tn(n, dup_s[...]).astype(BF16)
        gwd_ref[:, some] = mm_tn(hidden_s[...], up_ref[:, some]).astype(BF16)

    chunked(width, 128, weight_rows)

    @pl.when(j == pl.num_programs(0) - 1)
    def _():
        gain_out[...] = jnp.zeros_like(gain_out)
        do_ref[...] = jnp.zeros_like(do_ref)

        def finish(at):
            some = pl.ds(at, size)
            out_ref[some, :] = total[some, :].astype(BF16)
            change, grad_gain = norm_back(h2[some, :], gain_ref[...], back[some, :])
            gain_out[...] += grad_gain
            g2 = up_ref[some, :].astype(F32) + change
            g2_ref[some, :] = g2
            low = g2.astype(BF16)
            normed[some, :] = low
            do_ref[some, :] = mm_nt(low, wo_ref[...]).astype(BF16)

        chunked(rows, size, finish)

        def out_rows(at):
            some = pl.ds(at, 256)
            gwo_ref[some, :] = mm_tn(o_ref[0:rows, some], normed[...]).astype(BF16)

        chunked(width, 256, out_rows)


def feed(o, wo, h1, gain, upstream, wg, wu, wd):
    rows, width = h1.shape
    groups, _, cols = wg.shape
    out, g2, gg = shape(h1.shape), shape(h1.shape, F32), shape((1, width), F32)
    return kernel_call(
        feed_kernel, "feed", groups,
        [(o, full(o)), (wo, full(wo)), (h1, full(h1)), (gain, full(gain)), (upstream, full(upstream)),
         (wg, lead_block(wg)), (wu, lead_block(wu)), (wd, row_block(wd, groups))],
        [(out, full(out)), (g2, full(g2)), (gg, full(gg)), (wg, lead_block(wg)), (wu, lead_block(wu)),
         (wd, row_block(wd, groups)), (o, full(o)), (wo, full(wo))],
        [pltpu.VMEM((rows, width), F32), pltpu.VMEM((rows, width), BF16), pltpu.VMEM((rows, width), F32),
         pltpu.VMEM((rows, width), F32)] + [pltpu.VMEM((rows, cols), BF16)] * 3,
        18 * rows * width * groups * cols,
    )


def back_kernel(
    dq_ref, w_ref, n_ref, h_ref, gain_ref, g2_ref, wo_ref, o_ref,
    gw_ref, g1_ref, gain_out, do_ref, gwo_ref, back, low_s,
):
    rows, width = h_ref.shape
    qcols = dq_ref.shape[1]
    j = pl.program_id(0)
    size = row_chunk(rows)

    @pl.when(j == 0)
    def _():
        back[...] = jnp.zeros_like(back)

    back[...] += mm_nt(dq_ref[0:rows, :], w_ref[0, :, :qcols])

    def weight_rows(at):
        some = pl.ds(at, 256)
        gw_ref[0, some, :] = mm_tn(n_ref[:, some], dq_ref[0:rows, :]).astype(BF16)

    chunked(width, 256, weight_rows)

    @pl.when(j == pl.num_programs(0) - 1)
    def _():
        gain_out[...] = jnp.zeros_like(gain_out)
        do_ref[...] = jnp.zeros_like(do_ref)

        def finish(at):
            some = pl.ds(at, size)
            change, grad_gain = norm_back(h_ref[some, :], gain_ref[...], back[some, :])
            gain_out[...] += grad_gain
            g1 = g2_ref[some, :] + change
            g1_ref[some, :] = g1
            low = g1.astype(BF16)
            low_s[some, :] = low
            do_ref[some, :] = mm_nt(low, wo_ref[...]).astype(BF16)

        chunked(rows, size, finish)

        def out_rows(at):
            some = pl.ds(at, 256)
            gwo_ref[some, :] = mm_tn(o_ref[0:rows, some], low_s[...]).astype(BF16)

        chunked(width, 256, out_rows)


def cross_back(dq, w, n, h, gain, g2, wo, o):
    rows, width = h.shape
    groups, _, cols = w.shape
    gw = shape((groups, width, cols // 2))
    gg = shape((1, width), F32)
    return kernel_call(
        back_kernel, "cross_back", groups,
        [(dq, col_block(dq, groups)), (w, lead_block(w)), (n, full(n)), (h, full(h)), (gain, full(gain)),
         (g2, full(g2)), (wo, full(wo)), (o, full(o))],
        [(gw, lead_block(gw)), (g2, full(g2)), (gg, full(gg)), (o, full(o)), (wo, full(wo))],
        [pltpu.VMEM((rows, width), F32), pltpu.VMEM((rows, width), BF16)],
        8 * rows * width * width,
    )


def memory_kernel(dk_ref, dv_ref, w_ref, m_ref, gw_ref, gm_ref, back):
    j = pl.program_id(0)
    qcols = w_ref.shape[2] // 2
    kcols = qcols // 2

    @pl.when(j == 0)
    def _():
        back[...] = jnp.zeros_like(back)

    both = jnp.concatenate([dk_ref[...], dv_ref[...]], axis=1)
    back[...] += mm_nt(both, w_ref[0, :, qcols:])
    gw_ref[0] = mm_tn(m_ref[...], both).astype(BF16)

    @pl.when(j == pl.num_programs(0) - 1)
    def _():
        gm_ref[...] = back[...].astype(BF16)


def memory_back(dk, dv, w, memory):
    groups, width, cols = w.shape
    gw = shape((groups, width, cols // 2))
    return kernel_call(
        memory_kernel, "memory_back", groups,
        [(dk, col_block(dk, groups)), (dv, col_block(dv, groups)), (w, lead_block(w)), (memory, full(memory))],
        [(gw, lead_block(gw)), (memory, full(memory))],
        [pltpu.VMEM(memory.shape, F32)], 4 * memory.shape[0] * width * width,
    )


def last_kernel(
    dq_ref, dk_ref, dv_ref, w_ref, n_ref, x_ref, gain_ref, g1_ref,
    gwq_ref, gwkv_ref, gx_ref, gain_out, back,
):
    rows, width = x_ref.shape
    j = pl.program_id(0)
    size = row_chunk(rows)

    @pl.when(j == 0)
    def _():
        back[...] = jnp.zeros_like(back)

    dq = dq_ref[0:rows, :]
    dkv = jnp.concatenate([dk_ref[...], dv_ref[...]], axis=1)
    both = jnp.concatenate([dq, dkv], axis=1)
    back[...] += mm_nt(both, w_ref[0])

    def weight_rows(at):
        some = pl.ds(at, 256)
        gwq_ref[0, some, :] = mm_tn(n_ref[:, some], dq).astype(BF16)
        gwkv_ref[0, some, :] = mm_tn(n_ref[:, some], dkv).astype(BF16)

    chunked(width, 256, weight_rows)

    @pl.when(j == pl.num_programs(0) - 1)
    def _():
        gain_out[...] = jnp.zeros_like(gain_out)

        def finish(at):
            some = pl.ds(at, size)
            change, grad_gain = norm_back(x_ref[some, :].astype(F32), gain_ref[...], back[some, :])
            gain_out[...] += grad_gain
            gx_ref[some, :] = (g1_ref[some, :] + change).astype(BF16)

        chunked(rows, size, finish)


def self_back(dq, dk, dv, w, n, x, gain, g1):
    rows, width = x.shape
    groups, _, cols = w.shape
    gw = shape((groups, width, cols // 2))
    gg = shape((1, width), F32)
    return kernel_call(
        last_kernel, "self_back", groups,
        [(dq, col_block(dq, groups)), (dk, col_block(dk, groups)), (dv, col_block(dv, groups)),
         (w, lead_block(w)), (n, full(n)), (x, full(x)), (gain, full(gain)), (g1, full(g1))],
        [(gw, lead_block(gw)), (gw, lead_block(gw)), (x, full(x)), (gg, full(gg))],
        [pltpu.VMEM((rows, width), F32)],
        8 * rows * width * width,
    )


def gather(shard, dims):
    for axis, name in dims:
        shard = lax.all_gather(shard, name, axis=axis, tiled=True)
    return shard


ROWS_BY_DP = ((0, "dp"), (1, "mp"))
ROWS_BY_MP = ((1, "dp"), (0, "mp"))


def scatter(grad, dims):
    for axis, name in dims:
        grad = lax.psum_scatter(grad, name, scatter_dimension=axis, tiled=True)
    return grad.astype(F32)


def grouped(weight, groups):
    rows, cols = weight.shape
    return weight.reshape(rows, groups, cols // groups).transpose(1, 0, 2)


def ungrouped(weight):
    groups, rows, cols = weight.shape
    return weight.transpose(1, 0, 2).reshape(rows, groups * cols)


def body(
    inputs,
    encoded,
    decoder_segments,
    encoder_segments,
    buckets,
    self_gain,
    self_query,
    self_key,
    self_value,
    self_out,
    position_bias,
    cross_gain,
    cross_query,
    cross_key,
    cross_value,
    cross_out,
    feed_gain,
    feed_gate,
    feed_up,
    feed_down,
    cotangent,
    *,
    dp,
    mp,
):
    batches, length, width = inputs.shape
    enc_length = encoded.shape[1]
    parts = mp // batches
    rows = length // parts
    enc_rows = enc_length // parts
    place = lax.axis_index("mp")
    sequence = place // parts
    part = place % parts
    first = part * rows
    enc_first = part * enc_rows

    groups = self_key.shape[1] * mp // (2 * HEAD_DIM)
    native = mp == groups and dp == 8 and rows % 16 == 0

    gains = [gather(g, ((0, "dp"),)).astype(F32)[None] for g in (self_gain, cross_gain, feed_gain)]
    gain_one, gain_two, gain_three = gains
    table = gather(position_bias, ROWS_BY_DP).astype(F32)
    if native:
        order = ["by_dp", "by_mp"]
        w1 = jnp.concatenate([self_query, self_key, self_value], axis=1)
        w2 = jnp.concatenate([cross_query, cross_key, cross_value], axis=1)
        w1, wo1 = gather_weights([w1, self_out], order, dp, mp, 1, "gather_self")
        w2, wo2 = gather_weights([w2, cross_out], order, dp, mp, 2, "gather_cross")
        wg, wu, wd = gather_weights(
            [feed_gate, feed_up, feed_down], ["by_dp"] + order, dp, mp, 3, "gather_feed"
        )
        w1, w2, wg, wu = (w.reshape(mp, width, w.shape[3]) for w in (w1, w2, wg, wu))
    else:

        def blocks(*shards):
            return jnp.concatenate([grouped(gather(s, ROWS_BY_DP), groups) for s in shards], axis=2)

        w1 = blocks(self_query, self_key, self_value)
        w2 = blocks(cross_query, cross_key, cross_value)
        wg, wu = blocks(feed_gate), blocks(feed_up)
        wo1, wo2, wd = (gather(s, ROWS_BY_MP) for s in (self_out, cross_out, feed_down))

    whole = lax.dynamic_index_in_dim(inputs, sequence, keepdims=False)
    memory = lax.dynamic_index_in_dim(encoded, sequence, keepdims=False)
    docs = lax.dynamic_index_in_dim(decoder_segments, sequence, keepdims=False)
    enc_docs = lax.dynamic_index_in_dim(encoder_segments, sequence, keepdims=False)
    upstream = lax.dynamic_slice(cotangent, (sequence, first, 0), (1, rows, width))[0]

    def own(array):
        return lax.dynamic_slice_in_dim(array, first, rows, axis=0)

    padded = round_up(rows, TILE_Q)
    tiles = padded // TILE_Q
    front = round_up(length - rows, TILE_K)
    reach = ((rows - 1 + front) // TILE_K + 1) * TILE_K
    lead = TILE_K
    spread = (tiles - 1) * TILE_Q + front + lead + TILE_Q
    kinds = jnp.arange(4, dtype=jnp.int32)
    before = jnp.sum((docs[None, :] < kinds[:, None]).astype(jnp.int32), axis=1)
    enc_before = jnp.sum((enc_docs[None, :] < kinds[:, None]).astype(jnp.int32), axis=1)
    enc_until = jnp.sum((enc_docs[None, :] <= kinds[:, None]).astype(jnp.int32), axis=1)
    own_docs = own(docs)
    is_doc = (own_docs[:, None] == kinds[None, :]).astype(jnp.int32)
    start = jnp.sum(is_doc * before[None, :], axis=1) - first + front
    start = jnp.pad(start, (0, padded - rows), constant_values=1 << 20)
    tile_first = jnp.arange(tiles, dtype=jnp.int32) * TILE_Q
    tile_last = jnp.minimum(tile_first + TILE_Q - 1, rows - 1)
    lo_one = start[::TILE_Q] // TILE_K
    hi_one = (tile_last + front) // TILE_K + 1
    doc_first = own_docs[::TILE_Q]
    doc_last = jnp.concatenate([own_docs[TILE_Q - 1 :: TILE_Q], own_docs[-1:]])[:tiles]
    lo_two = jnp.sum((doc_first[:, None] == kinds) * enc_before[None, :], axis=1) // TILE_K
    hi_two = (jnp.sum((doc_last[:, None] == kinds) * enc_until[None, :], axis=1) - 1) // TILE_K + 1
    bounds_one = (lo_one.astype(jnp.int32), hi_one.astype(jnp.int32))
    bounds_two = (lo_two.astype(jnp.int32), hi_two.astype(jnp.int32))
    mask_one = start[None, :]
    mask_two = jnp.pad(own_docs, (0, padded - rows), constant_values=-1)[None, :]
    keys_two = jnp.broadcast_to(enc_docs[:, None], (enc_length, TILE_Q))

    onehot = (buckets[:, None] == jnp.arange(table.shape[0], dtype=jnp.int32)).astype(F32)
    by_distance = dot(table, onehot, ((0,), (1,)), HIGHEST)
    heads = by_distance.shape[0]
    vec = jnp.concatenate(
        [
            jnp.full((heads, lead), NEGATIVE, F32),
            by_distance,
            jnp.zeros((heads, max(0, spread - lead - length)), F32),
        ],
        axis=1,
    )[:, :spread]
    vec = vec.reshape(heads // 4, 4, spread)

    back_pad = max(0, reach - front - rows)
    window = jnp.pad(whole, ((front, back_pad), (0, 0)))
    window = lax.dynamic_slice_in_dim(window, first, reach, axis=0)
    x = own(whole)
    q1, k1, v1, n1 = self_project(window, gain_one, w1, front, padded, rows)
    o1, lse_one = attend_forward(
        q1, k1, v1, mask_one, vec, bounds_one, front, lead, True, "self_forward"
    )
    h1, n2, q2, k2, v2 = cross_project(o1, wo1, x, gain_two, memory, w2)
    o2, lse_two = attend_forward(
        q2, k2, v2, mask_two, keys_two, bounds_two, 0, 0, False, "cross_forward"
    )

    result, grad_two, grad_gain_three, gwg, gwu, gwd, do2, gwo2 = feed(
        o2, wo2, h1, gain_three, upstream, wg, wu, wd
    )
    outputs = lax.all_gather(result, "mp", axis=0, tiled=True).reshape(inputs.shape)

    dq2, dk2, dv2 = attend_backward(
        q2, k2, v2, o2, do2, lse_two, mask_two, keys_two, bounds_two, 0, 0, False, "cross_backward"
    )
    sharing = [[s * parts + p for p in range(parts)] for s in range(batches)]

    def share(array):
        return lax.psum_scatter(
            array, "mp", scatter_dimension=0, axis_index_groups=sharing, tiled=True
        )

    gwq2, grad_one, grad_gain_two, do1, gwo1 = cross_back(
        dq2, w2, n2, h1, gain_two, grad_two, wo1, o1
    )
    dkv2 = share(jnp.concatenate([dk2, dv2], axis=1))
    half = dkv2.shape[1] // 2
    own_memory = lax.dynamic_slice_in_dim(memory, enc_first, enc_rows, axis=0)
    gwkv2, grad_memory = memory_back(dkv2[:, :half], dkv2[:, half:], w2, own_memory)
    grad_encoded = lax.all_gather(grad_memory, "mp", axis=0, tiled=True).reshape(encoded.shape)

    dq1, dk1, dv1, slopes = attend_backward(
        q1, k1, v1, o1, do1, lse_one, mask_one, vec, bounds_one, front, lead, True, "self_backward"
    )
    dkv1 = jnp.concatenate([dk1, dv1], axis=1)
    dkv1 = jnp.pad(dkv1, ((0, max(0, front + length - reach)), (0, 0)))
    dkv1 = share(lax.dynamic_slice_in_dim(dkv1, front - first, length, axis=0))
    gwq1, gwkv1, grad_rows, grad_gain_one = self_back(
        dq1, dkv1[:, :half], dkv1[:, half:], w1, n1, x, gain_one, grad_one
    )
    grad_inputs = lax.all_gather(grad_rows, "mp", axis=0, tiled=True).reshape(inputs.shape)
    slopes = slopes.reshape(heads, spread)[:, lead : lead + length]
    slopes = jnp.pad(slopes, ((0, 0), (0, length - slopes.shape[1])))
    grad_table = dot(onehot, slopes, ((0,), (1,)), HIGHEST)

    small = jnp.concatenate(
        [grad_gain_one[0], grad_gain_two[0], grad_gain_three[0], grad_table.reshape(-1)]
    )
    small = lax.psum(small, ("dp", "mp"))
    data = lax.axis_index("dp")

    def gain_block(index):
        size = width // dp
        return lax.dynamic_slice_in_dim(small, index * width + data * size, size, axis=0)

    grad_table = small[3 * width :].reshape(table.shape)
    grad_table = lax.dynamic_slice(
        grad_table,
        (data * position_bias.shape[0], place * position_bias.shape[1]),
        position_bias.shape,
    )
    kcols = gwkv1.shape[2] // 2

    def summed(grad):
        if native:
            grad = lax.psum_scatter(grad, "mp", scatter_dimension=0, tiled=True)
            return lax.psum_scatter(grad[0], "dp", scatter_dimension=0, tiled=True).astype(F32)
        return scatter(ungrouped(grad), ROWS_BY_DP)

    return (
        outputs,
        grad_inputs,
        grad_encoded,
        gain_block(0),
        summed(gwq1),
        summed(gwkv1[:, :, :kcols]),
        summed(gwkv1[:, :, kcols:]),
        scatter(gwo1, ROWS_BY_MP),
        grad_table,
        gain_block(1),
        summed(gwq2),
        summed(gwkv2[:, :, :kcols]),
        summed(gwkv2[:, :, kcols:]),
        scatter(gwo2, ROWS_BY_MP),
        gain_block(2),
        summed(gwg),
        summed(gwu),
        scatter(gwd, ROWS_BY_MP),
    )


def solution(mesh):
    rows3 = P("dp", None, None)
    by_dp = P("dp", "mp")
    by_mp = P("mp", "dp")
    gain = P("dp")
    return jax.shard_map(
        functools.partial(body, dp=mesh.shape["dp"], mp=mesh.shape["mp"]),
        mesh=mesh,
        in_specs=(
            rows3, rows3, P("dp", None), P("dp", None), P(),
            gain, by_dp, by_dp, by_dp, by_mp, by_dp,
            gain, by_dp, by_dp, by_dp, by_mp,
            gain, by_dp, by_dp, by_mp, rows3,
        ),
        out_specs=(
            rows3, rows3, rows3,
            gain, by_dp, by_dp, by_dp, by_mp, by_dp,
            gain, by_dp, by_dp, by_dp, by_mp,
            gain, by_dp, by_dp, by_mp,
        ),
        check_vma=False,
    )
```

time: 3060 us -> 1780 us (0.58); the launches traced: 3020 us -> 1770 us
  local copies, waits for them, and re-layouts: 1240 us -> 69.3 us
  Pallas kernels: 0 us -> 487 us
  matrix products: 343 us -> 0.94 us
  other arithmetic: 196 us -> 25.8 us
  blocking collectives: 133 us -> 84.7 us
    psum x6 -> x0, waiting for transfers between devices: 1080 us -> none  [the longest x5 1080 us: collect(): return lax.psum(partial_value, 'mp')]
    unnamed x360 -> x58, local copies, waits for them, and re-layouts: 889 us -> 37.1 us
    reduce_scatter x4 -> x21, waiting for transfers between devices: 0.03 us -> 747 us  [the longest x8 422 us: summed(): grad = lax.psum_scatter(grad, 'mp', scatter_dimension=0, tiled=True)]
    pallas_call x0 -> x13, Pallas kernels: none -> 487 us  [the longest x4 196 us: attention_call(): pl.pallas_call(functools.partial(kernel, biased, front, lead), out_shape=...]
    dot_general x93 -> x2, matrix products: 343 us -> 0.94 us  [dot(): lax.dot_general(left, right, ((dims[0], dims[1]), ((), ())), precision=pr...]
    reshape x5 -> x4, local copies, waits for them, and re-layouts: 228 us -> 0.87 us  [the longest x1 0.67 us: body(): vec = vec.reshape(heads // 4, 4, spread)]
    all_gather x3, waiting for transfers between devices: 0.01 us -> 212 us  [the longest x1 84.1 us: body(): lax.all_gather(result, 'mp', axis=0, tiled=True).reshape(inputs.shape)]
    unnamed x27 -> x30, waiting for transfers between devices: 1.9 us -> 126 us
  transfers between devices with their start and end apart: 20 -> 27, of which waited for: 4 -> 25; matrix products, arithmetic and copies ran while one was open for 41% -> 3% of each run, Pallas kernels for 0% -> 6%
where the time goes in v1:
time: 1780 us; the launch traced here: 1770 us
  waiting for transfers between devices  1090 us (61%)
  Pallas kernels  487 us (27%)
  blocking collectives  84.7 us (5%)
  local copies, waits for them, and re-layouts  69.3 us (4%)
  other arithmetic  25.8 us (1%)
    reduce_scatter x8, waiting for transfers between devices, summed(): grad = lax.psum_scatter(grad, 'mp', scatter_dimension=0, tiled=True)  422 us
    reduce_scatter x8, waiting for transfers between devices, summed(): lax.psum_scatter(grad[0], 'dp', scatter_dimension=0, tiled=True).astype(F32)  256 us
    pallas_call x4, Pallas kernels, attention_call(): pl.pallas_call(functools.partial(kernel, biased, front, lead), out_shape=...  196 us
    pallas_call x3, Pallas kernels, gather_weights(): pl.pallas_call(functools.partial(gather_kernel, count, mp), out_shape=[ga...  162 us
    pallas_call x6, Pallas kernels, kernel_call(): pl.pallas_call(body, grid=(steps,), out_shape=[jax.ShapeDtypeStruct(a.sha...  129 us
    unnamed x30, waiting for transfers between devices  126 us
    all_gather x1, waiting for transfers between devices, body(): lax.all_gather(result, 'mp', axis=0, tiled=True).reshape(inputs.shape)  84.1 us
    all_gather x1, waiting for transfers between devices, body(): lax.all_gather(grad_rows, 'mp', axis=0, tiled=True).reshape(inputs.shape)  83.5 us
  transfers between devices with their start and end apart: 27, of which 25 were waited for; matrix products, arithmetic and copies ran while one was open for 3% of the time, Pallas kernels for 6%

profile of v1, /device:TPU:8, one launch (start us, length us, event | category | flops | bytes accessed | tf_op | source)
XLA Modules:
  0.0 1770.1 jit_solution(13365358085236884632)
XLA Ops:
  75.6 35.8 %gather_self.1 = (bf16[4,8,128,512]{3,2,1,0:T(8,128)(2,1)}, bf16[1024,1024]{1,0:T(8,128)(2,1)}) custom-call(bf16[128,512]{1,0:T(8,128)(2,1)} %pad_maximum_fusion.1.refs_0_, bf16[256,128]{1,0:T(8,128)(2,1)} %refs_1_.3), custom_call_target="tpu_custom_call" | custom-call | tf_op jit(solution)/shard_map/gather_self/pallas_call | solution.py:498
  112.1 39.1 %gather_cross.1 = (bf16[4,8,128,512]{3,2,1,0:T(8,128)(2,1)}, bf16[1024,1024]{1,0:T(8,128)(2,1)}) custom-call(bf16[128,512]{1,0:T(8,128)(2,1)} %pad_maximum_fusion.2.refs_0_, bf16[256,128]{1,0:T(8,128)(2,1)} %refs_1_.4), custom_call_target="tpu_custom_call" | custom-call | tf_op jit(solution)/shard_map/gather_cross/pallas_call | solution.py:498
  165.6 87.1 %gather_feed.1 = (bf16[4,8,128,704]{3,2,1,0:T(8,128)(2,1)}, bf16[4,8,128,704]{3,2,1,0:T(8,128)(2,1)}, bf16[2816,1024]{1,0:T(8,128)(2,1)}) custom-call(bf16[128,704]{1,0:T(8,128)(2,1)} %copy.57.refs_0_, bf16[128,704]{1,0:T(8,128)(2,1)} %copy.58.refs_1_, bf16[704,128]{1,0:T(8,128)(2,1)} %refs_2_.1), custom_call_target="tpu_custom_call" | custom-call | tf_op jit(solution)/shard_map/gather_feed/pallas_call | solution.py:498
  252.7 56.8 %self_forward.1 = (bf16[640,1024]{1,0:T(8,128)(2,1)}, f32[4,4,640]{2,1,0:T(4,128)}) custom-call(s32[5]{0:T(128)} %get-tuple-element.197.lo_ref, s32[5]{0:T(128)} %get-tuple-element.198.hi_ref, bf16[640,1024]{1,0:T(8,128)(2,1)} %get-tuple-element.65.refs_0_, bf16[1536,512]{1,0:T(8,128)(2,1)} %get-tuple-element.66.refs_1_, ...), custom_call_target="tpu_custom_call" | custom-call | flops 4026531840 | bytes 16777216 | tf_op jit(solution)/shard_map/self_forward/pallas_call | solution.py:250
  320.4 33.2 %cross_forward.1 = (bf16[640,1024]{1,0:T(8,128)(2,1)}, f32[4,4,640]{2,1,0:T(4,128)}) custom-call(s32[5]{0:T(128)} %and_select_fusion.3.lo_ref, s32[5]{0:T(128)} %fusion.10.hi_ref, bf16[640,1024]{1,0:T(8,128)(2,1)} %get-tuple-element.71.refs_0_, bf16[512,512]{1,0:T(8,128)(2,1)} %get-tuple-element.72.refs_1_, bf16[512,512]{1,0:T(8,128)(2,1)} %get-tuple-element.73.refs_2_, ...), custom_call_target="tpu_custom_call" | custom-call | flops 1342177280 | bytes 16777216 | tf_op jit(solution)/shard_map/cross_forward/pallas_call | solution.py:250
  353.6 63.1 %feed.1 = (bf16[544,1024]{1,0:T(8,128)(2,1)}, f32[544,1024]{1,0:T(8,128)}, f32[1,1024]{1,0:T(1,128)}, bf16[4,1024,704]{2,1,0:T(8,128)(2,1)}, bf16[4,1024,704]{2,...) custom-call(bf16[640,1024]{1,0:T(8,128)(2,1)} %get-tuple-element.74.o_ref.refs_, ...), custom_call_target="tpu_custom_call" | custom-call | flops 28236054528 | bytes 16777216 | tf_op jit(solution)/shard_map/feed/pallas_call | solution.py:552
  416.7 36.4 %cross_backward.1 = (bf16[640,1024]{1,0:T(8,128)(2,1)}, bf16[512,512]{1,0:T(8,128)(2,1)}, bf16[512,512]{1,0:T(8,128)(2,1)}) custom-call(s32[5]{0:T(128)} %and_select_fusion.3.lo_ref, s32[5]{0:T(128)} %fusion.10.hi_ref, bf16[640,1024]{1,0:T(8,128)(2,1)} %get-tuple-element.71.refs_0_, bf16[512,512]{1,0:T(8,128)(2,1)} %get-tuple-element.72.refs_1_, ...), custom_call_target="tpu_custom_call" | custom-call | flops 3355443200 | bytes 16777216 | tf_op jit(solution)/shard_map/cross_backward/pallas_call | solution.py:250
  475.2 69.7 %self_backward.1 = (bf16[640,1024]{1,0:T(8,128)(2,1)}, bf16[1536,512]{1,0:T(8,128)(2,1)}, bf16[1536,512]{1,0:T(8,128)(2,1)}, f32[4,4,1664]{2,1,0:T(4,128)}) custom-call(s32[5]{0:T(128)} %get-tuple-element.197.lo_ref, s32[5]{0:T(128)} %get-tuple-element.198.hi_ref, bf16[640,1024]{1,0:T(8,128)(2,1)} %get-tuple-element.65.refs_0_, ...), custom_call_target="tpu_custom_call" | custom-call | flops 10066329600 | bytes 16777216 | tf_op jit(solution)/shard_map/self_backward/pallas_call | solution.py:250
  626.9 42.9 %reduce-scatter.75.cloned.1.call-done = bf16[128,1024]{1,0:T(8,128)(2,1)} async-done(((bf16[1024,1024]{1,0:T(8,128)(2,1)}), bf16[128,1024]{1,0:T(8,128)(2,1)}) %reduce-scatter.75.cloned.1.call-update) | async-done | bytes 262160
  725.2 44.6 %reduce-scatter.49.cloned.1.call-done = bf16[1,1024,256]{2,1,0:T(8,128)(2,1)} async-done(((bf16[4,1024,256]{2,1,0:T(8,128)(2,1)}), bf16[1,1024,256]{2,1,0:T(8,128)(2,1)}) %reduce-scatter.49.cloned.1.call-update) | async-done | bytes 524304 | tf_op jit(solution)/shard_map/reduce_scatter | solution.py:1096
  827.0 45.1 %reduce-scatter.35.cloned.1.call-done = bf16[1,1024,256]{2,1,0:T(8,128)(2,1)} async-done(((bf16[4,1024,256]{2,1,0:T(8,128)(2,1)}), bf16[1,1024,256]{2,1,0:T(8,128)(2,1)}) %reduce-scatter.35.cloned.1.call-update) | async-done | bytes 524304 | tf_op jit(solution)/shard_map/reduce_scatter | solution.py:1096
  872.2 64.1 %reduce-scatter.77.cloned.1.call-done = bf16[128,2816]{1,0:T(8,128)(2,1)} async-done(((bf16[1024,2816]{1,0:T(8,128)(2,1)}), bf16[128,2816]{1,0:T(8,128)(2,1)}) %reduce-scatter.77.cloned.1.call-update) | async-done | bytes 720912
  939.4 109.9 %reduce-scatter.63.cloned.1.call-done = bf16[1,1024,704]{2,1,0:T(8,128)(2,1)} async-done(((bf16[4,1024,704]{2,1,0:T(8,128)(2,1)}), bf16[1,1024,704]{2,1,0:T(8,128)(2,1)}) %reduce-scatter.63.cloned.1.call-update) | async-done | bytes 1441808 | tf_op jit(solution)/shard_map/reduce_scatter | solution.py:1096
  1049.4 113.6 %reduce-scatter.67.cloned.1.call-done = bf16[1,1024,704]{2,1,0:T(8,128)(2,1)} async-done(((bf16[4,1024,704]{2,1,0:T(8,128)(2,1)}), bf16[1,1024,704]{2,1,0:T(8,128)(2,1)}) %reduce-scatter.67.cloned.1.call-update) | async-done | bytes 1441808 | tf_op jit(solution)/shard_map/reduce_scatter | solution.py:1096
  1205.2 42.4 %psum.7 = f32[3584]{0:T(1024)S(1)} all-reduce(f32[3584]{0:T(1024)S(1)} %pad_maximum_fusion.3), channel_id=1, replica_groups=mesh['dp'=8,'mp'=4] {'dp','mp'}, use_global_device_ids=true, to_apply=%region_8.9 | all-reduce | flops 3584 | bytes 28672 | tf_op jit(solution)/shard_map/psum | solution.py:1079
  1279.5 36.0 %reduce-scatter.51.cloned.1.call-done = bf16[128,256]{1,0:T(8,128)(2,1)} async-done(((bf16[1024,256]{1,0:T(8,128)(2,1)}), bf16[128,256]{1,0:T(8,128)(2,1)}) %reduce-scatter.51.cloned.1.call-update) | async-done | bytes 65552 | tf_op jit(solution)/shard_map/reduce_scatter | solution.py:1097
  1317.0 44.4 %all-gather.13.cloned.1.call-done = bf16[1024,1024]{1,0:T(8,128)(2,1)} async-done(((bf16[256,1024]{1,0:T(8,128)(2,1)}), bf16[1024,1024]{1,0:T(8,128)(2,1)}) %all-gather.13.cloned.1.call-update) | async-done | bytes 2097168 | tf_op jit(solution)/shard_map/all_gather | solution.py:1060
  1361.5 84.1 %all-gather.9.cloned.1.call-done = bf16[2176,1024]{1,0:T(8,128)(2,1)} async-done(((bf16[544,1024]{1,0:T(8,128)(2,1)}), bf16[2176,1024]{1,0:T(8,128)(2,1)}) %all-gather.9.cloned.1.call-update) | async-done | bytes 4456464 | tf_op jit(solution)/shard_map/all_gather | solution.py:1041
  1445.6 37.9 %reduce-scatter.41.cloned.1.call-done = bf16[128,128]{1,0:T(8,128)(2,1)} async-done(((bf16[1024,128]{1,0:T(8,128)(2,1)}), bf16[128,128]{1,0:T(8,128)(2,1)}) %reduce-scatter.41.cloned.1.call-update) | async-done | bytes 32784 | tf_op jit(solution)/shard_map/reduce_scatter | solution.py:1097
  1484.9 35.5 %reduce-scatter.45.cloned.1.call-done = bf16[128,128]{1,0:T(8,128)(2,1)} async-done(((bf16[1024,128]{1,0:T(8,128)(2,1)}), bf16[128,128]{1,0:T(8,128)(2,1)}) %reduce-scatter.45.cloned.1.call-update) | async-done | bytes 32784 | tf_op jit(solution)/shard_map/reduce_scatter | solution.py:1097
  1521.8 35.9 %reduce-scatter.37.cloned.1.call-done = bf16[128,256]{1,0:T(8,128)(2,1)} async-done(((bf16[1024,256]{1,0:T(8,128)(2,1)}), bf16[128,256]{1,0:T(8,128)(2,1)}) %reduce-scatter.37.cloned.1.call-update) | async-done | bytes 65552 | tf_op jit(solution)/shard_map/reduce_scatter | solution.py:1097
  1582.9 83.5 %all-gather.11.cloned.1.call-done = bf16[2176,1024]{1,0:T(8,128)(2,1)} async-done(((bf16[544,1024]{1,0:T(8,128)(2,1)}), bf16[2176,1024]{1,0:T(8,128)(2,1)}) %all-gather.11.cloned.1.call-update) | async-done | bytes 4456464 | tf_op jit(solution)/shard_map/all_gather | solution.py:1071
  1666.4 43.2 %reduce-scatter.65.cloned.1.call-done = bf16[128,704]{1,0:T(8,128)(2,1)} async-done(((bf16[1024,704]{1,0:T(8,128)(2,1)}), bf16[128,704]{1,0:T(8,128)(2,1)}) %reduce-scatter.65.cloned.1.call-update) | async-done | bytes 180240 | tf_op jit(solution)/shard_map/reduce_scatter | solution.py:1097
  1711.3 40.2 %reduce-scatter.69.cloned.1.call-done = bf16[128,704]{1,0:T(8,128)(2,1)} async-done(((bf16[1024,704]{1,0:T(8,128)(2,1)}), bf16[128,704]{1,0:T(8,128)(2,1)}) %reduce-scatter.69.cloned.1.call-update) | async-done | bytes 180240 | tf_op jit(solution)/shard_map/reduce_scatter | solution.py:1097
  (195 shorter events, 430.5 us)
Async XLA Ops:
  7.2 551.2 %reduce-scatter.33.cloned.1.call-start = ((), (), s32[]{:S(2)}) async-start(), calls=%async_computation.27 | async-start | bytes 1572864 | tf_op jit(solution)/shard_map/reduce_scatter | solution.py:1049
  557.4 139.7 %reduce-scatter.53.cloned.1.call-start = ((), (), s32[]{:S(2)}) async-start(), calls=%async_computation.38 | async-start | bytes 1310720 | tf_op jit(solution)/shard_map/reduce_scatter | solution.py:1096
  569.1 156.0 %reduce-scatter.57.cloned.1.call-start = ((), (), s32[]{:S(2)}) async-start(), calls=%async_computation.40 | async-start | bytes 1310720 | tf_op jit(solution)/shard_map/reduce_scatter | solution.py:1096
  569.7 200.1 %reduce-scatter.49.cloned.1.call-start = ((), (), s32[]{:S(2)}) async-start(), calls=%async_computation.36 | async-start | bytes 2621440 | tf_op jit(solution)/shard_map/reduce_scatter | solution.py:1096
  570.4 228.4 %reduce-scatter.39.cloned.1.call-start = ((), (), s32[]{:S(2)}) async-start(), calls=%async_computation.31 | async-start | bytes 1310720 | tf_op jit(solution)/shard_map/reduce_scatter | solution.py:1096
  600.1 226.8 %reduce-scatter.43.cloned.1.call-start = ((), (), s32[]{:S(2)}) async-start(), calls=%async_computation.33 | async-start | bytes 1310720 | tf_op jit(solution)/shard_map/reduce_scatter | solution.py:1096
  600.9 271.3 %reduce-scatter.35.cloned.1.call-start = ((), (), s32[]{:S(2)}) async-start(), calls=%async_computation.29 | async-start | bytes 2621440 | tf_op jit(solution)/shard_map/reduce_scatter | solution.py:1096
  601.5 334.8 %reduce-scatter.77.cloned.1.call-start = ((), (), s32[]{:S(2)}) async-start(), calls=%async_computation.50 | async-start | bytes 6488064
  609.9 439.4 %reduce-scatter.63.cloned.1.call-start = ((), (), s32[]{:S(2)}) async-start(), calls=%async_computation.43 | async-start | bytes 7864320 | tf_op jit(solution)/shard_map/reduce_scatter | solution.py:1096
  610.5 552.5 %reduce-scatter.67.cloned.1.call-start = ((), (), s32[]{:S(2)}) async-start(), calls=%async_computation.45 | async-start | bytes 7864320 | tf_op jit(solution)/shard_map/reduce_scatter | solution.py:1096
  611.3 571.8 %reduce-scatter.47.cloned.1.call-start = ((), (), s32[]{:S(2)}) async-start(), calls=%async_computation.35 | async-start | bytes 327680 | tf_op jit(solution)/shard_map/reduce_scatter | solution.py:898
  626.8 576.8 %reduce-scatter.61.cloned.1.call-start = ((), (), s32[]{:S(2)}) async-start(), calls=%async_computation.42 | async-start | bytes 327680 | tf_op jit(solution)/shard_map/reduce_scatter | solution.py:898
  671.6 577.3 %reduce-scatter.55.cloned.1.call-start = ((), (), s32[]{:S(2)}) async-start(), calls=%async_computation.39 | async-start | bytes 294912 | tf_op jit(solution)/shard_map/reduce_scatter | solution.py:1097
  697.1 581.1 %reduce-scatter.59.cloned.1.call-start = ((), (), s32[]{:S(2)}) async-start(), calls=%async_computation.41 | async-start | bytes 294912 | tf_op jit(solution)/shard_map/reduce_scatter | solution.py:1097
  725.2 590.4 %reduce-scatter.51.cloned.1.call-start = ((), (), s32[]{:S(2)}) async-start(), calls=%async_computation.37 | async-start | bytes 589824 | tf_op jit(solution)/shard_map/reduce_scatter | solution.py:1097
  769.8 591.7 %all-gather.13.cloned.1.call-start = ((), (), s32[]{:S(2)}) async-start(), calls=%async_computation.28 | async-start | bytes 2621440 | tf_op jit(solution)/shard_map/all_gather | solution.py:1060
  770.5 675.1 %all-gather.9.cloned.1.call-start = ((), (), s32[]{:S(2)}) async-start(), calls=%async_computation.24 | async-start | bytes 5570560 | tf_op jit(solution)/shard_map/all_gather | solution.py:1041
  771.1 712.4 %reduce-scatter.41.cloned.1.call-start = ((), (), s32[]{:S(2)}) async-start(), calls=%async_computation.32 | async-start | bytes 294912 | tf_op jit(solution)/shard_map/reduce_scatter | solution.py:1097
  798.9 721.5 %reduce-scatter.45.cloned.1.call-start = ((), (), s32[]{:S(2)}) async-start(), calls=%async_computation.34 | async-start | bytes 294912 | tf_op jit(solution)/shard_map/reduce_scatter | solution.py:1097
  827.0 730.7 %reduce-scatter.37.cloned.1.call-start = ((), (), s32[]{:S(2)}) async-start(), calls=%async_computation.30 | async-start | bytes 589824 | tf_op jit(solution)/shard_map/reduce_scatter | solution.py:1097
  872.2 709.0 %reduce-scatter.71.cloned.1.call-start = ((), (), s32[]{:S(2)}) async-start(), calls=%async_computation.47 | async-start | bytes 901120 | tf_op jit(solution)/shard_map/reduce_scatter | solution.py:898
  938.6 727.8 %all-gather.11.cloned.1.call-start = ((), (), s32[]{:S(2)}) async-start(), calls=%async_computation.26 | async-start | bytes 5570560 | tf_op jit(solution)/shard_map/all_gather | solution.py:1071
  939.4 770.2 %reduce-scatter.65.cloned.1.call-start = ((), (), s32[]{:S(2)}) async-start(), calls=%async_computation.44 | async-start | bytes 1769472 | tf_op jit(solution)/shard_map/reduce_scatter | solution.py:1097
  1049.4 702.1 %reduce-scatter.69.cloned.1.call-start = ((), (), s32[]{:S(2)}) async-start(), calls=%async_computation.46 | async-start | bytes 1769472 | tf_op jit(solution)/shard_map/reduce_scatter | solution.py:1097
  (25 other events, 1692.2 us)
Sparse Core Ops, SparseCore 0:
  549.3 29.3 reduce-scatter.30
  582.6 42.3 reduce-scatter.72
  628.5 41.2 reduce-scatter.74
  671.9 25.0 reduce-scatter.52
  699.3 25.8 reduce-scatter.56
  727.4 42.3 reduce-scatter.48
  772.2 26.6 reduce-scatter.38
  801.2 25.7 reduce-scatter.42
  829.8 42.3 reduce-scatter.34
  875.6 60.6 reduce-scatter.76
  938.6 110.7 reduce-scatter.62
  1051.7 111.2 reduce-scatter.66
  1206.8 34.7 reduce-scatter.54
  1244.5 33.6 reduce-scatter.58
  1281.4 34.0 reduce-scatter.50
  1317.1 44.3 all-gather.12
  1362.9 82.6 all-gather.8
  1448.6 34.8 reduce-scatter.40
  1486.8 33.5 reduce-scatter.44
  1523.5 34.1 reduce-scatter.36
  1560.5 20.6 reduce-scatter.70
  1582.8 83.4 all-gather.10
  1669.9 39.6 reduce-scatter.64
  1713.0 38.4 reduce-scatter.68
  (3 shorter events, 51.3 us)

commit v2 on v1

--- a/solution.py
+++ b/solution.py
@@ -39,6 +39,407 @@
     return (value + unit - 1) // unit * unit
 
 
+def chunked(total, size, run):
+    def once(n, carry):
+        run(pl.multiple_of(n * size, size))
+        return carry
+
+    lax.fori_loop(0, total // size, once, 0)
+
+
+MESH = pl.DeviceIdType.MESH
+
+
+class Place:
+    def __init__(self, mp):
+        self.mp = mp
+        self.i = lax.axis_index("dp")
+        self.z = lax.axis_index("mp")
+        core = lax.rem(self.i, 2)
+        across = lax.rem(lax.div(self.i, 2), 2)
+        up = lax.div(self.i, 4)
+        self.core, self.across, self.up = core, across, up
+        self.ic = self.i + 1 - 2 * core
+        self.ix = self.i + 2 - 4 * across
+        self.iy = self.i + 4 - 8 * up
+        self.ixy = self.ix + 4 - 8 * up
+
+
+def enter(place):
+    barrier = pltpu.get_barrier_semaphore()
+    z, mp = place.z, place.mp
+    for near in (place.ic, place.ix, place.iy):
+        pl.semaphore_signal(barrier, 1, device_id=(near, z), device_id_type=MESH)
+
+    @pl.when(z > 0)
+    def _():
+        pl.semaphore_signal(barrier, 1, device_id=(place.i, z - 1), device_id_type=MESH)
+
+    @pl.when(z < mp - 1)
+    def _():
+        pl.semaphore_signal(barrier, 1, device_id=(place.i, z + 1), device_id_type=MESH)
+
+    low = jnp.minimum(z, 1)
+    high = jnp.minimum(mp - 1 - z, 1)
+    pl.semaphore_wait(barrier, 3 + low + high)
+
+
+def all_slots(mp):
+    return [(0, 0)] + [(d, s) for d in range(1, mp) for s in (0, 1)]
+
+
+def for_slot(place, slot, run):
+    d, side = slot
+    if d == 0:
+        run(place.z)
+    elif side == 0:
+        pl.when(place.z >= d)(lambda: run(place.z - d))
+    else:
+        pl.when(place.z < place.mp - d)(lambda: run(place.z + d))
+
+
+def region(ref, i, z, shard):
+    if len(ref.shape) == 4:
+        return ref.at[z, i]
+    rows, cols = shard
+    return ref.at[pl.ds(pl.multiple_of(z * rows, rows), rows), pl.ds(pl.multiple_of(i * cols, cols), cols)]
+
+
+def gather_steps(place, shards, outs, send, recv, local):
+    mp, i, z = place.mp, place.i, place.z
+    units = range(len(shards))
+
+    def here(u, i2, z2):
+        return region(outs[u], i2, z2, shards[u].shape)
+
+    def copy(u, kind, i2, z2, to, src=None):
+        spot = here(u, i2, z2)
+        return pltpu.make_async_remote_copy(
+            src_ref=spot if src is None else src, dst_ref=spot, send_sem=send.at[u, kind, z2],
+            recv_sem=recv.at[u, kind, z2], device_id=to, device_id_type=MESH)
+
+    def route(u, z2):
+        odd = lax.rem(z2 + u, 2)
+        first = place.ix + odd * (place.iy - place.ix)
+        second = place.iy + odd * (place.ix - place.iy)
+        return odd, first, second
+
+    slots = all_slots(mp)
+
+    def stage1(slot):
+        d, s = slot
+
+        def run(z2):
+            for u in units:
+                src = shards[u] if d == 0 else None
+                if d > 0:
+                    kind = 0 if s == 0 else 1
+                    copy(u, kind, i, z2, (i, z)).wait_recv()
+                if d == 0 or s == 0:
+                    pl.when(z < mp - 1)(lambda u=u, src=src: copy(u, 0, i, z2, (i, z + 1), src).start())
+                if d == 0 or s == 1:
+                    pl.when(z > 0)(lambda u=u, src=src: copy(u, 1, i, z2, (i, z - 1), src).start())
+                copy(u, 2, i, z2, (place.ix, z), src).start()
+                copy(u, 3, i, z2, (place.iy, z), src).start()
+                copy(u, 5, i, z2, (place.ic, z), src).start()
+                if d == 0:
+                    pltpu.make_async_copy(shards[u], here(u, i, z), local.at[u]).start()
+
+        for_slot(place, slot, run)
+
+    def stage2(slot):
+        def run(z2):
+            for u in units:
+                odd, first, second = route(u, z2)
+                kind = 2 + odd
+                spot = here(u, first, z2)
+                pltpu.make_async_remote_copy(src_ref=spot, dst_ref=spot, send_sem=send.at[u, kind, z2],
+                    recv_sem=recv.at[u, kind, z2], device_id=(first, z), device_id_type=MESH).wait_recv()
+                copy(u, 4, first, z2, (second, z)).start()
+                copy(u, 6, first, z2, (place.ic, z)).start()
+
+        for_slot(place, slot, run)
+
+    def stage3(slot):
+        def run(z2):
+            for u in units:
+                odd, first, second = route(u, z2)
+                kind = 3 - odd
+                spot = here(u, second, z2)
+                pltpu.make_async_remote_copy(src_ref=spot, dst_ref=spot, send_sem=send.at[u, kind, z2],
+                    recv_sem=recv.at[u, kind, z2], device_id=(second, z), device_id_type=MESH).wait_recv()
+                copy(u, 7, second, z2, (place.ic, z)).start()
+                copy(u, 4, place.ixy, z2, (second, z)).wait_recv()
+                copy(u, 8, place.ixy, z2, (place.ic, z)).start()
+
+        for_slot(place, slot, run)
+
+    def other(i2):
+        return i2 + place.ic - i
+
+    def finish(slot):
+        d, s = slot
+
+        def run(z2):
+            for u in units:
+                odd, first, second = route(u, z2)
+                for kind, i2 in ((5, i), (6, first), (7, second), (8, place.ixy)):
+                    copy(u, kind, other(i2), z2, (place.ic, z)).wait_recv()
+                if d == 0 or s == 0:
+                    pl.when(z < mp - 1)(lambda u=u: copy(u, 0, i, z2, (i, z)).wait_send())
+                if d == 0 or s == 1:
+                    pl.when(z > 0)(lambda u=u: copy(u, 1, i, z2, (i, z)).wait_send())
+                for kind in range(2, 9):
+                    copy(u, kind, i, z2, (i, z)).wait_send()
+                if d == 0:
+                    pltpu.make_async_copy(shards[u], here(u, i, z), local.at[u]).wait()
+
+        for_slot(place, slot, run)
+
+    steps = []
+    n = len(slots)
+    for k in range(n + 2):
+        if k < n:
+            steps.append(functools.partial(stage1, slots[k]))
+        if 0 <= k - 1 < n:
+            steps.append(functools.partial(stage2, slots[k - 1]))
+        if 0 <= k - 2 < n:
+            steps.append(functools.partial(stage3, slots[k - 2]))
+    for slot in slots:
+        steps.append(functools.partial(finish, slot))
+    return steps
+
+
+def gather_shape(shard, kind, dp, mp):
+    rows, cols = shard.shape
+    if kind == "by_dp":
+        return jax.ShapeDtypeStruct((mp, dp, rows, cols), shard.dtype)
+    return jax.ShapeDtypeStruct((mp * rows, dp * cols), shard.dtype)
+
+
+def add_into(target, *others):
+    rows = target.shape[0]
+    size = 64 if rows % 64 == 0 else rows
+
+    def some(at):
+        part = pl.ds(at, size)
+        total = target[part, :].astype(F32)
+        for other in others:
+            total = total + other[part, :].astype(F32)
+        target[part, :] = total.astype(target.dtype)
+
+    chunked(rows, size, some)
+
+
+def scatter_scratch(shards, mp):
+    scratch = []
+    for dims, dtype in shards:
+        scratch += [
+            pltpu.VMEM((mp, 4) + dims, dtype),
+            pltpu.VMEM((mp, 4) + dims, dtype),
+            pltpu.VMEM((mp, 3) + dims, dtype),
+            pltpu.VMEM((mp, 2) + dims, dtype),
+        ]
+    sems = pltpu.SemaphoreType.DMA((len(shards), 9, mp))
+    return scratch + [sems, sems, pltpu.SemaphoreType.DMA((len(shards), 4, mp))]
+
+
+def scatter_steps(place, grads, outs, scratch):
+    mp, i, z = place.mp, place.i, place.z
+    units = range(len(grads))
+    send, recv, local = scratch[-3:]
+    own = [scratch[4 * u] for u in units]
+    sibling = [scratch[4 * u + 1] for u in units]
+    plane = [scratch[4 * u + 2] for u in units]
+    line = [scratch[4 * u + 3] for u in units]
+    chips = (place.i, place.ix, place.iy, place.ixy)
+    slots = all_slots(mp)[::-1]
+
+    def piece(u, i2, z2):
+        return region(grads[u], i2, z2, own[u].shape[2:])
+
+    def copy(u, kind, z2, src, dst, to):
+        return pltpu.make_async_remote_copy(
+            src_ref=src, dst_ref=dst, send_sem=send.at[u, kind, z2], recv_sem=recv.at[u, kind, z2],
+            device_id=to, device_id_type=MESH)
+
+    def load(u, k, z2):
+        return pltpu.make_async_copy(piece(u, chips[k], z2), own[u].at[z2, k], local.at[u, k, z2])
+
+    def across(u, k, z2):
+        other = chips[k] + place.ic - i
+        return copy(u, k, z2, piece(u, other, z2), sibling[u].at[z2, k], (place.ic, z))
+
+    def route(u, z2):
+        odd = lax.rem(z2 + u, 2)
+        first = place.ix + odd * (place.iy - place.ix)
+        second = place.iy + odd * (place.ix - place.iy)
+        return 1 + odd, 2 - odd, first, second
+
+    def to_second(u, z2, far):
+        _, ks, _, second = route(u, z2)
+        src = own[u].at[z2, 3] if far else own[u].at[z2, ks]
+        return copy(u, 4 if far else 5, z2, src, plane[u].at[z2, 0 if far else 1], (second, z))
+
+    def to_first(u, z2):
+        kf, _, first, _ = route(u, z2)
+        return copy(u, 6, z2, own[u].at[z2, kf], plane[u].at[z2, 2], (first, z))
+
+    def along(u, z2, up):
+        to = (i, z + 1) if up else (i, z - 1)
+        return copy(u, 7 if up else 8, z2, own[u].at[z2, 0], line[u].at[z2, 0 if up else 1], to)
+
+    def begin(slot):
+        def run(z2):
+            for u in units:
+                for k in (3, 2, 1, 0):
+                    load(u, k, z2).start()
+                    across(u, k, z2).start()
+
+        for_slot(place, slot, run)
+
+    def stage1(slot):
+        def run(z2):
+            for u in units:
+                for k in (3, 2, 1, 0):
+                    load(u, k, z2).wait()
+                    across(u, k, z2).wait_recv()
+                for k in range(4):
+                    add_into(own[u].at[z2, k], sibling[u].at[z2, k])
+                to_second(u, z2, True).start()
+                to_second(u, z2, False).start()
+
+        for_slot(place, slot, run)
+
+    def stage2(slot):
+        def run(z2):
+            for u in units:
+                kf = route(u, z2)[0]
+                to_second(u, z2, True).wait_recv()
+                add_into(own[u].at[z2, kf], plane[u].at[z2, 0])
+                to_first(u, z2).start()
+
+        for_slot(place, slot, run)
+
+    def stage3(slot):
+        d, side = slot
+
+        def run(z2):
+            for u in units:
+                mine = own[u].at[z2, 0]
+                to_second(u, z2, False).wait_recv()
+                to_first(u, z2).wait_recv()
+                add_into(mine, plane[u].at[z2, 1], plane[u].at[z2, 2])
+                if d == 0 or side == 1:
+
+                    @pl.when(z > 0)
+                    def _(u=u, mine=mine):
+                        along(u, z2, True).wait_recv()
+                        add_into(mine, line[u].at[z2, 0])
+
+                if d == 0 or side == 0:
+
+                    @pl.when(z < mp - 1)
+                    def _(u=u, mine=mine):
+                        along(u, z2, False).wait_recv()
+                        add_into(mine, line[u].at[z2, 1])
+
+                if d == 0:
+                    outs[u][...] = mine[...].astype(F32)
+                else:
+                    along(u, z2, side == 1).start()
+
+        for_slot(place, slot, run)
+
+    def finish(slot):
+        d, side = slot
+
+        def run(z2):
+            for u in units:
+                for k in range(4):
+                    across(u, k, z2).wait_send()
+                to_second(u, z2, True).wait_send()
+                to_second(u, z2, False).wait_send()
+                to_first(u, z2).wait_send()
+                if d > 0:
+                    along(u, z2, side == 1).wait_send()
+
+        for_slot(place, slot, run)
+
+    steps = [functools.partial(begin, slot) for slot in slots]
+    n = len(slots)
+    for k in range(n + 2):
+        if k < n:
+            steps.append(functools.partial(stage1, slots[k]))
+        if 0 <= k - 1 < n:
+            steps.append(functools.partial(stage2, slots[k - 1]))
+        if 0 <= k - 2 < n:
+            steps.append(functools.partial(stage3, slots[k - 2]))
+    for slot in slots:
+        steps.append(functools.partial(finish, slot))
+    return steps
+
+
+def shard_of(grad, dp, mp):
+    if len(grad.shape) == 4:
+        return grad.shape[2:]
+    return (grad.shape[0] // mp, grad.shape[1] // dp)
+
+
+class Transfers:
+    def __init__(self, dp, mp, cid, shards=(), kinds=(), grads=()):
+        self.dp, self.mp, self.cid = dp, mp, cid
+        self.shards, self.kinds, self.grads = list(shards), list(kinds), list(grads)
+        self.args = self.shards + self.grads
+        spots = [(shard_of(g, dp, mp), g.dtype) for g in self.grads]
+        self.outs = [gather_shape(s, k, dp, mp) for s, k in zip(shards, kinds)]
+        self.outs += [jax.ShapeDtypeStruct(s, F32) for s, _ in spots]
+        any_space = pl.BlockSpec(memory_space=pl.ANY)
+        self.in_specs = [any_space] * len(self.args)
+        self.out_specs = [any_space] * len(self.shards)
+        self.out_specs += [pl.BlockSpec(s, lambda *_: (0, 0)) for s, _ in spots]
+        self.scratch = []
+        if self.shards:
+            sems = pltpu.SemaphoreType.DMA((len(self.shards), 9, mp))
+            self.scratch += [sems, sems, pltpu.SemaphoreType.DMA((len(self.shards),))]
+        if self.grads:
+            self.scratch += scatter_scratch(spots, mp)
+
+    def steps(self, ins, outs, scratch):
+        place = Place(self.mp)
+        count = len(self.shards)
+        found = [functools.partial(enter, place)]
+        if count:
+            found += gather_steps(place, ins[:count], outs[:count], *scratch[:3])
+            scratch = scratch[3:]
+        if self.grads:
+            found += scatter_steps(place, ins[count:], outs[count:], scratch)
+        return found
+
+    def params(self, limit):
+        return pltpu.CompilerParams(
+            collective_id=self.cid, has_side_effects=True, vmem_limit_bytes=limit
+        )
+
+    def run(self, name):
+        count = len(self.args)
+
+        def kernel(*refs):
+            outs = refs[count : count + len(self.outs)]
+            for step in self.steps(refs[:count], outs, refs[count + len(self.outs) :]):
+                step()
+
+        return pl.pallas_call(
+            kernel, grid=(1,), out_shape=self.outs, in_specs=self.in_specs, out_specs=self.out_specs,
+            scratch_shapes=self.scratch, compiler_params=self.params(60 << 20), name=name,
+        )(*self.args)
+
+
+def spread_steps(steps, at, total):
+    for n, step in enumerate(steps):
+        pl.when(at == n * total // len(steps))(step)
+
+
 def skew(row, height):
     wide = jnp.broadcast_to(row, (height, row.shape[1]))
     return pltpu.roll(wide, 0, axis=1, stride=1, stride_axis=0)
@@ -74,7 +475,17 @@
     return jnp.concatenate([strip_ref[2 * g, :, lanes], strip_ref[2 * g + 1, :, lanes]], axis=1)
 
 
-def forward_kernel(biased, front, lead, lo_ref, hi_ref, *refs):
+def split_refs(refs, host, ins, outs):
+    if host is None:
+        return refs[2:], [], lambda a: (refs[0][a], refs[1][a])
+    a, b = len(host.args), len(host.outs)
+    cut = [0, ins, ins + a, ins + a + outs, ins + a + outs + b, len(refs) - len(host.scratch), len(refs)]
+    part = [refs[i:j] for i, j in zip(cut, cut[1:])]
+    return part[0] + part[2] + part[4], host.steps(part[1], part[3], part[5]), host.bounds
+
+
+def forward_kernel(biased, front, lead, host, *refs):
+    refs, steps, bounds = split_refs(refs, host, 5, 2)
     if biased:
         q_ref, k_ref, v_ref, mask_ref, vec_ref, o_ref, lse_ref, strip, m_s, l_s, acc_s = refs
         keys_ref = None
@@ -83,8 +494,11 @@
     else:
         q_ref, k_ref, v_ref, mask_ref, keys_ref, o_ref, lse_ref, m_s, l_s, acc_s = refs
     tiles = q_ref.shape[0] // TILE_Q
+    group = pl.program_id(0)
+    places = pl.num_programs(0) * tiles
 
     def q_tile(a, carry):
+        spread_steps(steps, group * tiles + a, places)
         rows = pl.ds(pl.multiple_of(a * TILE_Q, TILE_Q), TILE_Q)
         qt = q_ref[rows, :]
         q2 = [stacked(qt, g) for g in range(2)]
@@ -113,7 +527,7 @@
                 acc_s[g] = acc_s[g] * alpha + mm_tn(vt[:, head], p.astype(BF16))
             return carry
 
-        lax.fori_loop(lo_ref[a], hi_ref[a], k_tile, 0)
+        lax.fori_loop(*bounds(a), k_tile, 0)
         for g in range(2):
             total = l_s[g : g + 1, :]
             mixed = (acc_s[g] / total).T
@@ -126,7 +540,8 @@
     lax.fori_loop(0, tiles, q_tile, 0)
 
 
-def backward_kernel(biased, front, lead, lo_ref, hi_ref, *refs):
+def backward_kernel(biased, front, lead, host, *refs):
+    refs, steps, bounds = split_refs(refs, host, 8, 4 if biased else 3)
     if biased:
         (
             q_ref, k_ref, v_ref, o_ref, do_ref, lse_ref, mask_ref, vec_ref,
@@ -142,10 +557,13 @@
             dq_ref, dk_ref, dv_ref, dk_s, dv_s, dq_s,
         ) = refs
     tiles = q_ref.shape[0] // TILE_Q
+    group = pl.program_id(0)
+    places = pl.num_programs(0) * tiles
     dk_s[...] = jnp.zeros_like(dk_s)
     dv_s[...] = jnp.zeros_like(dv_s)
 
     def q_tile(a, carry):
+        spread_steps(steps, group * tiles + a, places)
         rows = pl.ds(pl.multiple_of(a * TILE_Q, TILE_Q), TILE_Q)
         qt = q_ref[rows, :]
         ot = o_ref[rows, :]
@@ -194,7 +612,7 @@
             dv_s[keys, :] += jnp.concatenate(grad_v, axis=1)
             return carry
 
-        lax.fori_loop(lo_ref[a], hi_ref[a], k_tile, 0)
+        lax.fori_loop(*bounds(a), k_tile, 0)
         for g in range(2):
             dq_ref[rows, 2 * HEAD_DIM * g : 2 * HEAD_DIM * (g + 1)] = unstacked(dq_s[g].T).astype(
                 BF16
@@ -222,8 +640,7 @@
     return pl.BlockSpec(shape, index)
 
 
-def attention_call(kernel, biased, outs, scratch, args, bounds, front, lead, name, flops):
-    rows = args[0].shape[0]
+def attention_call(kernel, biased, outs, scratch, args, bounds, front, lead, name, flops, host):
     steps = args[1].shape[1] // (2 * HEAD_DIM)
 
     def column(array, lanes):
@@ -247,20 +664,34 @@
             out_specs.append(column(item, 2 * HEAD_DIM))
         else:
             out_specs.append(spec((1,) + item.shape[1:], lambda i, *_: (i, 0, 0)))
-    return pl.pallas_call(
-        functools.partial(kernel, biased, front, lead),
-        out_shape=[item for item, _ in outs],
+    shapes = [item for item, _ in outs]
+    own = len(shapes)
+    scalars = list(bounds)
+    params = pltpu.CompilerParams(vmem_limit_bytes=56 << 20)
+    args = list(args)
+    if host is not None:
+        scalars = []
+        args += host.args
+        specs += host.in_specs
+        shapes += host.outs
+        out_specs += host.out_specs
+        scratch = scratch + host.scratch
+        params = host.params(60 << 20)
+    found = pl.pallas_call(
+        functools.partial(kernel, biased, front, lead, host),
+        out_shape=shapes,
         grid_spec=pltpu.PrefetchScalarGridSpec(
-            num_scalar_prefetch=2,
+            num_scalar_prefetch=len(scalars),
             grid=(steps,),
             in_specs=specs,
             out_specs=out_specs,
             scratch_shapes=scratch,
         ),
-        compiler_params=pltpu.CompilerParams(vmem_limit_bytes=56 << 20),
+        compiler_params=params,
         cost_estimate=pl.CostEstimate(flops=flops, bytes_accessed=16 << 20, transcendentals=0),
         name=name,
-    )(*bounds, *args)
+    )(*scalars, *args)
+    return found[:own], found[own:]
 
 
 def args_kinds(args, biased, kernel):
@@ -272,7 +703,7 @@
     return list(zip(args, kinds))
 
 
-def attend_forward(q, k, v, mask, extra, bounds, front, lead, biased, name):
+def attend_forward(q, k, v, mask, extra, bounds, front, lead, biased, name, host=None):
     rows = q.shape[0]
     steps = k.shape[1] // (2 * HEAD_DIM)
     outs = [
@@ -289,11 +720,14 @@
     ]
     flops = 4 * rows * k.shape[0] * q.shape[1]
     return attention_call(
-        forward_kernel, biased, outs, scratch, (q, k, v, mask, extra), bounds, front, lead, name, flops
-    )
-
-
-def attend_backward(q, k, v, o, do, lse, mask, extra, bounds, front, lead, biased, name):
+        forward_kernel, biased, outs, scratch, (q, k, v, mask, extra), bounds, front, lead, name,
+        flops, host,
+    )
+
+
+def attend_backward(
+    q, k, v, o, do, lse, mask, extra, bounds, front, lead, biased, name, host=None
+):
     rows = q.shape[0]
     keys = k.shape[0]
     outs = [
@@ -313,196 +747,8 @@
     flops = 10 * rows * keys * q.shape[1]
     return attention_call(
         backward_kernel, biased, outs, scratch, (q, k, v, o, do, lse, mask, extra), bounds, front,
-        lead, name, flops,
-    )
-
-
-MESH = pl.DeviceIdType.MESH
-
-
-class Place:
-    def __init__(self, mp):
-        self.mp = mp
-        self.i = lax.axis_index("dp")
-        self.z = lax.axis_index("mp")
-        core = lax.rem(self.i, 2)
-        across = lax.rem(lax.div(self.i, 2), 2)
-        up = lax.div(self.i, 4)
-        self.core, self.across, self.up = core, across, up
-        self.ic = self.i + 1 - 2 * core
-        self.ix = self.i + 2 - 4 * across
-        self.iy = self.i + 4 - 8 * up
-        self.ixy = self.ix + 4 - 8 * up
-
-
-def enter(place):
-    barrier = pltpu.get_barrier_semaphore()
-    z, mp = place.z, place.mp
-    for near in (place.ic, place.ix, place.iy):
-        pl.semaphore_signal(barrier, 1, device_id=(near, z), device_id_type=MESH)
-
-    @pl.when(z > 0)
-    def _():
-        pl.semaphore_signal(barrier, 1, device_id=(place.i, z - 1), device_id_type=MESH)
-
-    @pl.when(z < mp - 1)
-    def _():
-        pl.semaphore_signal(barrier, 1, device_id=(place.i, z + 1), device_id_type=MESH)
-
-    low = jnp.minimum(z, 1)
-    high = jnp.minimum(mp - 1 - z, 1)
-    pl.semaphore_wait(barrier, 3 + low + high)
-
-
-def region(ref, i, z, shard):
-    if len(ref.shape) == 4:
-        return ref.at[z, i]
-    rows, cols = shard
-    return ref.at[pl.ds(pl.multiple_of(z * rows, rows), rows), pl.ds(pl.multiple_of(i * cols, cols), cols)]
-
-
-def gather_steps(place, shards, outs, send, recv, local):
-    mp, i, z = place.mp, place.i, place.z
-    units = range(len(shards))
-
-    def here(u, i2, z2):
-        return region(outs[u], i2, z2, shards[u].shape)
-
-    def copy(u, kind, i2, z2, to, src=None):
-        spot = here(u, i2, z2)
-        return pltpu.make_async_remote_copy(
-            src_ref=spot if src is None else src, dst_ref=spot, send_sem=send.at[u, kind, z2],
-            recv_sem=recv.at[u, kind, z2], device_id=to, device_id_type=MESH)
-
-    def route(u, z2):
-        odd = lax.rem(z2 + u, 2)
-        first = place.ix + odd * (place.iy - place.ix)
-        second = place.iy + odd * (place.ix - place.iy)
-        return odd, first, second
-
-    slots = [(0, 0)] + [(d, s) for d in range(1, mp) for s in (0, 1)]
-
-    def when(slot, f):
-        d, s = slot
-        z2 = z if d == 0 else (z - d if s == 0 else z + d)
-        if d == 0:
-            f(z2)
-        elif s == 0:
-            pl.when(z >= d)(lambda: f(z2))
-        else:
-            pl.when(z < mp - d)(lambda: f(z2))
-
-    def stage1(slot):
-        d, s = slot
-
-        def run(z2):
-            for u in units:
-                src = shards[u] if d == 0 else None
-                if d > 0:
-                    kind = 0 if s == 0 else 1
-                    copy(u, kind, i, z2, (i, z)).wait_recv()
-                if d == 0 or s == 0:
-                    pl.when(z < mp - 1)(lambda u=u, src=src: copy(u, 0, i, z2, (i, z + 1), src).start())
-                if d == 0 or s == 1:
-                    pl.when(z > 0)(lambda u=u, src=src: copy(u, 1, i, z2, (i, z - 1), src).start())
-                copy(u, 2, i, z2, (place.ix, z), src).start()
-                copy(u, 3, i, z2, (place.iy, z), src).start()
-                copy(u, 5, i, z2, (place.ic, z), src).start()
-                if d == 0:
-                    pltpu.make_async_copy(shards[u], here(u, i, z), local.at[u]).start()
-
-        when(slot, run)
-
-    def stage2(slot):
-        def run(z2):
-            for u in units:
-                odd, first, second = route(u, z2)
-                kind = 2 + odd
-                spot = here(u, first, z2)
-                pltpu.make_async_remote_copy(src_ref=spot, dst_ref=spot, send_sem=send.at[u, kind, z2],
-                    recv_sem=recv.at[u, kind, z2], device_id=(first, z), device_id_type=MESH).wait_recv()
-                copy(u, 4, first, z2, (second, z)).start()
-                copy(u, 6, first, z2, (place.ic, z)).start()
-
-        when(slot, run)
-
-    def stage3(slot):
-        def run(z2):
-            for u in units:
-                odd, first, second = route(u, z2)
-                kind = 3 - odd
-                spot = here(u, second, z2)
-                pltpu.make_async_remote_copy(src_ref=spot, dst_ref=spot, send_sem=send.at[u, kind, z2],
-                    recv_sem=recv.at[u, kind, z2], device_id=(second, z), device_id_type=MESH).wait_recv()
-                copy(u, 7, second, z2, (place.ic, z)).start()
-                copy(u, 4, place.ixy, z2, (second, z)).wait_recv()
-                copy(u, 8, place.ixy, z2, (place.ic, z)).start()
-
-        when(slot, run)
-
-    def other(i2):
-        return i2 + place.ic - i
-
-    def finish(slot):
-        d, s = slot
-
-        def run(z2):
-            for u in units:
-                odd, first, second = route(u, z2)
-                for kind, i2 in ((5, i), (6, first), (7, second), (8, place.ixy)):
-                    copy(u, kind, other(i2), z2, (place.ic, z)).wait_recv()
-                if d == 0 or s == 0:
-                    pl.when(z < mp - 1)(lambda u=u: copy(u, 0, i, z2, (i, z)).wait_send())
-                if d == 0 or s == 1:
-                    pl.when(z > 0)(lambda u=u: copy(u, 1, i, z2, (i, z)).wait_send())
-                for kind in range(2, 9):
-                    copy(u, kind, i, z2, (i, z)).wait_send()
-                if d == 0:
-                    pltpu.make_async_copy(shards[u], here(u, i, z), local.at[u]).wait()
-
-        when(slot, run)
-
-    steps = []
-    n = len(slots)
-    for k in range(n + 2):
-        if k < n:
-            steps.append(functools.partial(stage1, slots[k]))
-        if 0 <= k - 1 < n:
-            steps.append(functools.partial(stage2, slots[k - 1]))
-        if 0 <= k - 2 < n:
-            steps.append(functools.partial(stage3, slots[k - 2]))
-    for slot in slots:
-        steps.append(functools.partial(finish, slot))
-    return steps
-
-
-def gather_shape(shard, kind, dp, mp):
-    rows, cols = shard.shape
-    if kind == "by_dp":
-        return jax.ShapeDtypeStruct((mp, dp, rows, cols), shard.dtype)
-    return jax.ShapeDtypeStruct((mp * rows, dp * cols), shard.dtype)
-
-
-def gather_kernel(count, mp, *refs):
-    shards, outs, (send, recv, local) = refs[:count], refs[count:2 * count], refs[2 * count:]
-    place = Place(mp)
-    enter(place)
-    for step in gather_steps(place, shards, outs, send, recv, local):
-        step()
-
-
-def gather_weights(shards, kinds, dp, mp, cid, name):
-    count = len(shards)
-    any_space = pl.BlockSpec(memory_space=pl.ANY)
-    sems = pltpu.SemaphoreType.DMA((count, 9, mp))
-    return pl.pallas_call(
-        functools.partial(gather_kernel, count, mp),
-        out_shape=[gather_shape(s, k, dp, mp) for s, k in zip(shards, kinds)],
-        in_specs=[any_space] * count, out_specs=[any_space] * count,
-        scratch_shapes=[sems, sems, pltpu.SemaphoreType.DMA((count,))],
-        compiler_params=pltpu.CompilerParams(collective_id=cid, has_side_effects=True),
-        name=name,
-    )(*shards)
+        lead, name, flops, host,
+    )
 
 
 def inverse_rms(state):
@@ -515,14 +761,6 @@
     grad_gain = jnp.sum(grad_normed * state * scale, axis=0, keepdims=True)
     inner = jnp.mean(weighted * state, axis=-1, keepdims=True)
     return scale * weighted - state * (scale * scale * scale) * inner, grad_gain
-
-
-def chunked(total, size, run):
-    def once(n, carry):
-        run(pl.multiple_of(n * size, size))
-        return carry
-
-    lax.fori_loop(0, total // size, once, 0)
 
 
 def row_chunk(rows):
@@ -949,20 +1187,24 @@
     groups = self_key.shape[1] * mp // (2 * HEAD_DIM)
     native = mp == groups and dp == 8 and rows % 16 == 0
 
-    gains = [gather(g, ((0, "dp"),)).astype(F32)[None] for g in (self_gain, cross_gain, feed_gain)]
-    gain_one, gain_two, gain_three = gains
-    table = gather(position_bias, ROWS_BY_DP).astype(F32)
     if native:
         order = ["by_dp", "by_mp"]
+        size = width // dp
+        gains = jnp.stack([self_gain, cross_gain, feed_gain])
+        little = jnp.pad(position_bias.reshape(1, -1), ((0, 0), (0, size - position_bias.size)))
+        little = jnp.pad(jnp.concatenate([gains, little]), ((0, 12), (0, 0)))
         w1 = jnp.concatenate([self_query, self_key, self_value], axis=1)
         w2 = jnp.concatenate([cross_query, cross_key, cross_value], axis=1)
-        w1, wo1 = gather_weights([w1, self_out], order, dp, mp, 1, "gather_self")
-        w2, wo2 = gather_weights([w2, cross_out], order, dp, mp, 2, "gather_cross")
-        wg, wu, wd = gather_weights(
-            [feed_gate, feed_up, feed_down], ["by_dp"] + order, dp, mp, 3, "gather_feed"
-        )
-        w1, w2, wg, wu = (w.reshape(mp, width, w.shape[3]) for w in (w1, w2, wg, wu))
+        w1, little, wo1 = Transfers(
+            dp, mp, 1, [w1, little, self_out], ["by_dp"] + order
+        ).run("gather_self")
+        gains = little[0, :, :3].transpose(1, 0, 2).reshape(3, 1, width).astype(F32)
+        table = little[:, :, 3, : position_bias.size].reshape((mp, dp) + position_bias.shape)
+        table = table.transpose(1, 2, 0, 3).reshape(dp * position_bias.shape[0], -1).astype(F32)
+        w1 = w1.reshape(mp, width, w1.shape[3])
     else:
+        gains = [gather(g, ((0, "dp"),)).astype(F32)[None] for g in (self_gain, cross_gain, feed_gain)]
+        table = gather(position_bias, ROWS_BY_DP).astype(F32)
 
         def blocks(*shards):
             return jnp.concatenate([grouped(gather(s, ROWS_BY_DP), groups) for s in shards], axis=2)
@@ -971,6 +1213,7 @@
         w2 = blocks(cross_query, cross_key, cross_value)
         wg, wu = blocks(feed_gate), blocks(feed_up)
         wo1, wo2, wd = (gather(s, ROWS_BY_MP) for s in (self_out, cross_out, feed_down))
+    gain_one, gain_two, gain_three = gains
 
     whole = lax.dynamic_index_in_dim(inputs, sequence, keepdims=False)
     memory = lax.dynamic_index_in_dim(encoded, sequence, keepdims=False)
@@ -1027,21 +1270,52 @@
     window = lax.dynamic_slice_in_dim(window, first, reach, axis=0)
     x = own(whole)
     q1, k1, v1, n1 = self_project(window, gain_one, w1, front, padded, rows)
-    o1, lse_one = attend_forward(
-        q1, k1, v1, mask_one, vec, bounds_one, front, lead, True, "self_forward"
-    )
+
+    def self_bounds(a):
+        here = lax.rem(lax.axis_index("mp"), parts)
+        last = jnp.minimum(a * TILE_Q + TILE_Q - 1, rows - 1)
+        return lax.div(front - here * rows, TILE_K), lax.div(last + front, TILE_K) + 1
+
+    def cross_bounds(a):
+        return 0, enc_length // TILE_K
+
+    def carried(bounds, *args, **more):
+        host = Transfers(dp, mp, *args, **more)
+        host.bounds = bounds
+        return host
+
+    hosts = [None] * 4
+    if native:
+        hosts[0] = carried(self_bounds, 2, [w2, cross_out, feed_gate], order + ["by_dp"])
+        hosts[1] = carried(cross_bounds, 3, [feed_up, feed_down], order)
+    (o1, lse_one), found = attend_forward(
+        q1, k1, v1, mask_one, vec, bounds_one, front, lead, True, "self_forward", hosts[0]
+    )
+    if native:
+        w2, wo2, wg = found
+        w2, wg = (w.reshape(mp, width, w.shape[3]) for w in (w2, wg))
     h1, n2, q2, k2, v2 = cross_project(o1, wo1, x, gain_two, memory, w2)
-    o2, lse_two = attend_forward(
-        q2, k2, v2, mask_two, keys_two, bounds_two, 0, 0, False, "cross_forward"
-    )
+    (o2, lse_two), found = attend_forward(
+        q2, k2, v2, mask_two, keys_two, bounds_two, 0, 0, False, "cross_forward", hosts[1]
+    )
+    if native:
+        wu, wd = found
+        wu = wu.reshape(mp, width, wu.shape[3])
 
     result, grad_two, grad_gain_three, gwg, gwu, gwd, do2, gwo2 = feed(
         o2, wo2, h1, gain_three, upstream, wg, wu, wd
     )
     outputs = lax.all_gather(result, "mp", axis=0, tiled=True).reshape(inputs.shape)
 
-    dq2, dk2, dv2 = attend_backward(
-        q2, k2, v2, o2, do2, lse_two, mask_two, keys_two, bounds_two, 0, 0, False, "cross_backward"
+    def pieces(grad):
+        return grad.reshape(grad.shape[0], dp, grad.shape[1] // dp, grad.shape[2])
+
+    if native:
+        hosts[2] = carried(cross_bounds, 4, grads=[gwd])
+        hosts[3] = carried(self_bounds, 5, grads=[pieces(gwg), pieces(gwu)])
+    (dq2, dk2, dv2), sums_down = attend_backward(
+        q2, k2, v2, o2, do2, lse_two, mask_two, keys_two, bounds_two, 0, 0, False,
+        "cross_backward", hosts[2],
     )
     sharing = [[s * parts + p for p in range(parts)] for s in range(batches)]
 
@@ -1059,8 +1333,9 @@
     gwkv2, grad_memory = memory_back(dkv2[:, :half], dkv2[:, half:], w2, own_memory)
     grad_encoded = lax.all_gather(grad_memory, "mp", axis=0, tiled=True).reshape(encoded.shape)
 
-    dq1, dk1, dv1, slopes = attend_backward(
-        q1, k1, v1, o1, do1, lse_one, mask_one, vec, bounds_one, front, lead, True, "self_backward"
+    (dq1, dk1, dv1, slopes), sums_feed = attend_backward(
+        q1, k1, v1, o1, do1, lse_one, mask_one, vec, bounds_one, front, lead, True,
+        "self_backward", hosts[3],
     )
     dkv1 = jnp.concatenate([dk1, dv1], axis=1)
     dkv1 = jnp.pad(dkv1, ((0, max(0, front + length - reach)), (0, 0)))
@@ -1072,50 +1347,51 @@
     slopes = slopes.reshape(heads, spread)[:, lead : lead + length]
     slopes = jnp.pad(slopes, ((0, 0), (0, length - slopes.shape[1])))
     grad_table = dot(onehot, slopes, ((0,), (1,)), HIGHEST)
-
-    small = jnp.concatenate(
-        [grad_gain_one[0], grad_gain_two[0], grad_gain_three[0], grad_table.reshape(-1)]
-    )
-    small = lax.psum(small, ("dp", "mp"))
-    data = lax.axis_index("dp")
-
-    def gain_block(index):
-        size = width // dp
-        return lax.dynamic_slice_in_dim(small, index * width + data * size, size, axis=0)
-
-    grad_table = small[3 * width :].reshape(table.shape)
-    grad_table = lax.dynamic_slice(
-        grad_table,
-        (data * position_bias.shape[0], place * position_bias.shape[1]),
-        position_bias.shape,
-    )
+    grad_gains = jnp.concatenate([grad_gain_one, grad_gain_two, grad_gain_three])
+
     kcols = gwkv1.shape[2] // 2
-
-    def summed(grad):
-        if native:
-            grad = lax.psum_scatter(grad, "mp", scatter_dimension=0, tiled=True)
-            return lax.psum_scatter(grad[0], "dp", scatter_dimension=0, tiled=True).astype(F32)
-        return scatter(ungrouped(grad), ROWS_BY_DP)
+    if native:
+        little = grad_gains.reshape(3, dp, size).transpose(1, 0, 2)
+        little = jnp.broadcast_to(little[None], (mp, dp, 3, size))
+        spots = grad_table.reshape(dp, position_bias.shape[0], mp, position_bias.shape[1])
+        spots = spots.transpose(2, 0, 1, 3).reshape(mp, dp, 1, position_bias.size)
+        spots = jnp.pad(spots, ((0, 0), (0, 0), (0, 4), (0, size - position_bias.size)))
+        little = jnp.concatenate([little, spots], axis=2)
+        grads = [pieces(g) for g in (gwq2, gwkv2, gwq1, gwkv1)] + [gwo2, gwo1, little]
+        *sums, little = Transfers(dp, mp, 6, grads=grads).run("scatter_rest")
+        sums = sums + list(sums_feed) + list(sums_down)
+        sums[1:2] = sums[1][:, :kcols], sums[1][:, kcols:]
+        sums[4:5] = sums[4][:, :kcols], sums[4][:, kcols:]
+        gwq2, gwk2, gwv2, gwq1, gwk1, gwv1, gwo2, gwo1, gwg, gwu, gwd = sums
+        grad_gains = [little[n] for n in range(3)]
+        grad_table = little[3, : position_bias.size].reshape(position_bias.shape)
+    else:
+
+        def summed(grad):
+            return scatter(ungrouped(grad), ROWS_BY_DP)
+
+        gwk1, gwv1 = summed(gwkv1[:, :, :kcols]), summed(gwkv1[:, :, kcols:])
+        gwk2, gwv2 = summed(gwkv2[:, :, :kcols]), summed(gwkv2[:, :, kcols:])
+        gwq1, gwq2, gwg, gwu = (summed(g) for g in (gwq1, gwq2, gwg, gwu))
+        gwo1, gwo2, gwd = (scatter(g, ROWS_BY_MP) for g in (gwo1, gwo2, gwd))
+        small = jnp.concatenate([grad_gains.reshape(-1), grad_table.reshape(-1)])
+        small = lax.psum(small, ("dp", "mp"))
+        data = lax.axis_index("dp")
+        grad_gains = lax.dynamic_slice_in_dim(
+            small[: 3 * width].reshape(3, dp, width // dp), data, 1, axis=1
+        )
+        grad_gains = [grad_gains[n, 0] for n in range(3)]
+        grad_table = lax.dynamic_slice(
+            small[3 * width :].reshape(table.shape),
+            (data * position_bias.shape[0], place * position_bias.shape[1]),
+            position_bias.shape,
+        )
 
     return (
-        outputs,
-        grad_inputs,
-        grad_encoded,
-        gain_block(0),
-        summed(gwq1),
-        summed(gwkv1[:, :, :kcols]),
-        summed(gwkv1[:, :, kcols:]),
-        scatter(gwo1, ROWS_BY_MP),
-        grad_table,
-        gain_block(1),
-        summed(gwq2),
-        summed(gwkv2[:, :, :kcols]),
-        summed(gwkv2[:, :, kcols:]),
-        scatter(gwo2, ROWS_BY_MP),
-        gain_block(2),
-        summed(gwg),
-        summed(gwu),
-        scatter(gwd, ROWS_BY_MP),
+        outputs, grad_inputs, grad_encoded,
+        grad_gains[0], gwq1, gwk1, gwv1, gwo1, grad_table,
+        grad_gains[1], gwq2, gwk2, gwv2, gwo2,
+        grad_gains[2], gwg, gwu, gwd,
     )
 
 

time: 1780 us -> 835 us (0.47)
  waiting for transfers between devices: 1090 us -> 135 us
  Pallas kernels: 487 us -> 618 us
  blocking collectives: 84.7 us -> 0 us
  local copies, waits for them, and re-layouts: 69.3 us -> 44.9 us
    reduce_scatter x19 -> x0, waiting for transfers between devices: 739 us -> none  [the longest x8 422 us: summed(): grad = lax.psum_scatter(grad, 'mp', scatter_dimension=0, tiled=True)]
    pallas_call x7 -> x6, Pallas kernels: 358 us -> 488 us  [the longest x4 358 us: attention_call(): pl.pallas_call(functools.partial(kernel, biased, front, lead, host), out_...]
    unnamed x30 -> x5, waiting for transfers between devices: 126 us -> 0.59 us
    all_gather x1, waiting for transfers between devices: 84.1 us -> 28.3 us  [body(): lax.all_gather(result, 'mp', axis=0, tiled=True).reshape(inputs.shape)]
    all_gather x1, waiting for transfers between devices: 44.4 us -> 0.01 us  [body(): lax.all_gather(grad_memory, 'mp', axis=0, tiled=True).reshape(encoded.shape)]
    psum x1 -> x0, blocking collectives: 42.4 us -> none  [body(): small = lax.psum(small, ('dp', 'mp'))]
    all_gather x5 -> x0, blocking collectives: 42.3 us -> none  [gather(): shard = lax.all_gather(shard, name, axis=axis, tiled=True)]
    unnamed x58, local copies, waits for them, and re-layouts: 37.1 us -> 16.4 us
  transfers between devices with their start and end apart: 27 -> 5, of which waited for: 25 -> 3; matrix products, arithmetic and copies ran while one was open for 3% -> 2% of each run, Pallas kernels for 6% -> 30%
where the time goes in v2:
time: 835 us; the launch traced here: 825 us
  Pallas kernels  618 us (74%)
  waiting for transfers between devices  135 us (16%)
  local copies, waits for them, and re-layouts  44.9 us (5%)
  between operations  14.4 us (2%)
  other arithmetic  11.2 us (1%)
    pallas_call x4, Pallas kernels, attention_call(): pl.pallas_call(functools.partial(kernel, biased, front, lead, host), out_...  358 us
    pallas_call x2, Pallas kernels, run(): pl.pallas_call(kernel, grid=(1,), out_shape=self.outs, in_specs=self.in_s...  130 us
    pallas_call x6, Pallas kernels, kernel_call(): pl.pallas_call(body, grid=(steps,), out_shape=[jax.ShapeDtypeStruct(a.sha...  129 us
    all_gather x1, waiting for transfers between devices, body(): lax.all_gather(grad_rows, 'mp', axis=0, tiled=True).reshape(inputs.shape)  85.5 us
    all_gather x1, waiting for transfers between devices, body(): lax.all_gather(result, 'mp', axis=0, tiled=True).reshape(inputs.shape)  28.3 us
    reduce_scatter x2, waiting for transfers between devices, share(): lax.psum_scatter(array, 'mp', scatter_dimension=0, axis_index_groups=shar...  21.1 us
  transfers between devices with their start and end apart: 5, of which 3 were waited for; matrix products, arithmetic and copies ran while one was open for 2% of the time, Pallas kernels for 30%

profile of v2, /device:TPU:8, one launch (start us, length us, event | category | flops | bytes accessed | tf_op | source)
XLA Modules:
  0.0 824.6 jit_solution(9811716890444864150)
XLA Ops:
  11.0 37.6 %gather_self.1 = (bf16[4,8,128,512]{3,2,1,0:T(8,128)(2,1)}, bf16[4,8,16,128]{3,2,1,0:T(8,128)(2,1)}, bf16[1024,1024]{1,0:T(8,128)(2,1)}) custom-call(bf16[128,512]{1,0:T(8,128)(2,1)} %pad_maximum_fusion.1.refs_0_, bf16[16,128]{1,0:T(8,128)(2,1)} %pad.29.refs_1_, bf16[256,128]{1,0:T(8,128)(2,1)} %refs_2_.1), custom_call_target="tpu_custom_call" | custom-call | tf_op jit(solution)/shard_map/gather_self/pallas_call | solution.py:432
  50.2 3.2 dynamic-slice_bitcast_fusion
  53.6 2.6 dynamic-slice_bitcast_fusion.2.x_ref
  62.3 2.5 dynamic-slice_bitcast_fusion.1.up_ref
  64.8 3.2 pad_dynamic-slice_fusion.x_ref
  68.0 14.6 %self_project.1 = (bf16[640,1024]{1,0:T(8,128)(2,1)}, bf16[1536,512]{1,0:T(8,128)(2,1)}, bf16[1536,512]{1,0:T(8,128)(2,1)}, bf16[544,1024]{1,0:T(8,128)(2,1)}) custom-call(bf16[1536,1024]{1,0:T(8,128)(2,1)} %pad_dynamic-slice_fusion.x_ref, f32[1,1024]{1,0:T(1,128)} %get-tuple-element.196.gain_ref, bf16[4,1024,512]{2,1,0:T(8,128)(2,1)} %bitcast.77), custom_call_target="tpu_custom_call" | custom-call | flops 4563402752 | bytes 16777216 | tf_op jit(solution)/shard_map/self_project/pallas_call | solution.py:790
  83.3 106.0 %self_forward.1 = (bf16[640,1024]{1,0:T(8,128)(2,1)}, f32[4,4,640]{2,1,0:T(4,128)}, bf16[4,8,128,512]{3,2,1,0:T(8,128)(2,1)}, bf16[1024,1024]{1,0:T(8,128)(2,1)}, bf16[4,8,128,704]{3,2,1,0:T(8,128)(2,1)}) custom-call(bf16[640,1024]{1,0:T(8,128)(2,1)} %get-tuple-element.77.refs_0_, bf16[1536,512]{1,0:T(8,128)(2,1)} %get-tuple-element.78.refs_1_, ...), custom_call_target="tpu_custom_call" | custom-call | flops 4026531840 | bytes 16777216 | tf_op jit(solution)/shard_map/self_forward/pallas_call | solution.py:680
  189.3 10.0 %cross_project.1 = (f32[544,1024]{1,0:T(8,128)}, bf16[544,1024]{1,0:T(8,128)(2,1)}, bf16[640,1024]{1,0:T(8,128)(2,1)}, bf16[512,512]{1,0:T(8,128)(2,1)}, bf16[512,512]{1,0:T(8,128)(2,1)}) custom-call(bf16[640,1024]{1,0:T(8,128)(2,1)} %get-tuple-element.80.o_ref.refs_3_, bf16[1024,1024]{1,0:T(8,128)(2,1)} %get-tuple-element.81.wo_ref, ...), custom_call_target="tpu_custom_call" | custom-call | flops 3422552064 | bytes 16777216 | tf_op jit(solution)/shard_map/cross_project/pallas_call | solution.py:790
  200.2 72.5 %cross_forward.1 = (bf16[640,1024]{1,0:T(8,128)(2,1)}, f32[4,4,640]{2,1,0:T(4,128)}, bf16[4,8,128,704]{3,2,1,0:T(8,128)(2,1)}, bf16[2816,1024]{1,0:T(8,128)(2,1)}) custom-call(bf16[640,1024]{1,0:T(8,128)(2,1)} %get-tuple-element.83.refs_0_, bf16[512,512]{1,0:T(8,128)(2,1)} %get-tuple-element.84.refs_1_, bf16[512,512]{1,0:T(8,128)(2,1)} %get-tuple-element.85.refs_2_, ...), custom_call_target="tpu_custom_call" | custom-call | flops 1342177280 | bytes 16777216 | tf_op jit(solution)/shard_map/cross_forward/pallas_call | solution.py:680
  272.7 63.3 %feed.1 = (bf16[544,1024]{1,0:T(8,128)(2,1)}, f32[544,1024]{1,0:T(8,128)}, f32[1,1024]{1,0:T(1,128)}, bf16[4,1024,704]{2,1,0:T(8,128)(2,1)}, bf16[4,1024,704]{2,...) custom-call(bf16[640,1024]{1,0:T(8,128)(2,1)} %get-tuple-element.86.o_ref.refs_, ...), custom_call_target="tpu_custom_call" | custom-call | flops 28236054528 | bytes 16777216 | tf_op jit(solution)/shard_map/feed/pallas_call | solution.py:790
  336.1 66.3 %cross_backward.1 = (bf16[640,1024]{1,0:T(8,128)(2,1)}, bf16[512,512]{1,0:T(8,128)(2,1)}, bf16[512,512]{1,0:T(8,128)(2,1)}, f32[704,128]{1,0:T(8,128)}) custom-call(bf16[640,1024]{1,0:T(8,128)(2,1)} %get-tuple-element.83.refs_0_, bf16[512,512]{1,0:T(8,128)(2,1)} %get-tuple-element.84.refs_1_, bf16[512,512]{1,0:T(8,128)(2,1)} %get-tuple-element.85.refs_2_, ...), custom_call_target="tpu_custom_call" | custom-call | flops 3355443200 | bytes 16777216 | tf_op jit(solution)/shard_map/cross_backward/pallas_call | solution.py:680
  402.4 2.3 pad_maximum_fusion
  404.7 19.7 %cross_back.1 = (bf16[4,1024,256]{2,1,0:T(8,128)(2,1)}, f32[544,1024]{1,0:T(8,128)}, f32[1,1024]{1,0:T(1,128)}, bf16[640,1024]{1,0:T(8,128)(2,1)}, bf16[1024,1024]{1,0:T(8,128)(2,1)}) custom-call(bf16[640,1024]{1,0:T(8,128)(2,1)} %get-tuple-element.96.dq_ref, bf16[4,1024,512]{2,1,0:T(8,128)(2,1)} %bitcast.63, bf16[544,1024]{1,0:T(8,128)(2,1)} %get-tuple-element.97.n_ref, ...), custom_call_target="tpu_custom_call" | custom-call | flops 4563402752 | bytes 16777216 | tf_op jit(solution)/shard_map/cross_back/pallas_call | solution.py:790
  424.4 113.5 %self_backward.1 = (bf16[640,1024]{1,0:T(8,128)(2,1)}, bf16[1536,512]{1,0:T(8,128)(2,1)}, bf16[1536,512]{1,0:T(8,128)(2,1)}, f32[4,4,1664]{2,1,0:T(4,128)}, f32[128,704]{1,0:T(8,128)}, /*index=5*/f32[128,704]{1,0:T(8,128)}) custom-call(bf16[640,1024]{1,0:T(8,128)(2,1)} %get-tuple-element.77.refs_0_, bf16[1536,512]{1,0:T(8,128)(2,1)} %get-tuple-element.78.refs_1_, ...), custom_call_target="tpu_custom_call" | custom-call | flops 10066329600 | bytes 16777216 | tf_op jit(solution)/shard_map/self_backward/pallas_call | solution.py:680
  537.9 4.3 fusion.2
  545.2 5.7 memory_back.1
  551.5 21.1 %reduce-scatter.3.cloned.1.call-done = bf16[544,1024]{1,0:T(8,128)(2,1)} async-done(((bf16[1088,1024]{1,0:T(8,128)(2,1)}), bf16[544,1024]{1,0:T(8,128)(2,1)}) %reduce-scatter.3.cloned.1.call-update) | async-done | bytes 1114128 | tf_op jit(solution)/shard_map/reduce_scatter | solution.py:1323
  572.7 2.3 fusion.10
  575.0 16.0 %self_back.1 = (bf16[4,1024,256]{2,1,0:T(8,128)(2,1)}, bf16[4,1024,256]{2,1,0:T(8,128)(2,1)}, bf16[544,1024]{1,0:T(8,128)(2,1)}, f32[1,1024]{1,0:T(1,128)}) custom-call(bf16[640,1024]{1,0:T(8,128)(2,1)} %get-tuple-element.103.dq_ref, bf16[544,512]{1,0:T(8,128)(2,1)} %get-tuple-element.187.dk_ref, bf16[544,512]{1,0:T(8,128)(2,1)} %get-tuple-element.186.dv_ref, ...), custom_call_target="tpu_custom_call" | custom-call | flops 4563402752 | bytes 16777216 | tf_op jit(solution)/shard_map/self_back/pallas_call | solution.py:790
  594.5 92.5 %scatter_rest.1 = (f32[128,256]{1,0:T(8,128)}, f32[128,256]{1,0:T(8,128)}, f32[128,256]{1,0:T(8,128)}, f32[128,256]{1,0:T(8,128)}, f32[256,128]{1,0:T(8,128)}, /*index=5*/f32[256,128]{1,0:T(8,128)}, f32[8,128]{1,0:T(8,128)}) custom-call(bf16[4,8,128,256]{3,2,1,0:T(8,128)(2,1)} %bitcast.65, bf16[4,8,128,256]{3,2,1,0:T(8,128)(2,1)} %bitcast.66, ...), custom_call_target="tpu_custom_call" | custom-call | tf_op jit(solution)/shard_map/scatter_rest/pallas_call | solution.py:432
  691.3 28.3 %all-gather.4.cloned.1.call-done = bf16[2176,1024]{1,0:T(8,128)(2,1)} async-done(((bf16[544,1024]{1,0:T(8,128)(2,1)}), bf16[2176,1024]{1,0:T(8,128)(2,1)}) %all-gather.4.cloned.1.call-update) | async-done | bytes 4456464 | tf_op jit(solution)/shard_map/all_gather | solution.py:1308
  719.5 85.5 %all-gather.6.cloned.1.call-done = bf16[2176,1024]{1,0:T(8,128)(2,1)} async-done(((bf16[544,1024]{1,0:T(8,128)(2,1)}), bf16[2176,1024]{1,0:T(8,128)(2,1)}) %all-gather.6.cloned.1.call-update) | async-done | bytes 4456464 | tf_op jit(solution)/shard_map/all_gather | solution.py:1346
  805.0 5.0 copy.71
  810.0 2.2 copy.72
  (110 shorter events, 30.0 us)
Async XLA Ops:
  7.2 52.7 %copy-start = (bf16[2,512,1024]{2,1,0:T(8,128)(2,1)S(1)}, bf16[2,512,1024]{2,1,0:T(8,128)(2,1)}, u32[]{:S(2)}) copy-start(bf16[2,512,1024]{2,1,0:T(8,128)(2,1)} %param.22) | copy-start | bytes 6291460
  7.2 536.1 %reduce-scatter.5.cloned.1.call-start = ((), (), s32[]{:S(2)}) async-start(), calls=%async_computation.5 | async-start | bytes 1572864 | tf_op jit(solution)/shard_map/reduce_scatter | solution.py:1323
  50.2 3.2 copy-start.17
  53.4 4.5 copy-start.22
  53.4 5.6 copy-start.7
  53.5 7.4 copy-start.21
  53.5 7.9 copy-start.8
  68.0 14.7 %copy-start.14 = (bf16[128,256]{1,0:T(8,128)(2,1)S(1)}, bf16[128,256]{1,0:T(8,128)(2,1)}, u32[]{:S(2)}) copy-start(bf16[128,256]{1,0:T(8,128)(2,1)} %param.33) | copy-start | bytes 196612
  68.0 14.7 %copy-start.15 = (bf16[128,128]{1,0:T(8,128)(2,1)S(1)}, bf16[128,128]{1,0:T(8,128)(2,1)}, u32[]{:S(2)}) copy-start(bf16[128,128]{1,0:T(8,128)(2,1)} %param.35) | copy-start | bytes 98308
  68.0 14.7 %copy-start.16 = (bf16[128,128]{1,0:T(8,128)(2,1)S(1)}, bf16[128,128]{1,0:T(8,128)(2,1)}, u32[]{:S(2)}) copy-start(bf16[128,128]{1,0:T(8,128)(2,1)} %param.34) | copy-start | bytes 98308
  404.7 168.0 %reduce-scatter.3.cloned.1.call-start = ((), (), s32[]{:S(2)}) async-start(), calls=%async_computation.3 | async-start | bytes 3342336 | tf_op jit(solution)/shard_map/reduce_scatter | solution.py:1323
  542.3 149.0 %all-gather.8.cloned.1.call-start = ((), (), s32[]{:S(2)}) async-start(), calls=%async_computation.6 | async-start | bytes 2621440 | tf_op jit(solution)/shard_map/all_gather | solution.py:1334
  550.9 168.6 %all-gather.4.cloned.1.call-start = ((), (), s32[]{:S(2)}) async-start(), calls=%async_computation.2 | async-start | bytes 5570560 | tf_op jit(solution)/shard_map/all_gather | solution.py:1308
  551.5 253.5 %all-gather.6.cloned.1.call-start = ((), (), s32[]{:S(2)}) async-start(), calls=%async_computation.4 | async-start | bytes 5570560 | tf_op jit(solution)/shard_map/all_gather | solution.py:1346
  575.0 16.1 %copy-start.13 = (f32[4,4,1664]{2,1,0:T(4,128)S(1)}, f32[4,4,1664]{2,1,0:T(4,128)}, u32[]{:S(2)}) copy-start(f32[4,4,1664]{2,1,0:T(4,128)} %get-tuple-element.121) | copy-start | bytes 319492
  575.0 16.9 %copy-start.5 = (f32[128,704]{1,0:T(8,128)S(1)}, f32[128,704]{1,0:T(8,128)}, u32[]{:S(2)}) copy-start(f32[128,704]{1,0:T(8,128)} %get-tuple-element.183) | copy-start | bytes 1081348
  591.0 2.7 copy-start.18
  591.1 2.7 copy-start.19
  591.1 2.7 copy-start.20
  805.0 5.0 copy-start.2
  810.0 3.1 copy-start.3
  813.2 2.7 copy-start.10
  813.2 3.3 copy-start.9
  813.2 4.0 copy-start.6
  (4 other events, 7.6 us)
Sparse Core Ops, SparseCore 0:
  404.8 17.3 reduce-scatter.4
  542.4 30.2 reduce-scatter.2
  574.3 50.8 all-gather.7
  626.6 92.9 all-gather.3
  721.0 84.0 all-gather.5

commit v3 on v2

v3 whole, which is shorter than its diff:
```python
import functools

import jax
import jax.numpy as jnp
from jax import lax
from jax.experimental import pallas as pl
from jax.experimental.pallas import tpu as pltpu
from jax.sharding import PartitionSpec as P

HEAD_DIM = 64
TILE_Q = 128
TILE_K = 256
EPSILON = 1e-06
NEGATIVE = -1e30
HIGHEST = lax.Precision.HIGHEST
F32 = jnp.float32
BF16 = jnp.bfloat16


def dot(left, right, dims, precision=None):
    return lax.dot_general(
        left, right, ((dims[0], dims[1]), ((), ())), precision=precision, preferred_element_type=F32
    )


def mm(left, right):
    return dot(left, right, ((1,), (0,)))


def mm_nt(left, right):
    return dot(left, right, ((1,), (1,)))


def mm_tn(left, right):
    return dot(left, right, ((0,), (0,)))


def round_up(value, unit):
    return (value + unit - 1) // unit * unit


def chunked(total, size, run):
    def once(n, carry):
        run(pl.multiple_of(n * size, size))
        return carry

    lax.fori_loop(0, total // size, once, 0)


MESH = pl.DeviceIdType.MESH


class Place:
    def __init__(self, mp):
        self.mp = mp
        self.i = lax.axis_index("dp")
        self.z = lax.axis_index("mp")
        core = lax.rem(self.i, 2)
        across = lax.rem(lax.div(self.i, 2), 2)
        up = lax.div(self.i, 4)
        self.core, self.across, self.up = core, across, up
        self.ic = self.i + 1 - 2 * core
        self.ix = self.i + 2 - 4 * across
        self.iy = self.i + 4 - 8 * up
        self.ixy = self.ix + 4 - 8 * up


def enter(place):
    barrier = pltpu.get_barrier_semaphore()
    z, mp = place.z, place.mp
    for near in (place.ic, place.ix, place.iy):
        pl.semaphore_signal(barrier, 1, device_id=(near, z), device_id_type=MESH)

    for d in range(1, mp):
        far = lax.rem(z + d, mp)
        pl.semaphore_signal(barrier, 1, device_id=(place.i, far), device_id_type=MESH)
    pl.semaphore_wait(barrier, 3 + mp - 1)


def all_slots(mp):
    return [(0, 0)] + [(d, s) for d in range(1, mp) for s in (0, 1)]


def for_slot(place, slot, run):
    d, side = slot
    if d == 0:
        run(place.z)
    elif side == 0:
        pl.when(place.z >= d)(lambda: run(place.z - d))
    else:
        pl.when(place.z < place.mp - d)(lambda: run(place.z + d))


def region(ref, i, z, shard):
    if len(ref.shape) == 4:
        return ref.at[z, i]
    rows, cols = shard
    return ref.at[pl.ds(pl.multiple_of(z * rows, rows), rows), pl.ds(pl.multiple_of(i * cols, cols), cols)]


def gather_steps(place, shards, outs, send, recv, local):
    mp, i, z = place.mp, place.i, place.z
    units = range(len(shards))

    def here(u, i2, z2):
        return region(outs[u], i2, z2, shards[u].shape)

    def copy(u, kind, i2, z2, to, src=None):
        spot = here(u, i2, z2)
        return pltpu.make_async_remote_copy(
            src_ref=spot if src is None else src, dst_ref=spot, send_sem=send.at[u, kind, z2],
            recv_sem=recv.at[u, kind, z2], device_id=to, device_id_type=MESH)

    def route(u, z2):
        odd = lax.rem(z2 + u, 2)
        first = place.ix + odd * (place.iy - place.ix)
        second = place.iy + odd * (place.ix - place.iy)
        return odd, first, second

    slots = all_slots(mp)

    def stage1(slot):
        d, s = slot

        def run(z2):
            for u in units:
                src = shards[u] if d == 0 else None
                if d > 0:
                    copy(u, s, i, z2, (i, z)).wait_recv()
                copy(u, 2, i, z2, (place.ix, z), src).start()
                copy(u, 3, i, z2, (place.iy, z), src).start()
                copy(u, 5, i, z2, (place.ic, z), src).start()
                if d == 0:
                    pltpu.make_async_copy(shards[u], here(u, i, z), local.at[u]).start()

        for_slot(place, slot, run)

    def along(u, d, up):
        return pltpu.make_async_remote_copy(
            src_ref=shards[u], dst_ref=here(u, i, z), send_sem=send.at[u, 0 if up else 1, d],
            recv_sem=recv.at[u, 0 if up else 1, z], device_id=(i, z + d if up else z - d),
            device_id_type=MESH)

    def depart():
        for d in range(1, mp):
            for u in units:
                pl.when(z < mp - d)(lambda u=u, d=d: along(u, d, True).start())
                pl.when(z >= d)(lambda u=u, d=d: along(u, d, False).start())

    def stage2(slot):
        def run(z2):
            for u in units:
                odd, first, second = route(u, z2)
                kind = 2 + odd
                spot = here(u, first, z2)
                pltpu.make_async_remote_copy(src_ref=spot, dst_ref=spot, send_sem=send.at[u, kind, z2],
                    recv_sem=recv.at[u, kind, z2], device_id=(first, z), device_id_type=MESH).wait_recv()
                copy(u, 4, first, z2, (second, z)).start()
                copy(u, 6, first, z2, (place.ic, z)).start()

        for_slot(place, slot, run)

    def stage3(slot):
        def run(z2):
            for u in units:
                odd, first, second = route(u, z2)
                kind = 3 - odd
                spot = here(u, second, z2)
                pltpu.make_async_remote_copy(src_ref=spot, dst_ref=spot, send_sem=send.at[u, kind, z2],
                    recv_sem=recv.at[u, kind, z2], device_id=(second, z), device_id_type=MESH).wait_recv()
                copy(u, 7, second, z2, (place.ic, z)).start()
                copy(u, 4, place.ixy, z2, (second, z)).wait_recv()
                copy(u, 8, place.ixy, z2, (place.ic, z)).start()

        for_slot(place, slot, run)

    def other(i2):
        return i2 + place.ic - i

    def finish(slot):
        d, s = slot

        def run(z2):
            for u in units:
                odd, first, second = route(u, z2)
                for kind, i2 in ((5, i), (6, first), (7, second), (8, place.ixy)):
                    copy(u, kind, other(i2), z2, (place.ic, z)).wait_recv()
                if d == 0:
                    for far in range(1, mp):
                        pl.when(z < mp - far)(lambda u=u, far=far: along(u, far, True).wait_send())
                        pl.when(z >= far)(lambda u=u, far=far: along(u, far, False).wait_send())
                for kind in range(2, 9):
                    copy(u, kind, i, z2, (i, z)).wait_send()
                if d == 0:
                    pltpu.make_async_copy(shards[u], here(u, i, z), local.at[u]).wait()

        for_slot(place, slot, run)

    steps = [depart]
    n = len(slots)
    for k in range(n + 2):
        if k < n:
            steps.append(functools.partial(stage1, slots[k]))
        if 0 <= k - 1 < n:
            steps.append(functools.partial(stage2, slots[k - 1]))
        if 0 <= k - 2 < n:
            steps.append(functools.partial(stage3, slots[k - 2]))
    return steps, [functools.partial(finish, slot) for slot in slots]


def gather_shape(shard, kind, dp, mp):
    rows, cols = shard.shape
    if kind == "by_dp":
        return jax.ShapeDtypeStruct((mp, dp, rows, cols), shard.dtype)
    return jax.ShapeDtypeStruct((mp * rows, dp * cols), shard.dtype)


def add_into(target, *others):
    rows = target.shape[0]
    size = 64 if rows % 64 == 0 else rows

    def some(at):
        part = pl.ds(at, size)
        total = target[part, :].astype(F32)
        for other in others:
            total = total + other[part, :].astype(F32)
        target[part, :] = total.astype(target.dtype)

    chunked(rows, size, some)


def scatter_scratch(shards, mp):
    scratch = []
    for dims, dtype in shards:
        scratch += [
            pltpu.VMEM((mp, 4) + dims, dtype),
            pltpu.VMEM((mp, 4) + dims, dtype),
            pltpu.VMEM((mp, 3) + dims, dtype),
            pltpu.VMEM((mp,) + dims, dtype),
        ]
    sems = pltpu.SemaphoreType.DMA((len(shards), 8, mp))
    return scratch + [sems, sems, pltpu.SemaphoreType.DMA((len(shards), 4, mp))]


def scatter_steps(place, grads, outs, scratch):
    mp, i, z = place.mp, place.i, place.z
    units = range(len(grads))
    send, recv, local = scratch[-3:]
    own = [scratch[4 * u] for u in units]
    sibling = [scratch[4 * u + 1] for u in units]
    plane = [scratch[4 * u + 2] for u in units]
    line = [scratch[4 * u + 3] for u in units]
    chips = (place.i, place.ix, place.iy, place.ixy)
    slots = all_slots(mp)[::-1]

    def piece(u, i2, z2):
        return region(grads[u], i2, z2, own[u].shape[2:])

    def copy(u, kind, z2, src, dst, to):
        return pltpu.make_async_remote_copy(
            src_ref=src, dst_ref=dst, send_sem=send.at[u, kind, z2], recv_sem=recv.at[u, kind, z2],
            device_id=to, device_id_type=MESH)

    def load(u, k, z2):
        return pltpu.make_async_copy(piece(u, chips[k], z2), own[u].at[z2, k], local.at[u, k, z2])

    def across(u, k, z2):
        other = chips[k] + place.ic - i
        return copy(u, k, z2, piece(u, other, z2), sibling[u].at[z2, k], (place.ic, z))

    def route(u, z2):
        odd = lax.rem(z2 + u, 2)
        first = place.ix + odd * (place.iy - place.ix)
        second = place.iy + odd * (place.ix - place.iy)
        return 1 + odd, 2 - odd, first, second

    def to_second(u, z2, far):
        _, ks, _, second = route(u, z2)
        src = own[u].at[z2, 3] if far else own[u].at[z2, ks]
        return copy(u, 4 if far else 5, z2, src, plane[u].at[z2, 0 if far else 1], (second, z))

    def to_first(u, z2):
        kf, _, first, _ = route(u, z2)
        return copy(u, 6, z2, own[u].at[z2, kf], plane[u].at[z2, 2], (first, z))

    def along(u, z2):
        return pltpu.make_async_remote_copy(
            src_ref=own[u].at[z2, 0], dst_ref=line[u].at[z], send_sem=send.at[u, 7, z2],
            recv_sem=recv.at[u, 7, z], device_id=(i, z2), device_id_type=MESH)

    def arrival(u, z2):
        return pltpu.make_async_remote_copy(
            src_ref=own[u].at[z, 0], dst_ref=line[u].at[z2], send_sem=send.at[u, 7, z],
            recv_sem=recv.at[u, 7, z2], device_id=(i, z), device_id_type=MESH)

    def begin(slot):
        def run(z2):
            for u in units:
                for k in (3, 2, 1, 0):
                    load(u, k, z2).start()
                    across(u, k, z2).start()

        for_slot(place, slot, run)

    def stage1(slot):
        def run(z2):
            for u in units:
                for k in (3, 2, 1, 0):
                    load(u, k, z2).wait()
                    across(u, k, z2).wait_recv()
                for k in range(4):
                    add_into(own[u].at[z2, k], sibling[u].at[z2, k])
                to_second(u, z2, True).start()
                to_second(u, z2, False).start()

        for_slot(place, slot, run)

    def stage2(slot):
        def run(z2):
            for u in units:
                kf = route(u, z2)[0]
                to_second(u, z2, True).wait_recv()
                add_into(own[u].at[z2, kf], plane[u].at[z2, 0])
                to_first(u, z2).start()

        for_slot(place, slot, run)

    def stage3(slot):
        d, side = slot

        def run(z2):
            for u in units:
                mine = own[u].at[z2, 0]
                to_second(u, z2, False).wait_recv()
                to_first(u, z2).wait_recv()
                add_into(mine, plane[u].at[z2, 1], plane[u].at[z2, 2])
                if d > 0:
                    along(u, z2).start()

        for_slot(place, slot, run)

    def finish(slot):
        d, side = slot

        def run(z2):
            for u in units:
                for k in range(4):
                    across(u, k, z2).wait_send()
                to_second(u, z2, True).wait_send()
                to_second(u, z2, False).wait_send()
                to_first(u, z2).wait_send()
                if d > 0:
                    along(u, z2).wait_send()

        for_slot(place, slot, run)

    def collect(slot):
        d, side = slot

        def run(z2):
            for u in units:
                if d == 0:
                    outs[u][...] = own[u][z, 0].astype(F32)
                else:
                    arrival(u, z2).wait_recv()
                    add_into(outs[u], line[u].at[z2])

        for_slot(place, slot, run)

    steps = [functools.partial(begin, slot) for slot in slots]
    n = len(slots)
    for k in range(n + 2):
        if k < n:
            steps.append(functools.partial(stage1, slots[k]))
        if 0 <= k - 1 < n:
            steps.append(functools.partial(stage2, slots[k - 1]))
        if 0 <= k - 2 < n:
            steps.append(functools.partial(stage3, slots[k - 2]))
    last = [functools.partial(collect, slot) for slot in all_slots(mp)]
    return steps, last + [functools.partial(finish, slot) for slot in slots]


def shard_of(grad, dp, mp):
    if len(grad.shape) == 4:
        return grad.shape[2:]
    return (grad.shape[0] // mp, grad.shape[1] // dp)


def line_steps(place, rows, outs, send, recv, local):
    mp, i, z = place.mp, place.i, place.z

    def spot(u, z2):
        parts = outs[u].shape[2]
        return outs[u].at[lax.div(z2, parts), :, lax.rem(z2, parts)]

    def copy(u, up, z2, to, src=None):
        here = spot(u, z2)
        kind = 0 if up else 1
        return pltpu.make_async_remote_copy(
            src_ref=here if src is None else src, dst_ref=here, send_sem=send.at[u, kind, z2],
            recv_sem=recv.at[u, kind, z2], device_id=(i, to), device_id_type=MESH)

    def keep(u):
        return pltpu.make_async_copy(rows[u], spot(u, z), local.at[u])

    def move(slot):
        d, side = slot

        def run(z2):
            for u in range(len(rows)):
                src = rows[u] if d == 0 else None
                if d > 0:
                    copy(u, side == 0, z2, z).wait_recv()
                else:
                    keep(u).start()
                if d == 0 or side == 0:
                    pl.when(z < mp - 1)(lambda u=u, src=src: copy(u, True, z2, z + 1, src).start())
                if d == 0 or side == 1:
                    pl.when(z > 0)(lambda u=u, src=src: copy(u, False, z2, z - 1, src).start())

        for_slot(place, slot, run)

    def finish(slot):
        d, side = slot

        def run(z2):
            for u in range(len(rows)):
                if d == 0:
                    keep(u).wait()
                if d == 0 or side == 0:
                    pl.when(z < mp - 1)(lambda u=u: copy(u, True, z2, z).wait_send())
                if d == 0 or side == 1:
                    pl.when(z > 0)(lambda u=u: copy(u, False, z2, z).wait_send())

        for_slot(place, slot, run)

    steps = [functools.partial(move, slot) for slot in all_slots(mp)]
    return steps, [functools.partial(finish, slot) for slot in all_slots(mp)]


def woven(*lists):
    total = [(n / len(steps), k, n) for k, steps in enumerate(lists) for n in range(len(steps))]
    return [lists[k][n] for _, k, n in sorted(total)]


class Transfers:
    swap = None

    def __init__(self, dp, mp, cid, shards=(), kinds=(), grads=(), rows=(), spread=()):
        self.dp, self.mp, self.cid = dp, mp, cid
        self.shards, self.kinds, self.grads = list(shards), list(kinds), list(grads)
        self.rows = list(rows)
        self.args = self.shards + self.grads + self.rows
        spots = [(shard_of(g, dp, mp), g.dtype) for g in self.grads]
        self.outs = [gather_shape(s, k, dp, mp) for s, k in zip(shards, kinds)]
        self.outs += [jax.ShapeDtypeStruct(s, F32) for s, _ in spots]
        any_space = pl.BlockSpec(memory_space=pl.ANY)
        self.in_specs = [any_space] * len(self.args)
        self.out_specs = [any_space] * len(self.shards)
        self.out_specs += [pl.BlockSpec(s, lambda *_: (0, 0)) for s, _ in spots]
        self.outs += [jax.ShapeDtypeStruct(dims, r.dtype) for r, dims in zip(self.rows, spread)]
        self.out_specs += [any_space] * len(self.rows)
        self.scratch = []
        if self.rows:
            sems = pltpu.SemaphoreType.DMA((len(self.rows), 2, mp))
            self.scratch += [sems, sems, pltpu.SemaphoreType.DMA((len(self.rows),))]
        if self.shards:
            sems = pltpu.SemaphoreType.DMA((len(self.shards), 9, mp))
            self.scratch += [sems, sems, pltpu.SemaphoreType.DMA((len(self.shards),))]
        if self.grads:
            self.scratch += scatter_scratch(spots, mp)

    def steps(self, ins, outs, scratch):
        place = Place(self.mp)
        lists, last = [], []

        def take(steps, ends):
            lists.append(steps)
            last.extend(ends)

        count, more = len(self.shards), len(self.shards) + len(self.grads)
        if self.rows:
            take(*line_steps(place, ins[more:], outs[more:], *scratch[:3]))
            scratch = scratch[3:]
        if count:
            take(*gather_steps(place, ins[:count], outs[:count], *scratch[:3]))
            scratch = scratch[3:]
        if self.grads:
            take(*scatter_steps(place, ins[count:more], outs[count:more], scratch))
        return [functools.partial(enter, place)] + woven(*lists), last

    def params(self, limit):
        return pltpu.CompilerParams(
            collective_id=self.cid, has_side_effects=True, vmem_limit_bytes=limit
        )

    def run(self, name):
        count = len(self.args)

        def kernel(*refs):
            outs = refs[count : count + len(self.outs)]
            steps, last = self.steps(refs[:count], outs, refs[count + len(self.outs) :])
            for step in steps + last:
                step()

        return pl.pallas_call(
            kernel, grid=(1,), out_shape=self.outs, in_specs=self.in_specs, out_specs=self.out_specs,
            scratch_shapes=self.scratch, compiler_params=self.params(60 << 20), name=name,
        )(*self.args)


class Pace:
    def __init__(self, found, each):
        self.steps, self.last = found
        self.group, self.groups, self.each, self.at = pl.program_id(0), pl.num_programs(0), each, 0

    def place(self):
        total = self.groups * self.each
        for n, step in enumerate(self.steps):
            group, at = divmod(n * total // len(self.steps), self.each)
            if at == self.at:
                pl.when(self.group == group)(step)
        self.at += 1

    def end(self):
        @pl.when(self.group == self.groups - 1)
        def _():
            for step in self.last:
                step()


def skew(row, height):
    wide = jnp.broadcast_to(row, (height, row.shape[1]))
    return pltpu.roll(wide, 0, axis=1, stride=1, stride_axis=0)


def widened(tile):
    zero = jnp.zeros((tile.shape[0], HEAD_DIM), tile.dtype)
    found = []
    for h in range(4):
        piece = tile[:, HEAD_DIM * h : HEAD_DIM * (h + 1)]
        found.append(jnp.concatenate([piece, zero] if h < 2 else [zero, piece], axis=1))
    return jnp.concatenate(found, axis=0)


def narrowed(wide):
    n = wide.shape[1] // 4
    found = []
    for h in range(4):
        base = HEAD_DIM * (h // 2)
        found.append(wide[base : base + HEAD_DIM, n * h : n * (h + 1)])
    return jnp.concatenate(found, axis=0).T


def four(row):
    return jnp.concatenate([row] * 4, axis=1)


class Tiles:
    def __init__(self, rows, length, parts):
        self.rows, self.parts, self.blk = rows, parts, 64 // parts
        self.list = [(at, min(TILE_Q, rows - at)) for at in range(0, rows, TILE_Q)]
        self.span = TILE_Q * parts // TILE_K
        self.reach = round_up(length, TILE_K)
        self.strips = len(self.list) * self.span
        self.lead = self.span * TILE_K
        self.width = self.lead + self.strips * TILE_K

    def keys(self, a):
        return min((a + 1) * self.span, self.reach // TILE_K)

    def strip(self, a, m):
        return (a + 1) * self.span - 1 - m

    def windows(self, n):
        runs = [(s * self.blk, 64 * s) for s in range(n // self.blk)]
        return [(e, self.lead + (e + 1 - self.span) * TILE_K, runs) for e in range(self.strips)]


def build_strips(tiles, vec_ref, strip, tail):
    for h in range(4):
        moved = skew(vec_ref[0, h : h + 1, :], TILE_K)
        for ref in (strip, tail):
            n = ref.shape[2] // 4
            for e, at, runs in tiles.windows(n):
                cut = [moved[:, at + far : at + far + tiles.blk] for _, far in runs]
                ref[e, :, n * h : n * (h + 1)] = jnp.concatenate(cut, axis=1)


def split_refs(refs, host, ins, outs):
    if host is None:
        return list(refs), ([], [])
    a, b = len(host.args), len(host.outs)
    cut = [0, ins, ins + a, ins + a + outs, ins + a + outs + b, len(refs) - len(host.scratch), len(refs)]
    part = [list(refs[i:j]) for i, j in zip(cut, cut[1:])]
    return part[0] + part[2] + part[4], host.steps(part[1], part[3], part[5])


def tile_valid(biased, mask, keys_ref, m):
    if biased:
        index = lax.broadcasted_iota(jnp.int32, (TILE_K, mask.shape[1]), 0)
        return index >= mask - m * TILE_K
    keys = keys_ref[pl.ds(m * TILE_K, TILE_K), :]
    reps = -(-mask.shape[1] // keys.shape[1])
    return jnp.concatenate([keys] * reps, axis=1)[:, : mask.shape[1]] == mask


def forward_kernel(biased, tiles, host, *refs):
    refs, steps = split_refs(refs, host, 5, 2)
    if biased:
        q_ref, k_ref, v_ref, mask_ref, vec_ref, o_ref, lse_ref, vt, s_s, strip, tail = refs
        keys_ref = None
        build_strips(tiles, vec_ref, strip, tail)
    else:
        q_ref, k_ref, v_ref, mask_ref, keys_ref, o_ref, lse_ref, vt, s_s = refs
    vt[...] = v_ref[...].T
    counts = [tiles.keys(a) if biased else k_ref.shape[0] // TILE_K for a in range(len(tiles.list))]
    pace = Pace(steps, 2 * sum(counts))
    for a, (at, n) in enumerate(tiles.list):
        lanes = 4 * n
        q4 = widened(q_ref[at : at + n, :])
        mask = mask_ref[a : a + 1, :lanes]
        count = counts[a]
        top = None
        for m in range(count):
            pace.place()
            some = slice(m * TILE_K, (m + 1) * TILE_K)
            s = mm_nt(k_ref[some, :], q4)
            if biased:
                s = s + (strip if n == TILE_Q else tail)[tiles.strip(a, m)]
            s = jnp.where(tile_valid(biased, mask, keys_ref, m), s, NEGATIVE)
            s_s[some, :lanes] = s
            here = jnp.max(s, axis=0, keepdims=True)
            top = here if top is None else jnp.maximum(top, here)
        total = jnp.zeros((1, lanes), F32)
        acc = jnp.zeros((2 * HEAD_DIM, lanes), F32)
        for m in range(count):
            pace.place()
            some = slice(m * TILE_K, (m + 1) * TILE_K)
            p = jnp.exp(s_s[some, :lanes] - top)
            total = total + jnp.sum(p, axis=0, keepdims=True)
            acc = acc + mm(vt[:, some], p.astype(BF16))
        o_ref[at : at + n, :] = narrowed(acc / total).astype(BF16)
        lse_ref[0, a : a + 1, :lanes] = top + jnp.log(total)
    pace.end()


class Exchange:
    def __init__(self, groups, blk, steps):
        self.groups, self.blk, self.steps = groups, blk, steps
        self.rows = groups * blk
        block = (steps, 2, groups, blk, 2 * HEAD_DIM)
        self.scratch = [pltpu.VMEM(block, BF16), pltpu.VMEM(block, BF16), pltpu.VMEM(block, F32)]
        sems = pltpu.SemaphoreType.DMA((steps,))
        self.scratch += [sems, sems]

    def copy(self, place, refs, n):
        gone, come, _, send, recv = refs
        mate = place.z + 1 - 2 * lax.rem(place.z, 2)
        return pltpu.make_async_remote_copy(
            src_ref=gone.at[n], dst_ref=come.at[n], send_sem=send.at[n], recv_sem=recv.at[n],
            device_id=(place.i, mate), device_id_type=MESH)

    def part_of(self, ref, part):
        base = pl.multiple_of(part * self.blk, self.blk)
        if self.groups == 1:
            return ref[pl.ds(base, self.blk), :][None]
        view = ref.reshape(ref.shape[0] // (2 * self.blk), 2 * self.blk, ref.shape[1])
        return view[0 : self.groups, pl.ds(base, self.blk), :]

    def give(self, place, refs, sums):
        n = pl.program_id(0)
        gone, _, kept, _, _ = refs
        part = lax.rem(place.z, 2)
        for which, ref in enumerate(sums):
            gone[n, which] = self.part_of(ref, 1 - part).astype(BF16)
            kept[n, which] = self.part_of(ref, part)
        self.copy(place, refs, n).start()

    def take(self, place, refs, out):
        _, come, kept, _, _ = refs
        cols = 2 * HEAD_DIM
        for n in range(self.steps):
            self.copy(place, refs, n).wait()
            for which in range(2):
                total = kept[n, which] + come[n, which].astype(F32)
                at = (which * self.steps + n) * cols
                out[:, at : at + cols] = total.reshape(self.rows, cols).astype(BF16)


def backward_kernel(biased, tiles, host, *refs):
    swap = None if host is None else host.swap
    refs, steps = split_refs(refs, host, 8, (4 if biased else 3) - (swap is not None))
    if swap is not None:
        swap_refs = refs[-len(swap.scratch) :]
        first = 10 + biased
        refs = refs[:first] + [None] + refs[first : -len(swap.scratch)]
    if biased:
        (
            q_ref, k_ref, v_ref, o_ref, do_ref, lse_ref, mask_ref, vec_ref,
            dq_ref, dist_ref, dv_ref, dk_ref, kt, dk_s, dv_s, strip, tail, slope, slope_tail, line,
        ) = refs
        keys_ref = None
        build_strips(tiles, vec_ref, strip, tail)
        slope[...] = jnp.zeros_like(slope)
        slope_tail[...] = jnp.zeros_like(slope_tail)
    else:
        (
            q_ref, k_ref, v_ref, o_ref, do_ref, lse_ref, mask_ref, keys_ref,
            dq_ref, dv_ref, dk_ref, kt, dk_s, dv_s,
        ) = refs
    kt[...] = k_ref[...].T
    dk_s[...] = jnp.zeros_like(dk_s)
    dv_s[...] = jnp.zeros_like(dv_s)
    counts = [tiles.keys(a) if biased else k_ref.shape[0] // TILE_K for a in range(len(tiles.list))]
    pace = Pace(steps, sum(counts))
    for a, (at, n) in enumerate(tiles.list):
        lanes = 4 * n
        q4 = widened(q_ref[at : at + n, :])
        do4 = widened(do_ref[at : at + n, :])
        mask = mask_ref[a : a + 1, :lanes]
        lse = lse_ref[0, a : a + 1, :lanes]
        both = widened(o_ref[at : at + n, :]).astype(F32) * do4.astype(F32)
        delta = jnp.sum(both.T, axis=0, keepdims=True)
        dq = jnp.zeros((2 * HEAD_DIM, lanes), F32)
        for m in range(counts[a]):
            pace.place()
            some = slice(m * TILE_K, (m + 1) * TILE_K)
            s = mm_nt(k_ref[some, :], q4)
            if biased:
                e = tiles.strip(a, m)
                s = s + (strip if n == TILE_Q else tail)[e]
            p = jnp.exp(jnp.where(tile_valid(biased, mask, keys_ref, m), s - lse, NEGATIVE))
            ds = p * (mm_nt(v_ref[some, :], do4) - delta)
            low = ds.astype(BF16)
            if biased:
                ref = slope if n == TILE_Q else slope_tail
                ref[e] += ds
            dv_s[some, :] += mm(p.astype(BF16), do4)
            dk_s[some, :] += mm(low, q4)
            dq = dq + mm(kt[:, some], low)
        dq_ref[at : at + n, :] = narrowed(dq).astype(BF16)

    if swap is None:
        dk_ref[...] = dk_s[...].astype(BF16)
        dv_ref[...] = dv_s[...].astype(BF16)
    else:
        place = Place(host.mp)
        swap.give(place, swap_refs, (dk_s, dv_s))
    if biased:
        width = tiles.width
        for h in range(4):
            line[...] = jnp.zeros_like(line)
            for ref in (slope, slope_tail):
                n = ref.shape[2] // 4
                for e, at, runs in tiles.windows(n):
                    for near, far in runs:
                        piece = ref[e, :, n * h + near : n * h + near + tiles.blk]
                        line[:, at + far : at + far + tiles.blk] += piece
            part = line[...]
            height = TILE_K
            while height > 8:
                height //= 2
                part = part[:height] + pltpu.roll(part[height:], width - height, axis=1)
            row = part[0:1]
            for j in range(1, 8):
                row = row + pltpu.roll(part, width - j, axis=1)[j : j + 1]
            dist_ref[0, h : h + 1, :] = row
    pace.end()
    if swap is not None:
        pl.when(pace.group == pace.groups - 1)(lambda: swap.take(place, swap_refs, dv_ref))


def spec(shape, index):
    return pl.BlockSpec(shape, index)


def attention_call(kernel, biased, tiles, outs, scratch, args, name, flops, host):
    steps = args[1].shape[1] // (2 * HEAD_DIM)

    def column(array, lanes):
        return spec((array.shape[0], lanes), lambda i: (0, i))

    def placed(array, kind):
        if kind == "wide":
            return column(array, 4 * HEAD_DIM)
        if kind == "key":
            return column(array, 2 * HEAD_DIM)
        if kind == "head":
            return spec((1,) + array.shape[1:], lambda i: (i, 0, 0))
        return spec(array.shape, lambda i: (0, 0))

    kinds = ["wide", "key", "key"]
    if kernel is backward_kernel:
        kinds += ["wide", "wide", "head"]
    kinds += ["flat", "head" if biased else "flat"]
    specs = [placed(array, kind) for array, kind in zip(args, kinds)]
    shapes = [item for item, _ in outs]
    out_specs = [placed(item, kind) for item, kind in outs]
    own = len(shapes)
    params = pltpu.CompilerParams(vmem_limit_bytes=60 << 20)
    args = list(args)
    if host is not None:
        args += host.args
        specs += host.in_specs
        shapes += host.outs
        out_specs += host.out_specs
        scratch = scratch + host.scratch
        params = host.params(62 << 20)
    found = pl.pallas_call(
        functools.partial(kernel, biased, tiles, host),
        grid=(steps,),
        out_shape=shapes,
        in_specs=specs,
        out_specs=out_specs,
        scratch_shapes=scratch,
        compiler_params=params,
        cost_estimate=pl.CostEstimate(flops=flops, bytes_accessed=16 << 20, transcendentals=0),
        name=name,
    )(*args)
    return found[:own], found[own:]


def strip_scratch(tiles):
    last = tiles.list[-1][1]
    return [
        pltpu.VMEM((tiles.strips, TILE_K, 4 * TILE_Q), F32),
        pltpu.VMEM((tiles.strips, TILE_K, 4 * last), F32),
    ]


def attend_forward(q, k, v, mask, extra, tiles, biased, name, host=None):
    steps = k.shape[1] // (2 * HEAD_DIM)
    outs = [
        (jax.ShapeDtypeStruct(q.shape, BF16), "wide"),
        (jax.ShapeDtypeStruct((steps,) + mask.shape, F32), "head"),
    ]
    scratch = [pltpu.VMEM((2 * HEAD_DIM, k.shape[0]), BF16), pltpu.VMEM((k.shape[0], 4 * TILE_Q), F32)]
    if biased:
        scratch += strip_scratch(tiles)
    flops = 4 * q.shape[0] * k.shape[0] * q.shape[1]
    return attention_call(
        forward_kernel, biased, tiles, outs, scratch, (q, k, v, mask, extra), name, flops, host
    )


def attend_backward(q, k, v, o, do, lse, mask, extra, tiles, biased, name, host=None):
    keys, cols = k.shape
    grad = jax.ShapeDtypeStruct(k.shape, BF16)
    outs = [(jax.ShapeDtypeStruct(q.shape, BF16), "wide")]
    scratch = [
        pltpu.VMEM((2 * HEAD_DIM, keys), BF16),
        pltpu.VMEM((keys, 2 * HEAD_DIM), F32),
        pltpu.VMEM((keys, 2 * HEAD_DIM), F32),
    ]
    if biased:
        outs.append((jax.ShapeDtypeStruct(extra.shape, F32), "head"))
        scratch += strip_scratch(tiles) * 2 + [pltpu.VMEM((TILE_K, tiles.width), F32)]
    if host is None:
        outs += [(grad, "key"), (grad, "key")]
    else:
        outs.append((jax.ShapeDtypeStruct((host.swap.rows, 2 * cols), BF16), "flat"))
        scratch += host.swap.scratch
    flops = 10 * q.shape[0] * keys * q.shape[1]
    return attention_call(
        backward_kernel, biased, tiles, outs, scratch, (q, k, v, o, do, lse, mask, extra), name,
        flops, host,
    )


def inverse_rms(state):
    return lax.rsqrt(jnp.mean(state * state, axis=-1, keepdims=True) + EPSILON)


def norm_back(state, gain, grad_normed):
    scale = inverse_rms(state)
    weighted = grad_normed * gain
    grad_gain = jnp.sum(grad_normed * state * scale, axis=0, keepdims=True)
    inner = jnp.mean(weighted * state, axis=-1, keepdims=True)
    return scale * weighted - state * (scale * scale * scale) * inner, grad_gain


def row_chunk(rows):
    for size in (272, 256, 128):
        if rows % size == 0:
            return size
    return rows


def full(array):
    return pl.BlockSpec(array.shape, lambda j, w: (0,) * len(array.shape))


def lead_block(array):
    return pl.BlockSpec((1,) + array.shape[1:], lambda j, w: (j,) + (0,) * (len(array.shape) - 1))


def col_block(array, parts):
    return pl.BlockSpec((array.shape[0], array.shape[1] // parts), lambda j, w: (0, j))


def row_block(array, parts):
    return pl.BlockSpec((array.shape[0] // parts, array.shape[1]), lambda j, w: (j, 0))


def kernel_call(body, name, steps, where, ins, outs, scratch, flops):
    return pl.pallas_call(
        lambda _, *refs: body(*refs),
        out_shape=[jax.ShapeDtypeStruct(a.shape, a.dtype) for a, _ in outs],
        grid_spec=pltpu.PrefetchScalarGridSpec(
            num_scalar_prefetch=1,
            grid=(steps,),
            in_specs=[s for _, s in ins],
            out_specs=[s for _, s in outs],
            scratch_shapes=scratch,
        ),
        compiler_params=pltpu.CompilerParams(vmem_limit_bytes=60 << 20),
        cost_estimate=pl.CostEstimate(flops=flops, bytes_accessed=16 << 20, transcendentals=0),
        name=name,
    )(where, *[a for a, _ in ins])


def my_rows(array):
    block = (None, array.shape[1], None) + array.shape[3:]
    return array, pl.BlockSpec(block, lambda j, w: (w[0], 0, w[1], 0, 0))


def my_sequence(array):
    return array, pl.BlockSpec((None,) + array.shape[1:], lambda j, w: (w[0], 0, 0))


def flat(ref):
    return ref.reshape(ref.shape[0] * ref.shape[1], ref.shape[2])


def shape(dims, dtype=BF16):
    return jax.ShapeDtypeStruct(dims, dtype)


def project_kernel(x_ref, own_ref, gain_ref, w_ref, q_ref, k_ref, v_ref, n_ref, normed):
    length = x_ref.shape[0]
    qcols = q_ref.shape[1]
    kcols = k_ref.shape[1]
    size = row_chunk(length)

    @pl.when(pl.program_id(0) == 0)
    def _():
        def norm_rows(at):
            x = x_ref[pl.ds(at, size), :].astype(F32)
            normed[pl.ds(at, size), :] = (x * inverse_rms(x) * gain_ref[...]).astype(BF16)

        chunked(length, size, norm_rows)
        x = flat(own_ref)[...].astype(F32)
        n_ref[...] = (x * inverse_rms(x) * gain_ref[...]).astype(BF16)

    q_ref[...] = mm(n_ref[...], w_ref[0, :, :qcols]).astype(BF16)

    def keys(at):
        kv = mm(normed[pl.ds(at, size), :], w_ref[0, :, qcols:]).astype(BF16)
        k_ref[pl.ds(at, size), :] = kv[:, :kcols]
        v_ref[pl.ds(at, size), :] = kv[:, kcols:]

    chunked(length, size, keys)
    k_ref[length:, :] = jnp.zeros((k_ref.shape[0] - length, kcols), BF16)
    v_ref[length:, :] = jnp.zeros((k_ref.shape[0] - length, kcols), BF16)


def self_project(where, x, own, gain, w, reach, rows):
    _, length, width = x.shape
    groups, _, cols = w.shape
    q, k = shape((rows, groups * cols // 2)), shape((reach, groups * cols // 4))
    n = shape((rows, width))
    return kernel_call(
        project_kernel, "self_project", groups, where,
        [my_sequence(x), my_rows(own), (gain, full(gain)), (w, lead_block(w))],
        [(q, col_block(q, groups)), (k, col_block(k, groups)), (k, col_block(k, groups)), (n, full(n))],
        [pltpu.VMEM((length, width), BF16)], (length + rows) * width * groups * cols,
    )


def middle_kernel(o_ref, wo_ref, x_ref, gain_ref, m_ref, w_ref, h_ref, n_ref, q_ref, k_ref, v_ref):
    rows, qcols = q_ref.shape
    kcols = k_ref.shape[1]
    size = row_chunk(rows)
    x_ref = flat(x_ref)

    @pl.when(pl.program_id(0) == 0)
    def _():
        def state(at):
            some = pl.ds(at, size)
            h = x_ref[some, :].astype(F32) + mm(o_ref[some, :], wo_ref[...])
            h_ref[some, :] = h
            n_ref[some, :] = (h * inverse_rms(h) * gain_ref[...]).astype(BF16)

        chunked(rows, size, state)

    q_ref[...] = mm(n_ref[...], w_ref[0, :, :qcols]).astype(BF16)
    kv = mm(m_ref[...], w_ref[0, :, qcols:]).astype(BF16)
    k_ref[...] = kv[:, :kcols]
    v_ref[...] = kv[:, kcols:]


def cross_project(where, o, wo, own, gain, memory, w):
    rows, width = o.shape
    groups, _, cols = w.shape
    h, n = shape((rows, width), F32), shape((rows, width))
    q = shape(o.shape)
    k = shape((memory.shape[1], groups * cols // 4))
    return kernel_call(
        middle_kernel, "cross_project", groups, where,
        [(o, full(o)), (wo, full(wo)), my_rows(own), (gain, full(gain)), my_sequence(memory),
         (w, lead_block(w))],
        [(h, full(h)), (n, full(n)), (q, col_block(q, groups)), (k, col_block(k, groups)),
         (k, col_block(k, groups))],
        [], 6 * rows * width * width,
    )


def gate_parts(value):
    square = value * value
    inner = jnp.tanh(0.7978845608028654 * (value + 0.044715 * square * value))
    half = 0.5 * (1.0 + inner)
    slope = 0.7978845608028654 * (1.0 + 3.0 * 0.044715 * square)
    return value * half, half + 0.5 * value * (1.0 - inner * inner) * slope


def feed_kernel(
    o_ref, wo_ref, h1_ref, gain_ref, up_ref, wg_ref, wu_ref, wd_ref,
    out_ref, g2_ref, gain_out, gwg_ref, gwu_ref, gwd_ref, do_ref, gwo_ref,
    h2, normed, total, back, hidden_s, dgate_s, dup_s,
):
    rows, width = h1_ref.shape
    j = pl.program_id(0)
    size = row_chunk(rows)
    up_ref = flat(up_ref)

    @pl.when(j == 0)
    def _():
        def state(at):
            some = pl.ds(at, size)
            h = h1_ref[some, :] + mm(o_ref[some, :], wo_ref[...])
            h2[some, :] = h
            normed[some, :] = (h * inverse_rms(h) * gain_ref[...]).astype(BF16)
            total[some, :] = h
            back[some, :] = jnp.zeros((size, width), F32)

        chunked(rows, size, state)

    def hidden_rows(at):
        some = pl.ds(at, size)
        n = normed[some, :]
        g = up_ref[some, :]
        gate = mm(n, wg_ref[0])
        up = mm(n, wu_ref[0])
        grad_hidden = mm_nt(g, wd_ref[...])
        active, pull = gate_parts(gate)
        hidden = (active * up).astype(BF16)
        grad_gate = (grad_hidden * up * pull).astype(BF16)
        grad_up = (grad_hidden * active).astype(BF16)
        hidden_s[some, :] = hidden
        dgate_s[some, :] = grad_gate
        dup_s[some, :] = grad_up
        total[some, :] += mm(hidden, wd_ref[...])
        back[some, :] += mm_nt(grad_gate, wg_ref[0]) + mm_nt(grad_up, wu_ref[0])

    chunked(rows, size, hidden_rows)

    def weight_rows(at):
        some = pl.ds(at, 512)
        n = normed[:, some]
        gwg_ref[0, some, :] = mm_tn(n, dgate_s[...]).astype(BF16)
        gwu_ref[0, some, :] = mm_tn(n, dup_s[...]).astype(BF16)
        gwd_ref[:, some] = mm_tn(hidden_s[...], up_ref[:, some]).astype(BF16)

    chunked(width, 512, weight_rows)

    @pl.when(j == pl.num_programs(0) - 1)
    def _():
        gain_out[...] = jnp.zeros_like(gain_out)
        do_ref[...] = jnp.zeros_like(do_ref)

        def finish(at):
            some = pl.ds(at, size)
            out_ref[some, :] = total[some, :].astype(BF16)
            change, grad_gain = norm_back(h2[some, :], gain_ref[...], back[some, :])
            gain_out[...] += grad_gain
            g2 = up_ref[some, :].astype(F32) + change
            g2_ref[some, :] = g2
            low = g2.astype(BF16)
            normed[some, :] = low
            do_ref[some, :] = mm_nt(low, wo_ref[...]).astype(BF16)

        chunked(rows, size, finish)

        def out_rows(at):
            some = pl.ds(at, 512)
            gwo_ref[some, :] = mm_tn(o_ref[0:rows, some], normed[...]).astype(BF16)

        chunked(width, 512, out_rows)


def feed(where, o, wo, h1, gain, upstream, wg, wu, wd):
    rows, width = h1.shape
    groups, _, cols = wg.shape
    out, g2, gg = shape(h1.shape), shape(h1.shape, F32), shape((1, width), F32)
    return kernel_call(
        feed_kernel, "feed", groups, where,
        [(o, full(o)), (wo, full(wo)), (h1, full(h1)), (gain, full(gain)), my_rows(upstream),
         (wg, lead_block(wg)), (wu, lead_block(wu)), (wd, row_block(wd, groups))],
        [(out, full(out)), (g2, full(g2)), (gg, full(gg)), (wg, lead_block(wg)), (wu, lead_block(wu)),
         (wd, row_block(wd, groups)), (o, full(o)), (wo, full(wo))],
        [pltpu.VMEM((rows, width), F32), pltpu.VMEM((rows, width), BF16), pltpu.VMEM((rows, width), F32),
         pltpu.VMEM((rows, width), F32)] + [pltpu.VMEM((rows, cols), BF16)] * 3,
        18 * rows * width * groups * cols,
    )


def back_kernel(
    dq_ref, w_ref, n_ref, h_ref, gain_ref, g2_ref, wo_ref, o_ref,
    gw_ref, g1_ref, gain_out, do_ref, gwo_ref, back, low_s,
):
    rows, width = h_ref.shape
    qcols = dq_ref.shape[1]
    j = pl.program_id(0)
    size = row_chunk(rows)

    @pl.when(j == 0)
    def _():
        back[...] = jnp.zeros_like(back)

    back[...] += mm_nt(dq_ref[0:rows, :], w_ref[0, :, :qcols])

    def weight_rows(at):
        some = pl.ds(at, 512)
        gw_ref[0, some, :] = mm_tn(n_ref[:, some], dq_ref[0:rows, :]).astype(BF16)

    chunked(width, 512, weight_rows)

    @pl.when(j == pl.num_programs(0) - 1)
    def _():
        gain_out[...] = jnp.zeros_like(gain_out)
        do_ref[...] = jnp.zeros_like(do_ref)

        def finish(at):
            some = pl.ds(at, size)
            change, grad_gain = norm_back(h_ref[some, :], gain_ref[...], back[some, :])
            gain_out[...] += grad_gain
            g1 = g2_ref[some, :] + change
            g1_ref[some, :] = g1
            low = g1.astype(BF16)
            low_s[some, :] = low
            do_ref[some, :] = mm_nt(low, wo_ref[...]).astype(BF16)

        chunked(rows, size, finish)

        def out_rows(at):
            some = pl.ds(at, 512)
            gwo_ref[some, :] = mm_tn(o_ref[0:rows, some], low_s[...]).astype(BF16)

        chunked(width, 512, out_rows)


def cross_back(where, dq, w, n, h, gain, g2, wo, o):
    rows, width = h.shape
    groups, _, cols = w.shape
    gw = shape((groups, width, cols // 2))
    gg = shape((1, width), F32)
    return kernel_call(
        back_kernel, "cross_back", groups, where,
        [(dq, col_block(dq, groups)), (w, lead_block(w)), (n, full(n)), (h, full(h)), (gain, full(gain)),
         (g2, full(g2)), (wo, full(wo)), (o, full(o))],
        [(gw, lead_block(gw)), (g2, full(g2)), (gg, full(gg)), (o, full(o)), (wo, full(wo))],
        [pltpu.VMEM((rows, width), F32), pltpu.VMEM((rows, width), BF16)],
        8 * rows * width * width,
    )


def memory_kernel(dk_ref, dv_ref, w_ref, m_ref, gw_ref, gm_ref, back):
    j = pl.program_id(0)
    qcols = w_ref.shape[2] // 2

    @pl.when(j == 0)
    def _():
        back[...] = jnp.zeros_like(back)

    both = jnp.concatenate([dk_ref[...], dv_ref[...]], axis=1)
    back[...] += mm_nt(both, w_ref[0, :, qcols:])
    gw_ref[0] = mm_tn(m_ref[...], both).astype(BF16)

    @pl.when(j == pl.num_programs(0) - 1)
    def _():
        gm_ref[...] = back[...].astype(BF16)


def key_halves(dkv, groups):
    cols = dkv.shape[1] // (2 * groups)
    return [
        (dkv, pl.BlockSpec((dkv.shape[0], cols), lambda j, w: (0, j))),
        (dkv, pl.BlockSpec((dkv.shape[0], cols), lambda j, w: (0, j + groups))),
    ]


def memory_back(where, dkv, w, memory):
    groups, width, cols = w.shape
    gw, gm = shape((groups, width, cols // 2)), shape((dkv.shape[0], width))
    rows = pl.BlockSpec((None,) + gm.shape, lambda j, w: (w[0], w[1], 0))
    return kernel_call(
        memory_kernel, "memory_back", groups, where,
        key_halves(dkv, groups) + [(w, lead_block(w)), (memory, rows)],
        [(gw, lead_block(gw)), (gm, full(gm))],
        [pltpu.VMEM(gm.shape, F32)], 4 * gm.shape[0] * width * width,
    )


def last_kernel(
    dq_ref, dk_ref, dv_ref, w_ref, n_ref, x_ref, gain_ref, g1_ref,
    gwq_ref, gwkv_ref, gx_ref, gain_out, back,
):
    rows, width = g1_ref.shape
    j = pl.program_id(0)
    size = row_chunk(rows)
    x_ref = flat(x_ref)

    @pl.when(j == 0)
    def _():
        back[...] = jnp.zeros_like(back)

    dq = dq_ref[0:rows, :]
    dkv = jnp.concatenate([dk_ref[...], dv_ref[...]], axis=1)
    both = jnp.concatenate([dq, dkv], axis=1)
    back[...] += mm_nt(both, w_ref[0])

    def weight_rows(at):
        some = pl.ds(at, 512)
        gwq_ref[0, some, :] = mm_tn(n_ref[:, some], dq).astype(BF16)
        gwkv_ref[0, some, :] = mm_tn(n_ref[:, some], dkv).astype(BF16)

    chunked(width, 512, weight_rows)

    @pl.when(j == pl.num_programs(0) - 1)
    def _():
        gain_out[...] = jnp.zeros_like(gain_out)

        def finish(at):
            some = pl.ds(at, size)
            change, grad_gain = norm_back(x_ref[some, :].astype(F32), gain_ref[...], back[some, :])
            gain_out[...] += grad_gain
            gx_ref[some, :] = (g1_ref[some, :] + change).astype(BF16)

        chunked(rows, size, finish)


def self_back(where, dq, dkv, w, n, own, gain, g1):
    rows, width = g1.shape
    groups, _, cols = w.shape
    gw = shape((groups, width, cols // 2))
    gx = shape(g1.shape)
    gg = shape((1, width), F32)
    return kernel_call(
        last_kernel, "self_back", groups, where,
        [(dq, col_block(dq, groups))] + key_halves(dkv, groups)
        + [(w, lead_block(w)), (n, full(n)), my_rows(own), (gain, full(gain)), (g1, full(g1))],
        [(gw, lead_block(gw)), (gw, lead_block(gw)), (gx, full(gx)), (gg, full(gg))],
        [pltpu.VMEM((rows, width), F32)],
        8 * rows * width * width,
    )


def gather(shard, dims):
    for axis, name in dims:
        shard = lax.all_gather(shard, name, axis=axis, tiled=True)
    return shard


ROWS_BY_DP = ((0, "dp"), (1, "mp"))
ROWS_BY_MP = ((1, "dp"), (0, "mp"))


def scatter(grad, dims):
    for axis, name in dims:
        grad = lax.psum_scatter(grad, name, scatter_dimension=axis, tiled=True)
    return grad.astype(F32)


def grouped(weight, groups):
    rows, cols = weight.shape
    return weight.reshape(rows, groups, cols // groups).transpose(1, 0, 2)


def ungrouped(weight):
    groups, rows, cols = weight.shape
    return weight.transpose(1, 0, 2).reshape(rows, groups * cols)


def body(
    inputs,
    encoded,
    decoder_segments,
    encoder_segments,
    buckets,
    self_gain,
    self_query,
    self_key,
    self_value,
    self_out,
    position_bias,
    cross_gain,
    cross_query,
    cross_key,
    cross_value,
    cross_out,
    feed_gain,
    feed_gate,
    feed_up,
    feed_down,
    cotangent,
    *,
    dp,
    mp,
):
    batches, length, width = inputs.shape
    enc_length = encoded.shape[1]
    parts = mp // batches
    rows = length // parts
    tiles = Tiles(rows, length, parts)
    place = lax.axis_index("mp")
    sequence = place // parts
    part = place % parts
    where = jnp.stack([sequence, part]).astype(jnp.int32)
    groups = self_key.shape[1] * mp // (2 * HEAD_DIM)
    native = mp == groups and dp == 8 and parts == 2

    if native:
        order = ["by_dp", "by_mp"]
        size = width // dp
        gains = jnp.stack([self_gain, cross_gain, feed_gain])
        little = jnp.pad(position_bias.reshape(1, -1), ((0, 0), (0, size - position_bias.size)))
        little = jnp.pad(jnp.concatenate([gains, little]), ((0, 12), (0, 0)))
        w1 = jnp.concatenate([self_query, self_key, self_value], axis=1)
        w2 = jnp.concatenate([cross_query, cross_key, cross_value], axis=1)
        w1, little, wo1 = Transfers(
            dp, mp, 1, [w1, little, self_out], ["by_dp"] + order
        ).run("gather_self")
        gains = little[0, :, :3].transpose(1, 0, 2).reshape(3, 1, width).astype(F32)
        table = little[:, :, 3, : position_bias.size].reshape((mp, dp) + position_bias.shape)
        table = table.transpose(1, 2, 0, 3).reshape(dp * position_bias.shape[0], -1).astype(F32)
        w1 = w1.reshape(mp, width, w1.shape[3])
    else:
        gains = [gather(g, ((0, "dp"),)).astype(F32)[None] for g in (self_gain, cross_gain, feed_gain)]
        table = gather(position_bias, ROWS_BY_DP).astype(F32)

        def blocks(*shards):
            return jnp.concatenate([grouped(gather(s, ROWS_BY_DP), groups) for s in shards], axis=2)

        w1 = blocks(self_query, self_key, self_value)
        w2 = blocks(cross_query, cross_key, cross_value)
        wg, wu = blocks(feed_gate), blocks(feed_up)
        wo1, wo2, wd = (gather(s, ROWS_BY_MP) for s in (self_out, cross_out, feed_down))
    gain_one, gain_two, gain_three = gains

    def cut(array):
        return array.reshape((array.shape[0], length // 64, parts, 64 // parts) + array.shape[2:])

    own_inputs = cut(inputs)
    docs = lax.dynamic_index_in_dim(decoder_segments, sequence, keepdims=False)
    enc_docs = lax.dynamic_index_in_dim(encoder_segments, sequence, keepdims=False)
    own_docs = lax.dynamic_slice_in_dim(docs.reshape(length // 64, 64), part * tiles.blk, tiles.blk, axis=1)
    own_docs = own_docs.reshape(rows)

    kinds = jnp.arange(4, dtype=jnp.int32)
    before = jnp.sum((docs[None, :] < kinds[:, None]).astype(jnp.int32), axis=1)
    is_doc = (own_docs[:, None] == kinds[None, :]).astype(jnp.int32)
    start = jnp.sum(is_doc * before[None, :], axis=1)

    def by_tile(row):
        found = []
        for at, n in tiles.list:
            piece = jnp.tile(row[at : at + n], 4)
            found.append(jnp.pad(piece, (0, 4 * (TILE_Q - n))))
        return jnp.stack(found)

    mask_one = by_tile(start)
    mask_two = by_tile(own_docs)
    keys_two = jnp.broadcast_to(enc_docs[:, None], (enc_length, TILE_Q))
    onehot = (buckets[:, None] == jnp.arange(table.shape[0], dtype=jnp.int32)).astype(F32)
    by_distance = dot(table, onehot, ((0,), (1,)), HIGHEST)
    heads = by_distance.shape[0]
    vec = jnp.pad(by_distance, ((0, 0), (0, tiles.width)))
    vec = jnp.concatenate([jnp.full((heads, tiles.lead), NEGATIVE, F32), vec], axis=1)
    vec = lax.dynamic_slice_in_dim(vec, part * tiles.blk, tiles.width, axis=1)
    vec = vec.reshape(heads // 4, 4, tiles.width)

    q1, k1, v1, n1 = self_project(where, inputs, own_inputs, gain_one, w1, tiles.reach, rows)
    hosts = [None] * 4
    if native:
        hosts[0] = Transfers(dp, mp, 2, [w2, cross_out, feed_gate], order + ["by_dp"])
        hosts[1] = Transfers(dp, mp, 3, [feed_up, feed_down], order)
    (o1, lse_one), found = attend_forward(
        q1, k1, v1, mask_one, vec, tiles, True, "self_forward", hosts[0]
    )
    if native:
        w2, wo2, wg = found
        w2, wg = (w.reshape(mp, width, w.shape[3]) for w in (w2, wg))
    h1, n2, q2, k2, v2 = cross_project(where, o1, wo1, own_inputs, gain_two, encoded, w2)
    (o2, lse_two), found = attend_forward(
        q2, k2, v2, mask_two, keys_two, tiles, False, "cross_forward", hosts[1]
    )
    if native:
        wu, wd = found
        wu = wu.reshape(mp, width, wu.shape[3])

    result, grad_two, grad_gain_three, gwg, gwu, gwd, do2, gwo2 = feed(
        where, o2, wo2, h1, gain_three, cut(cotangent), wg, wu, wd
    )

    def collect(array):
        array = lax.all_gather(array, "mp", axis=0, tiled=True)
        array = array.reshape(batches, parts, length // 64, tiles.blk, width)
        return array.transpose(0, 2, 1, 3, 4).reshape(batches, length, width)

    def pieces(grad):
        return grad.reshape(grad.shape[0], dp, grad.shape[1] // dp, grad.shape[2])

    sharing = [[s * parts + p for p in range(parts)] for s in range(batches)]

    def share(dk, dv, count):
        both = jnp.concatenate([dk, dv], axis=1)
        both = both.reshape(count, parts, -1, both.shape[1]).transpose(1, 0, 2, 3)
        both = both.reshape(-1, both.shape[3])
        return lax.psum_scatter(
            both, "mp", scatter_dimension=0, axis_index_groups=sharing, tiled=True
        )

    if native:
        hosts[2] = Transfers(
            dp, mp, 4, grads=[gwd], rows=[result.reshape(length // 64, tiles.blk, width)],
            spread=[(batches, length // 64, parts, tiles.blk, width)],
        )
        hosts[2].swap = Exchange(1, enc_length // 2, groups)
    (dq2, *dkv2), sums_down = attend_backward(
        q2, k2, v2, o2, do2, lse_two, mask_two, keys_two, tiles, False, "cross_backward", hosts[2]
    )
    if native:
        dkv2 = dkv2[0]
        *sums_down, outputs = sums_down
        outputs = outputs.reshape(inputs.shape)
    else:
        dkv2 = share(dkv2[1], dkv2[0], 1)
        outputs = collect(result)
    gwq2, grad_one, grad_gain_two, do1, gwo1 = cross_back(
        where, dq2, w2, n2, h1, gain_two, grad_two, wo1, o1
    )
    gwkv2, grad_memory = memory_back(where, dkv2, w2, encoded)

    if native:
        line = grad_memory.reshape(1, -1, width)
        hosts[3] = Transfers(
            dp, mp, 5, grads=[pieces(gwg), pieces(gwu)], rows=[line],
            spread=[(batches, 1, parts, enc_length // parts, width)],
        )
        hosts[3].swap = Exchange(length // 64, tiles.blk, groups)
    (dq1, slopes, *dkv1), sums_feed = attend_backward(
        q1, k1, v1, o1, do1, lse_one, mask_one, vec, tiles, True, "self_backward", hosts[3]
    )
    if native:
        dkv1 = dkv1[0]
        *sums_feed, grad_encoded = sums_feed
        grad_encoded = grad_encoded.reshape(encoded.shape)
    else:
        dkv1 = share(dkv1[1][:length], dkv1[0][:length], length // 64)
        grad_encoded = lax.all_gather(grad_memory, "mp", axis=0, tiled=True).reshape(encoded.shape)
    gwq1, gwkv1, grad_rows, grad_gain_one = self_back(
        where, dq1, dkv1, w1, n1, own_inputs, gain_one, grad_one
    )
    slopes = slopes.reshape(heads, tiles.width)
    slopes = jnp.pad(slopes, ((0, 0), (64, length)))
    slopes = lax.dynamic_slice_in_dim(slopes, 64 + tiles.lead - part * tiles.blk, length, axis=1)
    grad_table = dot(onehot, slopes, ((0,), (1,)), HIGHEST)
    grad_gains = jnp.concatenate([grad_gain_one, grad_gain_two, grad_gain_three])

    kcols = gwkv1.shape[2] // 2
    if native:
        little = grad_gains.reshape(3, dp, size).transpose(1, 0, 2)
        little = jnp.broadcast_to(little[None], (mp, dp, 3, size))
        spots = grad_table.reshape(dp, position_bias.shape[0], mp, position_bias.shape[1])
        spots = spots.transpose(2, 0, 1, 3).reshape(mp, dp, 1, position_bias.size)
        spots = jnp.pad(spots, ((0, 0), (0, 0), (0, 4), (0, size - position_bias.size)))
        little = jnp.concatenate([little, spots], axis=2)
        grads = [pieces(g) for g in (gwq2, gwkv2, gwq1, gwkv1)] + [gwo2, gwo1, little]
        *sums, little, grad_inputs = Transfers(
            dp, mp, 6, grads=grads, rows=[grad_rows.reshape(length // 64, tiles.blk, width)],
            spread=[(batches, length // 64, parts, tiles.blk, width)],
        ).run("scatter_rest")
        grad_inputs = grad_inputs.reshape(inputs.shape)
        sums = sums + list(sums_feed) + list(sums_down)
        gwq2, gwkv2, gwq1, gwkv1, gwo2, gwo1, gwg, gwu, gwd = sums
        gwk2, gwv2, gwk1, gwv1 = (
            g[:, at : at + kcols] for g in (gwkv2, gwkv1) for at in (0, kcols)
        )
        grad_gains = [little[n] for n in range(3)]
        grad_table = little[3, : position_bias.size].reshape(position_bias.shape)
    else:
        grad_inputs = collect(grad_rows)

        def summed(grad):
            return scatter(ungrouped(grad), ROWS_BY_DP)

        gwk1, gwv1 = summed(gwkv1[:, :, :kcols]), summed(gwkv1[:, :, kcols:])
        gwk2, gwv2 = summed(gwkv2[:, :, :kcols]), summed(gwkv2[:, :, kcols:])
        gwq1, gwq2, gwg, gwu = (summed(g) for g in (gwq1, gwq2, gwg, gwu))
        gwo1, gwo2, gwd = (scatter(g, ROWS_BY_MP) for g in (gwo1, gwo2, gwd))
        small = jnp.concatenate([grad_gains.reshape(-1), grad_table.reshape(-1)])
        small = lax.psum(small, ("dp", "mp"))
        data = lax.axis_index("dp")
        grad_gains = lax.dynamic_slice_in_dim(
            small[: 3 * width].reshape(3, dp, width // dp), data, 1, axis=1
        )
        grad_gains = [grad_gains[n, 0] for n in range(3)]
        grad_table = lax.dynamic_slice(
            small[3 * width :].reshape(table.shape),
            (data * position_bias.shape[0], place * position_bias.shape[1]),
            position_bias.shape,
        )

    return (
        outputs, grad_inputs, grad_encoded,
        grad_gains[0], gwq1, gwk1, gwv1, gwo1, grad_table,
        grad_gains[1], gwq2, gwk2, gwv2, gwo2,
        grad_gains[2], gwg, gwu, gwd,
    )


def solution(mesh):
    rows3 = P("dp", None, None)
    by_dp = P("dp", "mp")
    by_mp = P("mp", "dp")
    gain = P("dp")
    return jax.shard_map(
        functools.partial(body, dp=mesh.shape["dp"], mp=mesh.shape["mp"]),
        mesh=mesh,
        in_specs=(
            rows3, rows3, P("dp", None), P("dp", None), P(),
            gain, by_dp, by_dp, by_dp, by_mp, by_dp,
            gain, by_dp, by_dp, by_dp, by_mp,
            gain, by_dp, by_dp, by_mp, rows3,
        ),
        out_specs=(
            rows3, rows3, rows3,
            gain, by_dp, by_dp, by_dp, by_mp, by_dp,
            gain, by_dp, by_dp, by_dp, by_mp,
            gain, by_dp, by_dp, by_mp,
        ),
        check_vma=False,
    )
```

time: 835 us -> 693 us (0.83)
  waiting for transfers between devices: 135 us -> 0 us
  Pallas kernels: 618 us -> 650 us
  local copies, waits for them, and re-layouts: 44.9 us -> 30.4 us
  between operations: 14.4 us -> 1.25 us
    all_gather x3 -> x0, waiting for transfers between devices: 114 us -> none  [the longest x1 85.5 us: body(): lax.all_gather(grad_rows, 'mp', axis=0, tiled=True).reshape(inputs.shape)]
    pallas_call x2, Pallas kernels: 130 us -> 168 us  [run(): pl.pallas_call(kernel, grid=(1,), out_shape=self.outs, in_specs=self.in_s...]
    reduce_scatter x2 -> x0, waiting for transfers between devices: 21.1 us -> none  [share(): lax.psum_scatter(array, 'mp', scatter_dimension=0, axis_index_groups=shar...]
    unnamed x58 -> x44, local copies, waits for them, and re-layouts: 16.4 us -> 18.1 us
  transfers between devices with their start and end apart: 5 -> 0, of which waited for: 3 -> 0; matrix products, arithmetic and copies ran while one was open for 2% -> 0% of each run, Pallas kernels for 30% -> 0%
where the time goes in v3:
time: 693 us; the launch traced here: 689 us
  Pallas kernels  650 us (94%)
  local copies, waits for them, and re-layouts  30.4 us (4%)
    pallas_call x4, Pallas kernels, attention_call(): pl.pallas_call(functools.partial(kernel, biased, tiles, host), grid=(step...  364 us
    pallas_call x2, Pallas kernels, run(): pl.pallas_call(kernel, grid=(1,), out_shape=self.outs, in_specs=self.in_s...  168 us
    pallas_call x6, Pallas kernels, kernel_call(): pl.pallas_call(lambda _, *refs: body(*refs), out_shape=[jax.ShapeDtypeStr...  117 us
    unnamed x44, local copies, waits for them, and re-layouts  18.1 us

profile of v3, /device:TPU:8, one launch (start us, length us, event | category | flops | bytes accessed | tf_op | source)
XLA Modules:
  0.0 688.8 jit_solution(12395754654366210792)
XLA Ops:
  6.5 1.5 pad_maximum_fusion.refs_0_
  8.1 1.5 pad_maximum_fusion.1.refs_5_
  9.6 1.7 copy.56.refs_7_
  11.4 1.7 copy.57.refs_5_
  13.9 39.2 %gather_self.1 = (bf16[4,8,128,512]{3,2,1,0:T(8,128)(2,1)}, bf16[4,8,16,128]{3,2,1,0:T(8,128)(2,1)}, bf16[1024,1024]{1,0:T(8,128)(2,1)}) custom-call(bf16[128,512]{1,0:T(8,128)(2,1)} %pad_maximum_fusion.refs_0_, bf16[16,128]{1,0:T(8,128)(2,1)} %pad.29.refs_1_, bf16[256,128]{1,0:T(8,128)(2,1)} %refs_2_.1), custom_call_target="tpu_custom_call" | custom-call | tf_op jit(solution)/shard_map/gather_self/pallas_call | solution.py:506
  53.2 0.9 slice.74
  56.9 13.0 %self_project.1 = (bf16[544,1024]{1,0:T(8,128)(2,1)}, bf16[1280,512]{1,0:T(8,128)(2,1)}, bf16[1280,512]{1,0:T(8,128)(2,1)}, bf16[544,1024]{1,0:T(8,128)(2,1)}) custom-call(s32[2]{0:T(128)} %pad_add_fusion._, bf16[2,1088,1024]{2,1,0:T(8,128)(2,1)} %refs_0_.1, bf16[2,17,2,32,1024]{4,3,2,1,0:T(8,128)(2,1)} %bitcast.69, ...), custom_call_target="tpu_custom_call" | custom-call | flops 3422552064 | bytes 16777216 | tf_op jit(solution)/shard_map/self_project/pallas_call | solution.py:907
  69.9 78.2 %self_forward.1 = (bf16[544,1024]{1,0:T(8,128)(2,1)}, f32[4,5,512]{2,1,0:T(8,128)}, bf16[4,8,128,512]{3,2,1,0:T(8,128)(2,1)}, bf16[1024,1024]{1,0:T(8,128)(2,1)}, bf16[4,8,128,704]{3,2,1,0:T(8,128)(2,1)}) custom-call(bf16[544,1024]{1,0:T(8,128)(2,1)} %get-tuple-element.78.refs_0_, bf16[1280,512]{1,0:T(8,128)(2,1)} %get-tuple-element.79.refs_1_, ...), custom_call_target="tpu_custom_call" | custom-call | flops 2852126720 | bytes 16777216 | tf_op jit(solution)/shard_map/self_forward/pallas_call | solution.py:810
  148.1 10.3 %cross_project.1 = (f32[544,1024]{1,0:T(8,128)}, bf16[544,1024]{1,0:T(8,128)(2,1)}, bf16[544,1024]{1,0:T(8,128)(2,1)}, bf16[512,512]{1,0:T(8,128)(2,1)}, bf16[512,512]{1,0:T(8,128)(2,1)}) custom-call(s32[2]{0:T(128)} %pad_add_fusion._, bf16[544,1024]{1,0:T(8,128)(2,1)} %get-tuple-element.81.refs_0_.refs_7_.refs_3_, ...), custom_call_target="tpu_custom_call" | custom-call | flops 3422552064 | bytes 16777216 | tf_op jit(solution)/shard_map/cross_project/pallas_call | solution.py:907
  158.4 67.8 %cross_forward.1 = (bf16[544,1024]{1,0:T(8,128)(2,1)}, f32[4,5,512]{2,1,0:T(8,128)}, bf16[4,8,128,704]{3,2,1,0:T(8,128)(2,1)}, bf16[2816,1024]{1,0:T(8,128)(2,1)}) custom-call(bf16[544,1024]{1,0:T(8,128)(2,1)} %get-tuple-element.84.refs_0_, bf16[512,512]{1,0:T(8,128)(2,1)} %get-tuple-element.85.refs_1_, bf16[512,512]{1,0:T(8,128)(2,1)} %get-tuple-element.86.refs_2_, ...), custom_call_target="tpu_custom_call" | custom-call | flops 1140850688 | bytes 16777216 | tf_op jit(solution)/shard_map/cross_forward/pallas_call | solution.py:810
  226.2 55.2 %feed.1 = (bf16[544,1024]{1,0:T(8,128)(2,1)}, f32[544,1024]{1,0:T(8,128)}, f32[1,1024]{1,0:T(1,128)}, bf16[4,1024,704]{2,1,0:T(8,128)(2,1)}, bf16[4,1024,704]{2,...) custom-call(s32[2]{0:T(128)} %pad_add_fusion._, ...), custom_call_target="tpu_custom_call" | custom-call | flops 28236054528 | bytes 16777216 | tf_op jit(solution)/shard_map/feed/pallas_call | solution.py:907
  281.5 114.7 %cross_backward.1 = (bf16[544,1024]{1,0:T(8,128)(2,1)}, bf16[256,1024]{1,0:T(8,128)(2,1)}, f32[704,128]{1,0:T(8,128)}, bf16[2,17,2,32,1024]{4,3,2,1,0:T(8,128)(2,1)}) custom-call(bf16[544,1024]{1,0:T(8,128)(2,1)} %get-tuple-element.84.refs_0_, bf16[512,512]{1,0:T(8,128)(2,1)} %get-tuple-element.85.refs_1_, bf16[512,512]{1,0:T(8,128)(2,1)} %get-tuple-element.86.refs_2_, ...), custom_call_target="tpu_custom_call" | custom-call | flops 2852126720 | bytes 16777216 | tf_op jit(solution)/shard_map/cross_backward/pallas_call | solution.py:810
  396.1 17.6 %cross_back.1 = (bf16[4,1024,256]{2,1,0:T(8,128)(2,1)}, f32[544,1024]{1,0:T(8,128)}, f32[1,1024]{1,0:T(1,128)}, bf16[544,1024]{1,0:T(8,128)(2,1)}, bf16[1024,1024]{1,0:T(8,128)(2,1)}) custom-call(s32[2]{0:T(128)} %pad_add_fusion._, bf16[544,1024]{1,0:T(8,128)(2,1)} %get-tuple-element.98.refs_0_, bf16[4,1024,512]{2,1,0:T(8,128)(2,1)} %bitcast.73, ...), custom_call_target="tpu_custom_call" | custom-call | flops 4563402752 | bytes 16777216 | tf_op jit(solution)/shard_map/cross_back/pallas_call | solution.py:907
  413.8 6.3 memory_back.1
  420.1 103.6 %self_backward.1 = (bf16[544,1024]{1,0:T(8,128)(2,1)}, f32[4,4,1536]{2,1,0:T(4,128)}, bf16[544,1024]{1,0:T(8,128)(2,1)}, f32[128,704]{1,0:T(8,128)}, f32[128,704...) custom-call(bf16[544,1024]{1,0:T(8,128)(2,1)} %get-tuple-element.78.refs_0_, bf16[1280,512]{1,0:T(8,128)(2,1)} %get-tuple-element.79.refs_1_, ...), custom_call_target="tpu_custom_call" | custom-call | flops 7130316800 | bytes 16777216 | tf_op jit(solution)/shard_map/self_backward/pallas_call | solution.py:810
  523.8 15.0 %self_back.1 = (bf16[4,1024,256]{2,1,0:T(8,128)(2,1)}, bf16[4,1024,256]{2,1,0:T(8,128)(2,1)}, bf16[544,1024]{1,0:T(8,128)(2,1)}, f32[1,1024]{1,0:T(1,128)}) custom-call(s32[2]{0:T(128)} %pad_add_fusion._, bf16[544,1024]{1,0:T(8,128)(2,1)} %get-tuple-element.109.refs_0_, bf16[544,1024]{1,0:T(8,128)(2,1)} %get-tuple-element.110.refs_1_.refs_2_, ...), custom_call_target="tpu_custom_call" | custom-call | flops 4563402752 | bytes 16777216 | tf_op jit(solution)/shard_map/self_back/pallas_call | solution.py:907
  541.0 128.6 %scatter_rest.1 = (f32[128,256]{1,0:T(8,128)}, f32[128,256]{1,0:T(8,128)}, f32[128,256]{1,0:T(8,128)}, f32[128,256]{1,0:T(8,128)}, f32[256,128]{1,0:T(8,128)}, /...) custom-call(bf16[4,8,128,256]{3,2,1,0:T(8,128)(2,1)} %bitcast.82, ...), custom_call_target="tpu_custom_call" | custom-call | tf_op jit(solution)/shard_map/scatter_rest/pallas_call | solution.py:506
  670.3 1.3 slice_bitcast_fusion.3
  672.3 1.6 fusion.9
  673.9 0.9 copy.61
  674.8 0.9 copy.62
  675.7 5.0 copy.71
  680.8 2.2 copy.72
  683.8 1.3 copy.73
  (92 shorter events, 17.2 us)
Async XLA Ops:
  0.7 3.4 copy-start
  0.7 55.1 %copy-start.13 = (s32[1088]{0:T(1024)S(1)}, s32[1088]{0:T(1024)}, u32[]{:S(2)}) copy-start(s32[1088]{0:T(1024)} %param.25) | copy-start | bytes 13060
  523.7 15.0 %copy-start.11 = (f32[1,1024]{1,0:T(1,128)S(1)}, f32[1,1024]{1,0:T(1,128)}, u32[]{:S(2)}) copy-start(f32[1,1024]{1,0:T(1,128)} %get-tuple-element.119) | copy-start | bytes 12292
  523.7 15.0 %copy-start.12 = (f32[1,1024]{1,0:T(1,128)S(1)}, f32[1,1024]{1,0:T(1,128)}, u32[]{:S(2)}) copy-start(f32[1,1024]{1,0:T(1,128)} %get-tuple-element.118) | copy-start | bytes 12292
  523.8 15.7 %copy-start.10 = (f32[4,4,1536]{2,1,0:T(4,128)S(1)}, f32[4,4,1536]{2,1,0:T(4,128)}, u32[]{:S(2)}) copy-start(f32[4,4,1536]{2,1,0:T(4,128)} %get-tuple-element.120) | copy-start | bytes 294916
  541.0 132.9 %copy-start.4 = (f32[128,704]{1,0:T(8,128)S(1)}, f32[128,704]{1,0:T(8,128)}, u32[]{:S(2)}) copy-start(f32[128,704]{1,0:T(8,128)} %get-tuple-element.185) | copy-start | bytes 1081348
  541.0 133.8 %copy-start.3 = (f32[128,704]{1,0:T(8,128)S(1)}, f32[128,704]{1,0:T(8,128)}, u32[]{:S(2)}) copy-start(f32[128,704]{1,0:T(8,128)} %get-tuple-element.186) | copy-start | bytes 1081348
  674.8 5.9 slice-start
  675.7 5.0 slice-start.1
  680.7 3.1 copy-start.2
  680.7 7.8 %copy-start.1 = (s32[2,1088]{1,0:T(2,128)S(1)}, s32[2,1088]{1,0:T(2,128)}, u32[]{:S(2)}) copy-start(s32[2,1088]{1,0:T(2,128)} %param.23) | copy-start | bytes 26116
  683.8 1.3 copy-start.9
  683.8 2.0 copy-start.8
  683.8 2.7 copy-start.7
  683.8 3.3 copy-start.6
  683.8 4.0 copy-start.5

commit v4 on v3

--- a/solution.py
+++ b/solution.py
@@ -77,18 +77,28 @@
     pl.semaphore_wait(barrier, 3 + mp - 1)
 
 
-def all_slots(mp):
-    return [(0, 0)] + [(d, s) for d in range(1, mp) for s in (0, 1)]
-
-
-def for_slot(place, slot, run):
-    d, side = slot
-    if d == 0:
-        run(place.z)
-    elif side == 0:
-        pl.when(place.z >= d)(lambda: run(place.z - d))
+def nearest(z):
+    upper = lax.div(z, 2)
+    return [z, z + 1 - 2 * lax.rem(z, 2), 2 - upper, 3 - 3 * upper]
+
+
+def onward(place, z2, act):
+    z = place.z
+    if z2 is z:
+        pl.when(z < place.mp - 1)(lambda: act(True))
+        pl.when(z > 0)(lambda: act(False))
     else:
-        pl.when(place.z < place.mp - d)(lambda: run(place.z + d))
+        pl.when(jnp.logical_and(z2 < z, z < place.mp - 1))(lambda: act(True))
+        pl.when(jnp.logical_and(z2 > z, z > 0))(lambda: act(False))
+
+
+def staggered(slots, stages):
+    def step(k):
+        for late, stage in enumerate(stages):
+            if 0 <= k - late < len(slots):
+                stage(slots[k - late])
+
+    return [functools.partial(step, k) for k in range(len(slots) + len(stages) - 1)]
 
 
 def region(ref, i, z, shard):
@@ -117,28 +127,23 @@
         second = place.iy + odd * (place.ix - place.iy)
         return odd, first, second
 
-    slots = all_slots(mp)
-
-    def stage1(slot):
-        d, s = slot
-
-        def run(z2):
-            for u in units:
-                src = shards[u] if d == 0 else None
-                if d > 0:
-                    copy(u, s, i, z2, (i, z)).wait_recv()
-                copy(u, 2, i, z2, (place.ix, z), src).start()
-                copy(u, 3, i, z2, (place.iy, z), src).start()
-                copy(u, 5, i, z2, (place.ic, z), src).start()
-                if d == 0:
-                    pltpu.make_async_copy(shards[u], here(u, i, z), local.at[u]).start()
-
-        for_slot(place, slot, run)
+    slots = nearest(z)
+
+    def stage1(z2):
+        for u in units:
+            src = shards[u] if z2 is z else None
+            if z2 is not z:
+                copy(u, 0, i, z2, (i, z)).wait_recv()
+            copy(u, 2, i, z2, (place.ix, z), src).start()
+            copy(u, 3, i, z2, (place.iy, z), src).start()
+            copy(u, 5, i, z2, (place.ic, z), src).start()
+            if z2 is z:
+                pltpu.make_async_copy(shards[u], here(u, i, z), local.at[u]).start()
 
     def along(u, d, up):
         return pltpu.make_async_remote_copy(
             src_ref=shards[u], dst_ref=here(u, i, z), send_sem=send.at[u, 0 if up else 1, d],
-            recv_sem=recv.at[u, 0 if up else 1, z], device_id=(i, z + d if up else z - d),
+            recv_sem=recv.at[u, 0, z], device_id=(i, z + d if up else z - d),
             device_id_type=MESH)
 
     def depart():
@@ -147,65 +152,45 @@
                 pl.when(z < mp - d)(lambda u=u, d=d: along(u, d, True).start())
                 pl.when(z >= d)(lambda u=u, d=d: along(u, d, False).start())
 
-    def stage2(slot):
-        def run(z2):
-            for u in units:
-                odd, first, second = route(u, z2)
-                kind = 2 + odd
-                spot = here(u, first, z2)
-                pltpu.make_async_remote_copy(src_ref=spot, dst_ref=spot, send_sem=send.at[u, kind, z2],
-                    recv_sem=recv.at[u, kind, z2], device_id=(first, z), device_id_type=MESH).wait_recv()
-                copy(u, 4, first, z2, (second, z)).start()
-                copy(u, 6, first, z2, (place.ic, z)).start()
-
-        for_slot(place, slot, run)
-
-    def stage3(slot):
-        def run(z2):
-            for u in units:
-                odd, first, second = route(u, z2)
-                kind = 3 - odd
-                spot = here(u, second, z2)
-                pltpu.make_async_remote_copy(src_ref=spot, dst_ref=spot, send_sem=send.at[u, kind, z2],
-                    recv_sem=recv.at[u, kind, z2], device_id=(second, z), device_id_type=MESH).wait_recv()
-                copy(u, 7, second, z2, (place.ic, z)).start()
-                copy(u, 4, place.ixy, z2, (second, z)).wait_recv()
-                copy(u, 8, place.ixy, z2, (place.ic, z)).start()
-
-        for_slot(place, slot, run)
+    def stage2(z2):
+        for u in units:
+            odd, first, second = route(u, z2)
+            arrived(u, 2 + odd, first, z2)
+            copy(u, 4, first, z2, (second, z)).start()
+            copy(u, 6, first, z2, (place.ic, z)).start()
+
+    def stage3(z2):
+        for u in units:
+            odd, first, second = route(u, z2)
+            arrived(u, 3 - odd, second, z2)
+            copy(u, 7, second, z2, (place.ic, z)).start()
+            copy(u, 4, place.ixy, z2, (second, z)).wait_recv()
+            copy(u, 8, place.ixy, z2, (place.ic, z)).start()
+
+    def arrived(u, kind, i2, z2):
+        spot = here(u, i2, z2)
+        pltpu.make_async_remote_copy(
+            src_ref=spot, dst_ref=spot, send_sem=send.at[u, kind, z2], recv_sem=recv.at[u, kind, z2],
+            device_id=(i2, z), device_id_type=MESH).wait_recv()
 
     def other(i2):
         return i2 + place.ic - i
 
-    def finish(slot):
-        d, s = slot
-
-        def run(z2):
-            for u in units:
-                odd, first, second = route(u, z2)
-                for kind, i2 in ((5, i), (6, first), (7, second), (8, place.ixy)):
-                    copy(u, kind, other(i2), z2, (place.ic, z)).wait_recv()
-                if d == 0:
-                    for far in range(1, mp):
-                        pl.when(z < mp - far)(lambda u=u, far=far: along(u, far, True).wait_send())
-                        pl.when(z >= far)(lambda u=u, far=far: along(u, far, False).wait_send())
-                for kind in range(2, 9):
-                    copy(u, kind, i, z2, (i, z)).wait_send()
-                if d == 0:
-                    pltpu.make_async_copy(shards[u], here(u, i, z), local.at[u]).wait()
-
-        for_slot(place, slot, run)
-
-    steps = [depart]
-    n = len(slots)
-    for k in range(n + 2):
-        if k < n:
-            steps.append(functools.partial(stage1, slots[k]))
-        if 0 <= k - 1 < n:
-            steps.append(functools.partial(stage2, slots[k - 1]))
-        if 0 <= k - 2 < n:
-            steps.append(functools.partial(stage3, slots[k - 2]))
-    return steps, [functools.partial(finish, slot) for slot in slots]
+    def finish(z2):
+        for u in units:
+            odd, first, second = route(u, z2)
+            for kind, i2 in ((5, i), (6, first), (7, second), (8, place.ixy)):
+                copy(u, kind, other(i2), z2, (place.ic, z)).wait_recv()
+            for kind in range(2, 9):
+                copy(u, kind, i, z2, (i, z)).wait_send()
+            if z2 is z:
+                for far in range(1, mp):
+                    pl.when(z < mp - far)(lambda u=u, far=far: along(u, far, True).wait_send())
+                    pl.when(z >= far)(lambda u=u, far=far: along(u, far, False).wait_send())
+                pltpu.make_async_copy(shards[u], here(u, i, z), local.at[u]).wait()
+
+    steps = staggered(slots, (stage1, stage2, stage3))
+    return [depart, steps[0]], steps[1:], [functools.partial(finish, slot) for slot in slots]
 
 
 def gather_shape(shard, kind, dp, mp):
@@ -251,7 +236,7 @@
     plane = [scratch[4 * u + 2] for u in units]
     line = [scratch[4 * u + 3] for u in units]
     chips = (place.i, place.ix, place.iy, place.ixy)
-    slots = all_slots(mp)[::-1]
+    slots = nearest(z)[::-1]
 
     def piece(u, i2, z2):
         return region(grads[u], i2, z2, own[u].shape[2:])
@@ -293,91 +278,60 @@
             src_ref=own[u].at[z, 0], dst_ref=line[u].at[z2], send_sem=send.at[u, 7, z],
             recv_sem=recv.at[u, 7, z2], device_id=(i, z), device_id_type=MESH)
 
-    def begin(slot):
-        def run(z2):
-            for u in units:
-                for k in (3, 2, 1, 0):
-                    load(u, k, z2).start()
-                    across(u, k, z2).start()
-
-        for_slot(place, slot, run)
-
-    def stage1(slot):
-        def run(z2):
-            for u in units:
-                for k in (3, 2, 1, 0):
-                    load(u, k, z2).wait()
-                    across(u, k, z2).wait_recv()
-                for k in range(4):
-                    add_into(own[u].at[z2, k], sibling[u].at[z2, k])
-                to_second(u, z2, True).start()
-                to_second(u, z2, False).start()
-
-        for_slot(place, slot, run)
-
-    def stage2(slot):
-        def run(z2):
-            for u in units:
-                kf = route(u, z2)[0]
-                to_second(u, z2, True).wait_recv()
-                add_into(own[u].at[z2, kf], plane[u].at[z2, 0])
-                to_first(u, z2).start()
-
-        for_slot(place, slot, run)
-
-    def stage3(slot):
-        d, side = slot
-
-        def run(z2):
-            for u in units:
-                mine = own[u].at[z2, 0]
-                to_second(u, z2, False).wait_recv()
-                to_first(u, z2).wait_recv()
-                add_into(mine, plane[u].at[z2, 1], plane[u].at[z2, 2])
-                if d > 0:
-                    along(u, z2).start()
-
-        for_slot(place, slot, run)
-
-    def finish(slot):
-        d, side = slot
-
-        def run(z2):
-            for u in units:
-                for k in range(4):
-                    across(u, k, z2).wait_send()
-                to_second(u, z2, True).wait_send()
-                to_second(u, z2, False).wait_send()
-                to_first(u, z2).wait_send()
-                if d > 0:
-                    along(u, z2).wait_send()
-
-        for_slot(place, slot, run)
-
-    def collect(slot):
-        d, side = slot
-
-        def run(z2):
-            for u in units:
-                if d == 0:
-                    outs[u][...] = own[u][z, 0].astype(F32)
-                else:
-                    arrival(u, z2).wait_recv()
-                    add_into(outs[u], line[u].at[z2])
-
-        for_slot(place, slot, run)
-
-    steps = [functools.partial(begin, slot) for slot in slots]
-    n = len(slots)
-    for k in range(n + 2):
-        if k < n:
-            steps.append(functools.partial(stage1, slots[k]))
-        if 0 <= k - 1 < n:
-            steps.append(functools.partial(stage2, slots[k - 1]))
-        if 0 <= k - 2 < n:
-            steps.append(functools.partial(stage3, slots[k - 2]))
-    last = [functools.partial(collect, slot) for slot in all_slots(mp)]
-    return steps, last + [functools.partial(finish, slot) for slot in slots]
+    def begin(z2):
+        for u in units:
+            for k in (3, 2, 1, 0):
+                load(u, k, z2).start()
+                across(u, k, z2).start()
+
+    def stage1(z2):
+        for u in units:
+            for k in (3, 2, 1, 0):
+                load(u, k, z2).wait()
+                across(u, k, z2).wait_recv()
+                add_into(own[u].at[z2, k], sibling[u].at[z2, k])
+                if k == 3:
+                    to_second(u, z2, True).start()
+            to_second(u, z2, False).start()
+
+    def stage2(z2):
+        for u in units:
+            kf = route(u, z2)[0]
+            to_second(u, z2, True).wait_recv()
+            add_into(own[u].at[z2, kf], plane[u].at[z2, 0])
+            to_first(u, z2).start()
+
+    def stage3(z2):
+        for u in units:
+            mine = own[u].at[z2, 0]
+            to_second(u, z2, False).wait_recv()
+            to_first(u, z2).wait_recv()
+            add_into(mine, plane[u].at[z2, 1], plane[u].at[z2, 2])
+            if z2 is not z:
+                along(u, z2).start()
+
+    def collect(z2):
+        for u in units:
+            if z2 is z:
+                outs[u][...] = own[u][z, 0].astype(F32)
+            else:
+                arrival(u, z2).wait_recv()
+                add_into(outs[u], line[u].at[z2])
+
+    def finish(z2):
+        for u in units:
+            for k in range(4):
+                across(u, k, z2).wait_send()
+            to_second(u, z2, True).wait_send()
+            to_second(u, z2, False).wait_send()
+            to_first(u, z2).wait_send()
+            if z2 is not z:
+                along(u, z2).wait_send()
+
+    steps = staggered(slots, (stage1, stage2, stage3))
+    head = [functools.partial(begin, z2) for z2 in slots]
+    last = [functools.partial(collect, z2) for z2 in nearest(z)]
+    return head, steps, last + [functools.partial(finish, z2) for z2 in slots]
 
 
 def shard_of(grad, dp, mp):
@@ -403,44 +357,31 @@
     def keep(u):
         return pltpu.make_async_copy(rows[u], spot(u, z), local.at[u])
 
-    def move(slot):
-        d, side = slot
-
-        def run(z2):
-            for u in range(len(rows)):
-                src = rows[u] if d == 0 else None
-                if d > 0:
-                    copy(u, side == 0, z2, z).wait_recv()
-                else:
-                    keep(u).start()
-                if d == 0 or side == 0:
-                    pl.when(z < mp - 1)(lambda u=u, src=src: copy(u, True, z2, z + 1, src).start())
-                if d == 0 or side == 1:
-                    pl.when(z > 0)(lambda u=u, src=src: copy(u, False, z2, z - 1, src).start())
-
-        for_slot(place, slot, run)
-
-    def finish(slot):
-        d, side = slot
-
-        def run(z2):
-            for u in range(len(rows)):
-                if d == 0:
-                    keep(u).wait()
-                if d == 0 or side == 0:
-                    pl.when(z < mp - 1)(lambda u=u: copy(u, True, z2, z).wait_send())
-                if d == 0 or side == 1:
-                    pl.when(z > 0)(lambda u=u: copy(u, False, z2, z).wait_send())
-
-        for_slot(place, slot, run)
-
-    steps = [functools.partial(move, slot) for slot in all_slots(mp)]
-    return steps, [functools.partial(finish, slot) for slot in all_slots(mp)]
-
-
-def woven(*lists):
-    total = [(n / len(steps), k, n) for k, steps in enumerate(lists) for n in range(len(steps))]
-    return [lists[k][n] for _, k, n in sorted(total)]
+    def move(z2):
+        for u in range(len(rows)):
+            src = None
+            if z2 is z:
+                src = rows[u]
+                keep(u).start()
+            else:
+                pl.when(z2 < z)(lambda: copy(u, True, z2, z).wait_recv())
+                pl.when(z2 > z)(lambda: copy(u, False, z2, z).wait_recv())
+            onward(place, z2, lambda up: copy(u, up, z2, z + 1 if up else z - 1, src).start())
+
+    def finish(z2):
+        for u in range(len(rows)):
+            if z2 is z:
+                keep(u).wait()
+            onward(place, z2, lambda up: copy(u, up, z2, z).wait_send())
+
+    slots = nearest(z)
+    steps = [functools.partial(move, z2) for z2 in slots]
+    return steps[:1], steps[1:], [functools.partial(finish, z2) for z2 in slots]
+
+
+def woven(lists):
+    placed = [(place, k, n) for k, (_, places) in enumerate(lists) for n, place in enumerate(places)]
+    return [lists[k][0][n] for _, k, n in sorted(placed)]
 
 
 class Transfers:
@@ -472,22 +413,24 @@
 
     def steps(self, ins, outs, scratch):
         place = Place(self.mp)
-        lists, last = [], []
-
-        def take(steps, ends):
-            lists.append(steps)
+        first, lists, last = [functools.partial(enter, place)], [], []
+
+        def take(head, steps, ends, slow=False):
+            first.extend(head)
+            paces = [0.45 * (n + 1) if slow else n / len(steps) for n in range(len(steps))]
+            lists.append((steps, paces))
             last.extend(ends)
 
         count, more = len(self.shards), len(self.shards) + len(self.grads)
         if self.rows:
-            take(*line_steps(place, ins[more:], outs[more:], *scratch[:3]))
+            take(*line_steps(place, ins[more:], outs[more:], *scratch[:3]), slow=True)
             scratch = scratch[3:]
         if count:
             take(*gather_steps(place, ins[:count], outs[:count], *scratch[:3]))
             scratch = scratch[3:]
         if self.grads:
             take(*scatter_steps(place, ins[count:more], outs[count:more], scratch))
-        return [functools.partial(enter, place)] + woven(*lists), last
+        return first, woven(lists), last
 
     def params(self, limit):
         return pltpu.CompilerParams(
@@ -499,8 +442,8 @@
 
         def kernel(*refs):
             outs = refs[count : count + len(self.outs)]
-            steps, last = self.steps(refs[:count], outs, refs[count + len(self.outs) :])
-            for step in steps + last:
+            first, steps, last = self.steps(refs[:count], outs, refs[count + len(self.outs) :])
+            for step in first + steps + last:
                 step()
 
         return pl.pallas_call(
@@ -511,13 +454,20 @@
 
 class Pace:
     def __init__(self, found, each):
-        self.steps, self.last = found
+        self.first, self.steps, self.last = found
         self.group, self.groups, self.each, self.at = pl.program_id(0), pl.num_programs(0), each, 0
 
     def place(self):
         total = self.groups * self.each
+
+        def begin():
+            for step in self.first:
+                step()
+
+        if self.at == 0 and self.first:
+            pl.when(self.group == 0)(begin)
         for n, step in enumerate(self.steps):
-            group, at = divmod(n * total // len(self.steps), self.each)
+            group, at = divmod((n + 1) * total // (len(self.steps) + 1), self.each)
             if at == self.at:
                 pl.when(self.group == group)(step)
         self.at += 1
@@ -589,7 +539,7 @@
 
 def split_refs(refs, host, ins, outs):
     if host is None:
-        return list(refs), ([], [])
+        return list(refs), ([], [], [])
     a, b = len(host.args), len(host.outs)
     cut = [0, ins, ins + a, ins + a + outs, ins + a + outs + b, len(refs) - len(host.scratch), len(refs)]
     part = [list(refs[i:j]) for i, j in zip(cut, cut[1:])]
@@ -881,7 +831,7 @@
 
 
 def row_chunk(rows):
-    for size in (272, 256, 128):
+    for size in (544, 272, 256, 128):
         if rows % size == 0:
             return size
     return rows
@@ -1025,14 +975,16 @@
 
 
 def feed_kernel(
-    o_ref, wo_ref, h1_ref, gain_ref, up_ref, wg_ref, wu_ref, wd_ref,
-    out_ref, g2_ref, gain_out, gwg_ref, gwu_ref, gwd_ref, do_ref, gwo_ref,
-    h2, normed, total, back, hidden_s, dgate_s, dup_s,
+    o_ref, wo_ref, h1_ref, gain_ref, up_ref, wa_ref, wb_ref, wd_ref,
+    out_ref, g2_ref, gain_out, gwa_ref, gwb_ref, gwd_ref, do_ref, gwo_ref,
+    h2, normed, total, back, hidden_s, grad_s,
 ):
     rows, width = h1_ref.shape
     j = pl.program_id(0)
     size = row_chunk(rows)
     up_ref = flat(up_ref)
+    cols = wd_ref.shape[0]
+    cut = wa_ref.shape[2]
 
     @pl.when(j == 0)
     def _():
@@ -1050,26 +1002,27 @@
         some = pl.ds(at, size)
         n = normed[some, :]
         g = up_ref[some, :]
-        gate = mm(n, wg_ref[0])
-        up = mm(n, wu_ref[0])
+        both = jnp.concatenate([mm(n, wa_ref[0]), mm(n, wb_ref[0])], axis=1)
+        gate, up = both[:, :cols], both[:, cols:]
         grad_hidden = mm_nt(g, wd_ref[...])
         active, pull = gate_parts(gate)
         hidden = (active * up).astype(BF16)
         grad_gate = (grad_hidden * up * pull).astype(BF16)
         grad_up = (grad_hidden * active).astype(BF16)
         hidden_s[some, :] = hidden
-        dgate_s[some, :] = grad_gate
-        dup_s[some, :] = grad_up
+        grads = jnp.concatenate([grad_gate, grad_up], axis=1)
+        grad_s[some, :] = grads
         total[some, :] += mm(hidden, wd_ref[...])
-        back[some, :] += mm_nt(grad_gate, wg_ref[0]) + mm_nt(grad_up, wu_ref[0])
+        back[some, :] += mm_nt(grads[:, :cut], wa_ref[0]) + mm_nt(grads[:, cut:], wb_ref[0])
 
     chunked(rows, size, hidden_rows)
 
     def weight_rows(at):
         some = pl.ds(at, 512)
         n = normed[:, some]
-        gwg_ref[0, some, :] = mm_tn(n, dgate_s[...]).astype(BF16)
-        gwu_ref[0, some, :] = mm_tn(n, dup_s[...]).astype(BF16)
+        gw = mm_tn(n, grad_s[...]).astype(BF16)
+        gwa_ref[0, some, :] = gw[:, :cut]
+        gwb_ref[0, some, :] = gw[:, cut:]
         gwd_ref[:, some] = mm_tn(hidden_s[...], up_ref[:, some]).astype(BF16)
 
     chunked(width, 512, weight_rows)
@@ -1099,19 +1052,20 @@
         chunked(width, 512, out_rows)
 
 
-def feed(where, o, wo, h1, gain, upstream, wg, wu, wd):
+def feed(where, o, wo, h1, gain, upstream, wa, wb, wd):
     rows, width = h1.shape
-    groups, _, cols = wg.shape
+    groups = wa.shape[0]
+    cols = wa.shape[2] + wb.shape[2]
     out, g2, gg = shape(h1.shape), shape(h1.shape, F32), shape((1, width), F32)
     return kernel_call(
         feed_kernel, "feed", groups, where,
         [(o, full(o)), (wo, full(wo)), (h1, full(h1)), (gain, full(gain)), my_rows(upstream),
-         (wg, lead_block(wg)), (wu, lead_block(wu)), (wd, row_block(wd, groups))],
-        [(out, full(out)), (g2, full(g2)), (gg, full(gg)), (wg, lead_block(wg)), (wu, lead_block(wu)),
+         (wa, lead_block(wa)), (wb, lead_block(wb)), (wd, row_block(wd, groups))],
+        [(out, full(out)), (g2, full(g2)), (gg, full(gg)), (wa, lead_block(wa)), (wb, lead_block(wb)),
          (wd, row_block(wd, groups)), (o, full(o)), (wo, full(wo))],
         [pltpu.VMEM((rows, width), F32), pltpu.VMEM((rows, width), BF16), pltpu.VMEM((rows, width), F32),
-         pltpu.VMEM((rows, width), F32)] + [pltpu.VMEM((rows, cols), BF16)] * 3,
-        18 * rows * width * groups * cols,
+         pltpu.VMEM((rows, width), F32)] + [pltpu.VMEM((rows, cols // 2), BF16), pltpu.VMEM((rows, cols), BF16)],
+        9 * rows * width * groups * cols,
     )
 
 
@@ -1354,7 +1308,8 @@
 
         w1 = blocks(self_query, self_key, self_value)
         w2 = blocks(cross_query, cross_key, cross_value)
-        wg, wu = blocks(feed_gate), blocks(feed_up)
+        w3 = blocks(feed_gate, feed_up)
+        wa, wb = w3[:, :, : w3.shape[2] // 2], w3[:, :, w3.shape[2] // 2 :]
         wo1, wo2, wd = (gather(s, ROWS_BY_MP) for s in (self_out, cross_out, feed_down))
     gain_one, gain_two, gain_three = gains
 
@@ -1393,30 +1348,33 @@
     q1, k1, v1, n1 = self_project(where, inputs, own_inputs, gain_one, w1, tiles.reach, rows)
     hosts = [None] * 4
     if native:
-        hosts[0] = Transfers(dp, mp, 2, [w2, cross_out, feed_gate], order + ["by_dp"])
-        hosts[1] = Transfers(dp, mp, 3, [feed_up, feed_down], order)
+        w3 = jnp.concatenate([feed_gate, feed_up], axis=1)
+        hosts[0] = Transfers(dp, mp, 2, [w2, cross_out, feed_down], order + ["by_mp"])
+        middle = round_up(w3.shape[1] // 2, 128)
+        hosts[1] = Transfers(dp, mp, 3, [w3[:, :middle], w3[:, middle:]], ["by_dp", "by_dp"])
     (o1, lse_one), found = attend_forward(
         q1, k1, v1, mask_one, vec, tiles, True, "self_forward", hosts[0]
     )
     if native:
-        w2, wo2, wg = found
-        w2, wg = (w.reshape(mp, width, w.shape[3]) for w in (w2, wg))
+        w2, wo2, wd = found
+        w2 = w2.reshape(mp, width, w2.shape[3])
     h1, n2, q2, k2, v2 = cross_project(where, o1, wo1, own_inputs, gain_two, encoded, w2)
     (o2, lse_two), found = attend_forward(
         q2, k2, v2, mask_two, keys_two, tiles, False, "cross_forward", hosts[1]
     )
     if native:
-        wu, wd = found
-        wu = wu.reshape(mp, width, wu.shape[3])
-
-    result, grad_two, grad_gain_three, gwg, gwu, gwd, do2, gwo2 = feed(
-        where, o2, wo2, h1, gain_three, cut(cotangent), wg, wu, wd
+        wa, wb = (w.reshape(mp, width, w.shape[3]) for w in found)
+
+    result, grad_two, grad_gain_three, gwa, gwb, gwd, do2, gwo2 = feed(
+        where, o2, wo2, h1, gain_three, cut(cotangent), wa, wb, wd
     )
 
     def collect(array):
         array = lax.all_gather(array, "mp", axis=0, tiled=True)
         array = array.reshape(batches, parts, length // 64, tiles.blk, width)
         return array.transpose(0, 2, 1, 3, 4).reshape(batches, length, width)
+
+    outputs = collect(result)
 
     def pieces(grad):
         return grad.reshape(grad.shape[0], dp, grad.shape[1] // dp, grad.shape[2])
@@ -1432,43 +1390,29 @@
         )
 
     if native:
-        hosts[2] = Transfers(
-            dp, mp, 4, grads=[gwd], rows=[result.reshape(length // 64, tiles.blk, width)],
-            spread=[(batches, length // 64, parts, tiles.blk, width)],
-        )
+        hosts[2] = Transfers(dp, mp, 4, grads=[gwd])
         hosts[2].swap = Exchange(1, enc_length // 2, groups)
     (dq2, *dkv2), sums_down = attend_backward(
         q2, k2, v2, o2, do2, lse_two, mask_two, keys_two, tiles, False, "cross_backward", hosts[2]
     )
-    if native:
-        dkv2 = dkv2[0]
-        *sums_down, outputs = sums_down
-        outputs = outputs.reshape(inputs.shape)
-    else:
-        dkv2 = share(dkv2[1], dkv2[0], 1)
-        outputs = collect(result)
+    dkv2 = dkv2[0] if native else share(dkv2[1], dkv2[0], 1)
     gwq2, grad_one, grad_gain_two, do1, gwo1 = cross_back(
         where, dq2, w2, n2, h1, gain_two, grad_two, wo1, o1
     )
     gwkv2, grad_memory = memory_back(where, dkv2, w2, encoded)
 
     if native:
-        line = grad_memory.reshape(1, -1, width)
-        hosts[3] = Transfers(
-            dp, mp, 5, grads=[pieces(gwg), pieces(gwu)], rows=[line],
-            spread=[(batches, 1, parts, enc_length // parts, width)],
-        )
+        grads = [pieces(gwa), pieces(gwb)]
+        hosts[3] = Transfers(dp, mp, 5, grads=grads)
         hosts[3].swap = Exchange(length // 64, tiles.blk, groups)
     (dq1, slopes, *dkv1), sums_feed = attend_backward(
         q1, k1, v1, o1, do1, lse_one, mask_one, vec, tiles, True, "self_backward", hosts[3]
     )
     if native:
         dkv1 = dkv1[0]
-        *sums_feed, grad_encoded = sums_feed
-        grad_encoded = grad_encoded.reshape(encoded.shape)
     else:
         dkv1 = share(dkv1[1][:length], dkv1[0][:length], length // 64)
-        grad_encoded = lax.all_gather(grad_memory, "mp", axis=0, tiled=True).reshape(encoded.shape)
+    grad_encoded = lax.all_gather(grad_memory, "mp", axis=0, tiled=True).reshape(encoded.shape)
     gwq1, gwkv1, grad_rows, grad_gain_one = self_back(
         where, dq1, dkv1, w1, n1, own_inputs, gain_one, grad_one
     )
@@ -1493,7 +1437,10 @@
         ).run("scatter_rest")
         grad_inputs = grad_inputs.reshape(inputs.shape)
         sums = sums + list(sums_feed) + list(sums_down)
-        gwq2, gwkv2, gwq1, gwkv1, gwo2, gwo1, gwg, gwu, gwd = sums
+        gwq2, gwkv2, gwq1, gwkv1, gwo2, gwo1, gwa, gwb, gwd = sums
+        gw3 = jnp.concatenate([gwa, gwb], axis=1)
+        half = gw3.shape[1] // 2
+        gwg, gwu = gw3[:, :half], gw3[:, half:]
         gwk2, gwv2, gwk1, gwv1 = (
             g[:, at : at + kcols] for g in (gwkv2, gwkv1) for at in (0, kcols)
         )
@@ -1507,7 +1454,8 @@
 
         gwk1, gwv1 = summed(gwkv1[:, :, :kcols]), summed(gwkv1[:, :, kcols:])
         gwk2, gwv2 = summed(gwkv2[:, :, :kcols]), summed(gwkv2[:, :, kcols:])
-        gwq1, gwq2, gwg, gwu = (summed(g) for g in (gwq1, gwq2, gwg, gwu))
+        gwg, gwu = summed(gwa), summed(gwb)
+        gwq1, gwq2 = summed(gwq1), summed(gwq2)
         gwo1, gwo2, gwd = (scatter(g, ROWS_BY_MP) for g in (gwo1, gwo2, gwd))
         small = jnp.concatenate([grad_gains.reshape(-1), grad_table.reshape(-1)])
         small = lax.psum(small, ("dp", "mp"))

time: 693 us -> 668 us (0.964)
  Pallas kernels: 650 us -> 607 us
  between operations: 1.25 us -> 14.8 us
    pallas_call x4, Pallas kernels: 364 us -> 341 us  [attention_call(): pl.pallas_call(functools.partial(kernel, biased, tiles, host), grid=(step...]
    pallas_call x2, Pallas kernels: 168 us -> 153 us  [run(): pl.pallas_call(kernel, grid=(1,), out_shape=self.outs, in_specs=self.in_s...]
    unnamed x44 -> x51, local copies, waits for them, and re-layouts: 18.1 us -> 12.3 us
  transfers between devices with their start and end apart: 0 -> 2, of which waited for: 0 -> 0; matrix products, arithmetic and copies ran while one was open for 0% -> 1% of each run, Pallas kernels for 0% -> 44%
where the time goes in v4:
time: 668 us; the launch traced here: 661 us
  Pallas kernels  607 us (91%)
  local copies, waits for them, and re-layouts  30.8 us (5%)
  between operations  14.8 us (2%)
  other arithmetic  6.88 us (1%)
    pallas_call x4, Pallas kernels, attention_call(): pl.pallas_call(functools.partial(kernel, biased, tiles, host), grid=(step...  341 us
    pallas_call x2, Pallas kernels, run(): pl.pallas_call(kernel, grid=(1,), out_shape=self.outs, in_specs=self.in_s...  153 us
    pallas_call x6, Pallas kernels, kernel_call(): pl.pallas_call(lambda _, *refs: body(*refs), out_shape=[jax.ShapeDtypeStr...  113 us
  transfers between devices with their start and end apart: 2, of which 0 were waited for; matrix products, arithmetic and copies ran while one was open for 1% of the time, Pallas kernels for 44%

profile of v4, /device:TPU:8, one launch (start us, length us, event | category | flops | bytes accessed | tf_op | source)
XLA Modules:
  0.0 660.9 jit_solution(6965728525527017217)
XLA Ops:
  10.4 1.5 pad_maximum_fusion.2.refs_0_
  12.0 36.6 %gather_self.1 = (bf16[4,8,128,512]{3,2,1,0:T(8,128)(2,1)}, bf16[4,8,16,128]{3,2,1,0:T(8,128)(2,1)}, bf16[1024,1024]{1,0:T(8,128)(2,1)}) custom-call(bf16[128,512]{1,0:T(8,128)(2,1)} %pad_maximum_fusion.2.refs_0_, bf16[16,128]{1,0:T(8,128)(2,1)} %pad.29.refs_1_, bf16[256,128]{1,0:T(8,128)(2,1)} %refs_2_.1), custom_call_target="tpu_custom_call" | custom-call | tf_op jit(solution)/shard_map/gather_self/pallas_call | solution.py:449
  48.6 0.9 slice.86
  51.5 1.1 copy.61
  53.4 1.1 copy.60
  58.6 11.7 %self_project.1 = (bf16[544,1024]{1,0:T(8,128)(2,1)}, bf16[1280,512]{1,0:T(8,128)(2,1)}, bf16[1280,512]{1,0:T(8,128)(2,1)}, bf16[544,1024]{1,0:T(8,128)(2,1)}) custom-call(s32[2]{0:T(128)} %pad_add_fusion._, bf16[2,1088,1024]{2,1,0:T(8,128)(2,1)} %refs_0_.1, bf16[2,17,2,32,1024]{4,3,2,1,0:T(8,128)(2,1)} %bitcast.70, ...), custom_call_target="tpu_custom_call" | custom-call | flops 3422552064 | bytes 16777216 | tf_op jit(solution)/shard_map/self_project/pallas_call | solution.py:857
  71.6 72.6 %self_forward.1 = (bf16[544,1024]{1,0:T(8,128)(2,1)}, f32[4,5,512]{2,1,0:T(8,128)}, bf16[4,8,128,512]{3,2,1,0:T(8,128)(2,1)}, bf16[1024,1024]{1,0:T(8,128)(2,1)}, bf16[2816,1024]{1,0:T(8,128)(2,1)}) custom-call(bf16[544,1024]{1,0:T(8,128)(2,1)} %get-tuple-element.76.refs_0_, bf16[1280,512]{1,0:T(8,128)(2,1)} %get-tuple-element.77.refs_1_, ...), custom_call_target="tpu_custom_call" | custom-call | flops 2852126720 | bytes 16777216 | tf_op jit(solution)/shard_map/self_forward/pallas_call | solution.py:760
  144.2 10.1 %cross_project.1 = (f32[544,1024]{1,0:T(8,128)}, bf16[544,1024]{1,0:T(8,128)(2,1)}, bf16[544,1024]{1,0:T(8,128)(2,1)}, bf16[512,512]{1,0:T(8,128)(2,1)}, bf16[512,512]{1,0:T(8,128)(2,1)}) custom-call(s32[2]{0:T(128)} %pad_add_fusion._, bf16[544,1024]{1,0:T(8,128)(2,1)} %get-tuple-element.79.refs_0_.refs_7_.refs_3_, ...), custom_call_target="tpu_custom_call" | custom-call | flops 3422552064 | bytes 16777216 | tf_op jit(solution)/shard_map/cross_project/pallas_call | solution.py:857
  154.3 0.8 broadcast_in_dim.7.refs_4_.refs_7_
  155.1 64.4 %cross_forward.1 = (bf16[544,1024]{1,0:T(8,128)(2,1)}, f32[4,5,512]{2,1,0:T(8,128)}, bf16[4,8,128,768]{3,2,1,0:T(8,128)(2,1)}, bf16[4,8,128,640]{3,2,1,0:T(8,128)(2,1)}) custom-call(bf16[544,1024]{1,0:T(8,128)(2,1)} %get-tuple-element.82.refs_0_, bf16[512,512]{1,0:T(8,128)(2,1)} %get-tuple-element.83.refs_1_, bf16[512,512]{1,0:T(8,128)(2,1)} %get-tuple-element.84.refs_2_, ...), custom_call_target="tpu_custom_call" | custom-call | flops 1140850688 | bytes 16777216 | tf_op jit(solution)/shard_map/cross_forward/pallas_call | solution.py:760
  219.5 53.0 %feed.1 = (bf16[544,1024]{1,0:T(8,128)(2,1)}, f32[544,1024]{1,0:T(8,128)}, f32[1,1024]{1,0:T(1,128)}, bf16[4,1024,768]{2,1,0:T(8,128)(2,1)}, bf16[4,1024,640]{2,...) custom-call(s32[2]{0:T(128)} %pad_add_fusion._, ...), custom_call_target="tpu_custom_call" | custom-call | flops 28236054528 | bytes 16777216 | tf_op jit(solution)/shard_map/feed/pallas_call | solution.py:857
  272.5 61.6 %cross_backward.1 = (bf16[544,1024]{1,0:T(8,128)(2,1)}, bf16[256,1024]{1,0:T(8,128)(2,1)}, f32[704,128]{1,0:T(8,128)}) custom-call(bf16[544,1024]{1,0:T(8,128)(2,1)} %get-tuple-element.82.refs_0_, bf16[512,512]{1,0:T(8,128)(2,1)} %get-tuple-element.83.refs_1_, bf16[512,512]{1,0:T(8,128)(2,1)} %get-tuple-element.84.refs_2_, ...), custom_call_target="tpu_custom_call" | custom-call | flops 2852126720 | bytes 16777216 | tf_op jit(solution)/shard_map/cross_backward/pallas_call | solution.py:760
  334.1 6.4 memory_back.1
  341.3 17.3 %cross_back.1 = (bf16[4,1024,256]{2,1,0:T(8,128)(2,1)}, f32[544,1024]{1,0:T(8,128)}, f32[1,1024]{1,0:T(1,128)}, bf16[544,1024]{1,0:T(8,128)(2,1)}, bf16[1024,1024]{1,0:T(8,128)(2,1)}) custom-call(s32[2]{0:T(128)} %pad_add_fusion._, bf16[544,1024]{1,0:T(8,128)(2,1)} %get-tuple-element.95.refs_0_, bf16[4,1024,512]{2,1,0:T(8,128)(2,1)} %bitcast.75, ...), custom_call_target="tpu_custom_call" | custom-call | flops 4563402752 | bytes 16777216 | tf_op jit(solution)/shard_map/cross_back/pallas_call | solution.py:857
  358.6 142.0 %self_backward.1 = (bf16[544,1024]{1,0:T(8,128)(2,1)}, f32[4,4,1536]{2,1,0:T(4,128)}, bf16[544,1024]{1,0:T(8,128)(2,1)}, f32[128,768]{1,0:T(8,128)}, f32[128,640]{1,0:T(8,128)}) custom-call(bf16[544,1024]{1,0:T(8,128)(2,1)} %get-tuple-element.76.refs_0_, bf16[1280,512]{1,0:T(8,128)(2,1)} %get-tuple-element.77.refs_1_, ...), custom_call_target="tpu_custom_call" | custom-call | flops 7130316800 | bytes 16777216 | tf_op jit(solution)/shard_map/self_backward/pallas_call | solution.py:760
  500.6 0.9 reshape.187
  502.3 14.9 %self_back.1 = (bf16[4,1024,256]{2,1,0:T(8,128)(2,1)}, bf16[4,1024,256]{2,1,0:T(8,128)(2,1)}, bf16[544,1024]{1,0:T(8,128)(2,1)}, f32[1,1024]{1,0:T(1,128)}) custom-call(s32[2]{0:T(128)} %pad_add_fusion._, bf16[544,1024]{1,0:T(8,128)(2,1)} %get-tuple-element.105.refs_0_, bf16[544,1024]{1,0:T(8,128)(2,1)} %get-tuple-element.106.refs_1_.refs_2_, ...), custom_call_target="tpu_custom_call" | custom-call | flops 4563402752 | bytes 16777216 | tf_op jit(solution)/shard_map/self_back/pallas_call | solution.py:857
  518.6 116.4 %scatter_rest.1 = (f32[128,256]{1,0:T(8,128)}, f32[128,256]{1,0:T(8,128)}, f32[128,256]{1,0:T(8,128)}, f32[128,256]{1,0:T(8,128)}, f32[256,128]{1,0:T(8,128)}, /...) custom-call(bf16[4,8,128,256]{3,2,1,0:T(8,128)(2,1)} %bitcast.85, ...), custom_call_target="tpu_custom_call" | custom-call | tf_op jit(solution)/shard_map/scatter_rest/pallas_call | solution.py:449
  636.6 0.9 copy.68
  637.5 0.9 copy.67
  638.4 1.3 slice_bitcast_fusion.3
  640.4 5.4 copy.63
  645.8 2.2 copy.76
  648.9 1.3 copy.77
  (109 shorter events, 20.8 us)
Async XLA Ops:
  7.2 0.7 copy-start
  7.2 49.0 %copy-start.17 = (s32[1088]{0:T(1024)S(1)}, s32[1088]{0:T(1024)}, u32[]{:S(2)}) copy-start(s32[1088]{0:T(1024)} %param.25) | copy-start | bytes 13060
  7.2 50.7 %copy-start.13 = (bf16[128,128]{1,0:T(8,128)(2,1)S(1)}, bf16[128,128]{1,0:T(8,128)(2,1)}, u32[]{:S(2)}) copy-start(bf16[128,128]{1,0:T(8,128)(2,1)} %param.35) | copy-start | bytes 98308
  7.2 50.7 %copy-start.14 = (bf16[128,128]{1,0:T(8,128)(2,1)S(1)}, bf16[128,128]{1,0:T(8,128)(2,1)}, u32[]{:S(2)}) copy-start(bf16[128,128]{1,0:T(8,128)(2,1)} %param.34) | copy-start | bytes 98308
  7.2 50.7 %copy-start.12 = (bf16[128,256]{1,0:T(8,128)(2,1)S(1)}, bf16[128,256]{1,0:T(8,128)(2,1)}, u32[]{:S(2)}) copy-start(bf16[128,256]{1,0:T(8,128)(2,1)} %param.33) | copy-start | bytes 196612
  7.2 633.1 %all-gather.5.cloned.1.call-start = ((), (), s32[]{:S(2)}) async-start(), calls=%async_computation.1 | async-start | bytes 2621440 | tf_op jit(solution)/shard_map/all_gather | solution.py:1415
  340.5 299.9 %all-gather.3.cloned.1.call-start = ((), (), s32[]{:S(2)}) async-start(), calls=%async_computation | async-start | bytes 5570560 | tf_op jit(solution)/shard_map/all_gather | solution.py:1373
  502.3 14.9 %copy-start.15 = (f32[1,1024]{1,0:T(1,128)S(1)}, f32[1,1024]{1,0:T(1,128)}, u32[]{:S(2)}) copy-start(f32[1,1024]{1,0:T(1,128)} %get-tuple-element.115) | copy-start | bytes 12292
  502.3 14.9 %copy-start.16 = (f32[1,1024]{1,0:T(1,128)S(1)}, f32[1,1024]{1,0:T(1,128)}, u32[]{:S(2)}) copy-start(f32[1,1024]{1,0:T(1,128)} %get-tuple-element.114) | copy-start | bytes 12292
  518.6 117.8 %copy-start.3 = (f32[128,768]{1,0:T(8,128)S(1)}, f32[128,768]{1,0:T(8,128)}, u32[]{:S(2)}) copy-start(f32[128,768]{1,0:T(8,128)} %get-tuple-element.127) | copy-start | bytes 1179652
  518.6 117.8 %copy-start.5 = (f32[128,640]{1,0:T(8,128)S(1)}, f32[128,640]{1,0:T(8,128)}, u32[]{:S(2)}) copy-start(f32[128,640]{1,0:T(8,128)} %get-tuple-element.128) | copy-start | bytes 983044
  635.0 4.7 copy-start.10
  635.0 4.7 copy-start.11
  640.4 5.4 slice-start
  640.4 5.4 slice-start.1
  645.8 3.1 copy-start.2
  645.8 7.8 %copy-start.1 = (s32[2,1088]{1,0:T(2,128)S(1)}, s32[2,1088]{1,0:T(2,128)}, u32[]{:S(2)}) copy-start(s32[2,1088]{1,0:T(2,128)} %param.23) | copy-start | bytes 26116
  648.9 1.3 copy-start.9
  648.9 2.0 copy-start.8
  648.9 2.7 copy-start.7
  648.9 3.3 copy-start.6
  648.9 4.0 copy-start.4
Sparse Core Ops, SparseCore 0:
  340.6 48.7 all-gather.4
  390.9 117.8 all-gather.2

commit v5 on v4

--- a/solution.py
+++ b/solution.py
@@ -1390,7 +1390,7 @@
         )
 
     if native:
-        hosts[2] = Transfers(dp, mp, 4, grads=[gwd])
+        hosts[2] = Transfers(dp, mp, 4, grads=[gwd, gwo2])
         hosts[2].swap = Exchange(1, enc_length // 2, groups)
     (dq2, *dkv2), sums_down = attend_backward(
         q2, k2, v2, o2, do2, lse_two, mask_two, keys_two, tiles, False, "cross_backward", hosts[2]
@@ -1430,14 +1430,14 @@
         spots = spots.transpose(2, 0, 1, 3).reshape(mp, dp, 1, position_bias.size)
         spots = jnp.pad(spots, ((0, 0), (0, 0), (0, 4), (0, size - position_bias.size)))
         little = jnp.concatenate([little, spots], axis=2)
-        grads = [pieces(g) for g in (gwq2, gwkv2, gwq1, gwkv1)] + [gwo2, gwo1, little]
+        grads = [pieces(g) for g in (gwq2, gwkv2, gwq1, gwkv1)] + [gwo1, little]
         *sums, little, grad_inputs = Transfers(
             dp, mp, 6, grads=grads, rows=[grad_rows.reshape(length // 64, tiles.blk, width)],
             spread=[(batches, length // 64, parts, tiles.blk, width)],
         ).run("scatter_rest")
         grad_inputs = grad_inputs.reshape(inputs.shape)
         sums = sums + list(sums_feed) + list(sums_down)
-        gwq2, gwkv2, gwq1, gwkv1, gwo2, gwo1, gwa, gwb, gwd = sums
+        gwq2, gwkv2, gwq1, gwkv1, gwo1, gwa, gwb, gwd, gwo2 = sums
         gw3 = jnp.concatenate([gwa, gwb], axis=1)
         half = gw3.shape[1] // 2
         gwg, gwu = gw3[:, :half], gw3[:, half:]

time: 668 us -> 664 us (level)
  transfers between devices with their start and end apart: 2 -> 2, of which waited for: 0 -> 0; matrix products, arithmetic and copies ran while one was open for 1% -> 1% of each run, Pallas kernels for 44% -> 43%
where the time goes in v5:
time: 664 us; the launch traced here: 657 us
  Pallas kernels  603 us (91%)
  local copies, waits for them, and re-layouts  30.8 us (5%)
  between operations  14.8 us (2%)
  other arithmetic  6.88 us (1%)
    pallas_call x4, Pallas kernels, attention_call(): pl.pallas_call(functools.partial(kernel, biased, tiles, host), grid=(step...  343 us
    pallas_call x2, Pallas kernels, run(): pl.pallas_call(kernel, grid=(1,), out_shape=self.outs, in_specs=self.in_s...  146 us
    pallas_call x6, Pallas kernels, kernel_call(): pl.pallas_call(lambda _, *refs: body(*refs), out_shape=[jax.ShapeDtypeStr...  113 us
  transfers between devices with their start and end apart: 2, of which 0 were waited for; matrix products, arithmetic and copies ran while one was open for 1% of the time, Pallas kernels for 43%

profile of v5, /device:TPU:8, one launch (start us, length us, event | category | flops | bytes accessed | tf_op | source)
XLA Modules:
  0.0 656.8 jit_solution(1448028038219431877)
XLA Ops:
  10.4 1.5 pad_maximum_fusion.2.refs_0_
  12.0 36.6 %gather_self.1 = (bf16[4,8,128,512]{3,2,1,0:T(8,128)(2,1)}, bf16[4,8,16,128]{3,2,1,0:T(8,128)(2,1)}, bf16[1024,1024]{1,0:T(8,128)(2,1)}) custom-call(bf16[128,512]{1,0:T(8,128)(2,1)} %pad_maximum_fusion.2.refs_0_, bf16[16,128]{1,0:T(8,128)(2,1)} %pad.29.refs_1_, bf16[256,128]{1,0:T(8,128)(2,1)} %refs_2_.1), custom_call_target="tpu_custom_call" | custom-call | tf_op jit(solution)/shard_map/gather_self/pallas_call | solution.py:449
  48.6 0.9 slice.86
  51.5 1.1 copy.61
  53.4 1.1 copy.60
  58.6 11.7 %self_project.1 = (bf16[544,1024]{1,0:T(8,128)(2,1)}, bf16[1280,512]{1,0:T(8,128)(2,1)}, bf16[1280,512]{1,0:T(8,128)(2,1)}, bf16[544,1024]{1,0:T(8,128)(2,1)}) custom-call(s32[2]{0:T(128)} %pad_add_fusion._, bf16[2,1088,1024]{2,1,0:T(8,128)(2,1)} %refs_0_.1, bf16[2,17,2,32,1024]{4,3,2,1,0:T(8,128)(2,1)} %bitcast.70, ...), custom_call_target="tpu_custom_call" | custom-call | flops 3422552064 | bytes 16777216 | tf_op jit(solution)/shard_map/self_project/pallas_call | solution.py:857
  71.6 72.6 %self_forward.1 = (bf16[544,1024]{1,0:T(8,128)(2,1)}, f32[4,5,512]{2,1,0:T(8,128)}, bf16[4,8,128,512]{3,2,1,0:T(8,128)(2,1)}, bf16[1024,1024]{1,0:T(8,128)(2,1)}, bf16[2816,1024]{1,0:T(8,128)(2,1)}) custom-call(bf16[544,1024]{1,0:T(8,128)(2,1)} %get-tuple-element.76.refs_0_, bf16[1280,512]{1,0:T(8,128)(2,1)} %get-tuple-element.77.refs_1_, ...), custom_call_target="tpu_custom_call" | custom-call | flops 2852126720 | bytes 16777216 | tf_op jit(solution)/shard_map/self_forward/pallas_call | solution.py:760
  144.2 10.1 %cross_project.1 = (f32[544,1024]{1,0:T(8,128)}, bf16[544,1024]{1,0:T(8,128)(2,1)}, bf16[544,1024]{1,0:T(8,128)(2,1)}, bf16[512,512]{1,0:T(8,128)(2,1)}, bf16[512,512]{1,0:T(8,128)(2,1)}) custom-call(s32[2]{0:T(128)} %pad_add_fusion._, bf16[544,1024]{1,0:T(8,128)(2,1)} %get-tuple-element.79.refs_0_.refs_7_.refs_3_, ...), custom_call_target="tpu_custom_call" | custom-call | flops 3422552064 | bytes 16777216 | tf_op jit(solution)/shard_map/cross_project/pallas_call | solution.py:857
  154.3 0.8 broadcast_in_dim.7.refs_4_.refs_7_
  155.1 64.4 %cross_forward.1 = (bf16[544,1024]{1,0:T(8,128)(2,1)}, f32[4,5,512]{2,1,0:T(8,128)}, bf16[4,8,128,768]{3,2,1,0:T(8,128)(2,1)}, bf16[4,8,128,640]{3,2,1,0:T(8,128)(2,1)}) custom-call(bf16[544,1024]{1,0:T(8,128)(2,1)} %get-tuple-element.82.refs_0_, bf16[512,512]{1,0:T(8,128)(2,1)} %get-tuple-element.83.refs_1_, bf16[512,512]{1,0:T(8,128)(2,1)} %get-tuple-element.84.refs_2_, ...), custom_call_target="tpu_custom_call" | custom-call | flops 1140850688 | bytes 16777216 | tf_op jit(solution)/shard_map/cross_forward/pallas_call | solution.py:760
  219.5 53.0 %feed.1 = (bf16[544,1024]{1,0:T(8,128)(2,1)}, f32[544,1024]{1,0:T(8,128)}, f32[1,1024]{1,0:T(1,128)}, bf16[4,1024,768]{2,1,0:T(8,128)(2,1)}, bf16[4,1024,640]{2,...) custom-call(s32[2]{0:T(128)} %pad_add_fusion._, ...), custom_call_target="tpu_custom_call" | custom-call | flops 28236054528 | bytes 16777216 | tf_op jit(solution)/shard_map/feed/pallas_call | solution.py:857
  272.5 63.5 %cross_backward.1 = (bf16[544,1024]{1,0:T(8,128)(2,1)}, bf16[256,1024]{1,0:T(8,128)(2,1)}, f32[704,128]{1,0:T(8,128)}, f32[256,128]{1,0:T(8,128)}) custom-call(bf16[544,1024]{1,0:T(8,128)(2,1)} %get-tuple-element.82.refs_0_, bf16[512,512]{1,0:T(8,128)(2,1)} %get-tuple-element.83.refs_1_, bf16[512,512]{1,0:T(8,128)(2,1)} %get-tuple-element.84.refs_2_, ...), custom_call_target="tpu_custom_call" | custom-call | flops 2852126720 | bytes 16777216 | tf_op jit(solution)/shard_map/cross_backward/pallas_call | solution.py:760
  336.0 6.4 memory_back.1
  343.1 17.3 %cross_back.1 = (bf16[4,1024,256]{2,1,0:T(8,128)(2,1)}, f32[544,1024]{1,0:T(8,128)}, f32[1,1024]{1,0:T(1,128)}, bf16[544,1024]{1,0:T(8,128)(2,1)}, bf16[1024,1024]{1,0:T(8,128)(2,1)}) custom-call(s32[2]{0:T(128)} %pad_add_fusion._, bf16[544,1024]{1,0:T(8,128)(2,1)} %get-tuple-element.96.refs_0_, bf16[4,1024,512]{2,1,0:T(8,128)(2,1)} %bitcast.75, ...), custom_call_target="tpu_custom_call" | custom-call | flops 4563402752 | bytes 16777216 | tf_op jit(solution)/shard_map/cross_back/pallas_call | solution.py:857
  360.5 142.6 %self_backward.1 = (bf16[544,1024]{1,0:T(8,128)(2,1)}, f32[4,4,1536]{2,1,0:T(4,128)}, bf16[544,1024]{1,0:T(8,128)(2,1)}, f32[128,768]{1,0:T(8,128)}, f32[128,640]{1,0:T(8,128)}) custom-call(bf16[544,1024]{1,0:T(8,128)(2,1)} %get-tuple-element.76.refs_0_, bf16[1280,512]{1,0:T(8,128)(2,1)} %get-tuple-element.77.refs_1_, ...), custom_call_target="tpu_custom_call" | custom-call | flops 7130316800 | bytes 16777216 | tf_op jit(solution)/shard_map/self_backward/pallas_call | solution.py:760
  503.1 0.9 reshape.187
  504.7 14.9 %self_back.1 = (bf16[4,1024,256]{2,1,0:T(8,128)(2,1)}, bf16[4,1024,256]{2,1,0:T(8,128)(2,1)}, bf16[544,1024]{1,0:T(8,128)(2,1)}, f32[1,1024]{1,0:T(1,128)}) custom-call(s32[2]{0:T(128)} %pad_add_fusion._, bf16[544,1024]{1,0:T(8,128)(2,1)} %get-tuple-element.106.refs_0_, bf16[544,1024]{1,0:T(8,128)(2,1)} %get-tuple-element.107.refs_1_.refs_2_, ...), custom_call_target="tpu_custom_call" | custom-call | flops 4563402752 | bytes 16777216 | tf_op jit(solution)/shard_map/self_back/pallas_call | solution.py:857
  521.1 109.8 %scatter_rest.1 = (f32[128,256]{1,0:T(8,128)}, f32[128,256]{1,0:T(8,128)}, f32[128,256]{1,0:T(8,128)}, f32[128,256]{1,0:T(8,128)}, f32[256,128]{1,0:T(8,128)}, /...) custom-call(bf16[4,8,128,256]{3,2,1,0:T(8,128)(2,1)} %bitcast.85, bf16[4,8,128,256]{3,2,1,0:T(8,128)(2,1)} %bitcast.84, ...), custom_call_target="tpu_custom_call" | custom-call | tf_op jit(solution)/shard_map/scatter_rest/pallas_call | solution.py:449
  632.5 0.9 copy.68
  633.4 0.9 copy.67
  634.3 1.3 slice_bitcast_fusion.3
  636.3 5.4 copy.63
  641.7 2.2 copy.76
  644.8 1.3 copy.77
  (109 shorter events, 20.8 us)
Async XLA Ops:
  7.2 0.7 copy-start
  7.2 49.0 %copy-start.17 = (s32[1088]{0:T(1024)S(1)}, s32[1088]{0:T(1024)}, u32[]{:S(2)}) copy-start(s32[1088]{0:T(1024)} %param.25) | copy-start | bytes 13060
  7.2 50.7 %copy-start.13 = (bf16[128,128]{1,0:T(8,128)(2,1)S(1)}, bf16[128,128]{1,0:T(8,128)(2,1)}, u32[]{:S(2)}) copy-start(bf16[128,128]{1,0:T(8,128)(2,1)} %param.35) | copy-start | bytes 98308
  7.2 50.7 %copy-start.14 = (bf16[128,128]{1,0:T(8,128)(2,1)S(1)}, bf16[128,128]{1,0:T(8,128)(2,1)}, u32[]{:S(2)}) copy-start(bf16[128,128]{1,0:T(8,128)(2,1)} %param.34) | copy-start | bytes 98308
  7.2 50.7 %copy-start.12 = (bf16[128,256]{1,0:T(8,128)(2,1)S(1)}, bf16[128,256]{1,0:T(8,128)(2,1)}, u32[]{:S(2)}) copy-start(bf16[128,256]{1,0:T(8,128)(2,1)} %param.33) | copy-start | bytes 196612
  7.2 629.1 %all-gather.5.cloned.1.call-start = ((), (), s32[]{:S(2)}) async-start(), calls=%async_computation.1 | async-start | bytes 2621440 | tf_op jit(solution)/shard_map/all_gather | solution.py:1415
  342.4 293.9 %all-gather.3.cloned.1.call-start = ((), (), s32[]{:S(2)}) async-start(), calls=%async_computation | async-start | bytes 5570560 | tf_op jit(solution)/shard_map/all_gather | solution.py:1373
  504.7 14.9 %copy-start.15 = (f32[1,1024]{1,0:T(1,128)S(1)}, f32[1,1024]{1,0:T(1,128)}, u32[]{:S(2)}) copy-start(f32[1,1024]{1,0:T(1,128)} %get-tuple-element.115) | copy-start | bytes 12292
  504.7 14.9 %copy-start.16 = (f32[1,1024]{1,0:T(1,128)S(1)}, f32[1,1024]{1,0:T(1,128)}, u32[]{:S(2)}) copy-start(f32[1,1024]{1,0:T(1,128)} %get-tuple-element.114) | copy-start | bytes 12292
  521.1 111.3 %copy-start.3 = (f32[128,768]{1,0:T(8,128)S(1)}, f32[128,768]{1,0:T(8,128)}, u32[]{:S(2)}) copy-start(f32[128,768]{1,0:T(8,128)} %get-tuple-element.127) | copy-start | bytes 1179652
  521.1 111.3 %copy-start.5 = (f32[128,640]{1,0:T(8,128)S(1)}, f32[128,640]{1,0:T(8,128)}, u32[]{:S(2)}) copy-start(f32[128,640]{1,0:T(8,128)} %get-tuple-element.128) | copy-start | bytes 983044
  630.9 4.7 copy-start.10
  630.9 4.7 copy-start.11
  636.3 5.4 slice-start
  636.3 5.4 slice-start.1
  641.7 3.1 copy-start.2
  641.7 7.8 %copy-start.1 = (s32[2,1088]{1,0:T(2,128)S(1)}, s32[2,1088]{1,0:T(2,128)}, u32[]{:S(2)}) copy-start(s32[2,1088]{1,0:T(2,128)} %param.23) | copy-start | bytes 26116
  644.8 1.3 copy-start.9
  644.8 2.0 copy-start.8
  644.8 2.7 copy-start.7
  644.8 3.3 copy-start.6
  644.8 4.0 copy-start.4
Sparse Core Ops, SparseCore 0:
  342.5 50.0 all-gather.4
  394.1 118.0 all-gather.2
